TPU v7x, 32 devices: a whole 2x2x4 slice. The times are simulated.
32 devices in a mesh: comp: 2 (over y), gx: 8 (over z, core), gy: 2 (over x).
Axes of the slice: x: 2, y: 2, z: 4, core: 2. Of those that a mesh axis runs over, the one named last changes fastest.
Arguments:
- state: float32 [2, 7, 256, 64, 128], P('comp', None, 'gx', 'gy'), may hold values from -6 to 6
- diffusivity: float32 [2, 7], replicated, may hold values from 0.01 to 0.06
- advection: float32 [2, 7], replicated, may hold values from 0.05 to 0.3
- solid_mask: int32 [256, 64, 128], P('gx', 'gy'), may hold values 0 or 1
- iface_map: int32 [64], P('gy'), may hold values from 0 to 63, each once
Outputs:
- new_state: float32 [2, 7, 256, 64, 128], P('comp', None, 'gx', 'gy')
Inputs may be any that keep to these rules, and one draw needn't show every extreme that they name: `iface_map`: each turbine inlet row takes exactly one combustor exit-plane row, and every exit-plane row is taken once.
All inputs are finite; a program needn't handle non-finite values. No bound on the sum of `solid_mask` on one device may be relied on, other than what follows from the above.
Results may differ from a plain program's by a relative error of at most 0.0014.
Values may be sent and summed in bfloat16 or wider, within the bound.
No kernel may reach another device: no remote copies, remote signals or barrier semaphores. Data moves between devices by JAX's collectives and lax.ppermute only.
A program may use at most 64 MiB of HBM per device.

v0:
```python
import jax
import jax.numpy as jnp
from jax import lax
from jax.sharding import PartitionSpec as P

RATIO = 1.5
GAIN = 0.4


def swapped(block, axis, apart):
    count = lax.axis_size(axis)
    route = []
    for low in range(count):
        high = low | 1 << apart
        if high != low and high < count:
            route += [(low, high), (high, low)]
    return lax.ppermute(block, axis, route)


def extended(block, sides, width):
    for axis, dim in sides:
        count = lax.axis_size(axis)
        forward = [(i, i + 1) for i in range(count - 1)]
        forward.append((count - 1, 0))
        backward = [(target, source) for source, target in forward]
        low = lax.ppermute(
            lax.slice_in_dim(block, block.shape[dim] - width, None, axis=dim), axis, forward
        )
        high = lax.ppermute(lax.slice_in_dim(block, 0, width, axis=dim), axis, backward)
        block = jnp.concatenate([low, block, high], axis=dim)
    return block


def rates(padded, solid, diff, speed):
    gfac = jnp.exp(GAIN * jnp.tanh(padded[4]))[None]
    mid = padded[:, 1:-1, 1:-1]
    east = padded[:, 2:, 1:-1]
    west = padded[:, :-2, 1:-1]
    north = padded[:, 1:-1, 2:]
    south = padded[:, 1:-1, :-2]
    gmid = gfac[:, 1:-1, 1:-1]
    geast = gfac[:, 2:, 1:-1]
    gwest = gfac[:, :-2, 1:-1]
    gnorth = gfac[:, 1:-1, 2:]
    gsouth = gfac[:, 1:-1, :-2]
    upper = jnp.roll(mid, -1, 3)
    lower = jnp.roll(mid, 1, 3)
    gupper = jnp.roll(gmid, -1, 3)
    glower = jnp.roll(gmid, 1, 3)
    along_x = 0.5 * (gmid + geast) * (east - mid) - 0.5 * (gmid + gwest) * (mid - west)
    along_y = 0.5 * (gmid + gnorth) * (north - mid) - 0.5 * (gmid + gsouth) * (mid - south)
    along_z = 0.5 * (gmid + gupper) * (upper - mid) - 0.5 * (gmid + glower) * (mid - lower)
    diffusion = along_x + along_y + along_z
    dcol = diff[:, None, None, None]
    scol = speed[:, None, None, None]
    fluid = dcol * diffusion - scol * (0.5 * (east - west))
    return jnp.where(solid[None], RATIO * dcol * diffusion, fluid)


def set_edges(padded, first_row, last_row, left_value, on_left, on_right):
    padded = padded.at[:, first_row].set(jnp.where(on_left, left_value, padded[:, first_row]))
    return padded.at[:, last_row].set(
        jnp.where(on_right, jnp.zeros_like(left_value), padded[:, last_row])
    )


def edge_rows(interface, map_whole, row_ids, turbine):
    inflow = jnp.take(interface, jnp.take(map_whole, row_ids), axis=1)
    matches = map_whole[None, :] == row_ids[:, None]
    counting = jnp.arange(map_whole.shape[0], dtype=jnp.int32)[None, :]
    anchor = jnp.sum(jnp.where(matches, counting, 0), axis=1)
    backflow = jnp.take(interface, anchor, axis=1)
    return jnp.where(turbine, inflow, backflow)


def body(state, diffusivity, advection, solid_mask, iface_map):
    fields = state[0]
    comp_pos = lax.axis_index("comp")
    turbine = comp_pos == 1
    diff = lax.dynamic_index_in_dim(diffusivity, comp_pos, 0, keepdims=False)
    speed_raw = lax.dynamic_index_in_dim(advection, comp_pos, 0, keepdims=False)
    speed = jnp.where(turbine, speed_raw, -speed_raw)
    stream_pos = lax.axis_index("gx")
    last_block = lax.axis_size("gx") - 1
    on_left = stream_pos == 0
    on_right = stream_pos == last_block
    solid = (solid_mask == 1) & turbine
    across = swapped(fields[:, 0].astype(jnp.bfloat16), "comp", 0).astype(jnp.float32)
    interface = lax.all_gather(across.astype(jnp.bfloat16), "gy", axis=1, tiled=True).astype(
        across.dtype
    )
    map_whole = lax.all_gather(iface_map, "gy", axis=0, tiled=True)
    rows_dev = fields.shape[2]
    row_base = lax.axis_index("gy") * rows_dev
    row_ids = row_base + jnp.arange(rows_dev, dtype=jnp.int32)
    left_value = edge_rows(interface, map_whole, row_ids, turbine)
    left_full = jnp.pad(left_value, ((0, 0), (1, 1), (0, 0)))

    def with_rim(block):
        padded = extended(block.astype(jnp.bfloat16), (("gx", 1), ("gy", 2)), 1).astype(block.dtype)
        return set_edges(padded, 0, -1, left_full, on_left, on_right)

    first = fields + rates(with_rim(fields), solid, diff, speed)
    second = rates(with_rim(first), solid, diff, speed)
    result = 0.5 * fields + 0.5 * (first + second)
    return result[None]


def solution(mesh):
    return jax.shard_map(
        body,
        mesh=mesh,
        in_specs=(P("comp", None, "gx", "gy", None), P(), P(), P("gx", "gy", None), P("gy")),
        out_specs=P("comp", None, "gx", "gy", None),
        check_vma=False,
    )
```

profile of v0, /device:TPU:0, one launch (start us, length us, event | category | flops | bytes accessed | tf_op | source)
XLA Modules:
  0.0 103.4 jit_solution(14877481706035770598)
XLA Ops:
  0.0 5.4 %copy.31 = bf16[1,7,32,32,128]{4,1,3,2,0:T(8,128)(2,1)S(1)} copy(f32[1,7,32,32,128]{4,3,2,1,0:T(8,128)} %param.15) | data formatting | bytes 5505024 | tf_op args[0]
  5.4 3.0 %collective-permute-start.4 = (bf16[7,32,128]{2,0,1:T(8,128)(2,1)S(1)}, bf16[7,32,128]{2,0,1:T(8,128)(2,1)S(1)}, u32[]{:S(2)}, u32[]{:S(2)}) collective-permute-start(bf16[7,32,128]{2,0,1:T(8,128)(2,1)S(1)} %get-tuple-element.74), channel_id=1, source_target_pairs={{0,16},{16,0},{1,17},{17,1},{2,18},{18,2},{3,19},{19,3},{4,20},{20... | collective-permute-start | bytes 172040 | tf_op jit(solution)/shard_map/ppermute | solution.py:17
  8.5 2.8 %collective-permute-start.1 = (bf16[7,1,32,128]{3,0,2,1:T(8,128)(2,1)S(1)}, bf16[7,1,32,128]{3,0,2,1:T(8,128)(2,1)S(1)}, u32[]{:S(2)}, u32[]{:S(2)}) collective-permute-start(bf16[7,1,32,128]{3,0,2,1:T(8,128)(2,1)S(1)} %get-tuple-element.75), channel_id=1, source_target_pairs={{2,0},{4,2},{6,4},{8,6},{10,8},{12,10},{14,12},{0,14},{3,1},{5,3},... | collective-permute-start | bytes 172040 | tf_op jit(solution)/shard_map/ppermute | solution.py:29
  12.8 4.3 %all-reduce.1 = s32[64]{0:T(128)S(1)} all-reduce(s32[64]{0:T(128)S(1)} %dynamic-update-slice.12), channel_id=1, replica_groups=mesh['comp'=2,'gx'=8,'gy'=2] {'gy'}, use_global_device_ids=true, to_apply=%add.1 | all-reduce | flops 64 | bytes 512
  17.3 0.7 gather_fusion
  18.2 5.6 %all_gather.6 = bf16[7,64,128]{2,1,0:T(8,128)(2,1)S(1)} all-gather(bf16[7,32,128]{2,1,0:T(8,128)(2,1)S(1)} %copy.19), channel_id=1, replica_groups=mesh['comp'=2,'gx'=8,'gy'=2] {'gy'}, dimensions={1}, use_global_device_ids=true | all-gather | bytes 172032 | tf_op jit(solution)/shard_map/all_gather | solution.py:89
  23.9 1.6 %collective-permute-start.2 = (bf16[7,34,1,128]{3,0,2,1:T(8,128)(2,1)S(1)}, bf16[7,34,1,128]{3,0,2,1:T(8,128)(2,1)S(1)}, u32[]{:S(2)}, u32[]{:S(2)}) collective-permute-start(bf16[7,34,1,128]{3,0,2,1:T(8,128)(2,1)S(1)} %get-tuple-element.70), channel_id=1, source_target_pairs={{0,1},{1,0},{2,3},{3,2},{4,5},{5,4},{6,7},{7,6},{8,9},{9,8},{10,11... | collective-permute-start | bytes 182792 | tf_op jit(solution)/shard_map/ppermute | solution.py:26
  27.4 0.9 collective-permute-done.2
  28.3 1.5 %collective-permute-done.3 = bf16[7,34,1,128]{3,0,2,1:T(8,128)(2,1)S(1)} collective-permute-done((bf16[7,34,1,128]{3,0,2,1:T(8,128)(2,1)S(1)}, bf16[7,34,1,128]{3,0,2,1:T(8,128)(2,1)S(1)}, u32[]{:S(2)}, u32[]{:S(2)}) %collective-permute-start.3) | collective-permute-done | bytes 60960 | tf_op jit(solution)/shard_map/ppermute | solution.py:29
  29.8 1.3 %maximum_convert_fusion = f32[7,34,34,128]{3,0,2,1:T(8,128)S(1)} fusion(bf16[7,34,1,128]{3,0,2,1:T(8,128)(2,1)S(1)} %collective-permute-done.3, bf16[7,1,32,128]{3,0,2,1:T(8,128)(2,1)S(1)} %collective-permute-done.1, bf16[7,32,32,128]{3,0,2,1:T(8,128)(2,1)S(1)} %bitcast.66, bf16[7,1,32,128]{3,0,2,1:T(8,128)(2,1)S(1)} %collective-permute-done, ...), kind=kLoop, calls=%fused_computation.32 | loop fusion | flops 5178880 | bytes 6214656 | tf_op jit(solution)/shard_map/convert_element_type | solution.py:100
  31.2 1.2 %fusion.21 = f32[1,34,34,128]{3,0,2,1:T(1,128)S(1)} fusion(f32[7,34,34,128]{3,0,2,1:T(8,128)S(1)} %fusion.38), kind=kLoop, calls=%fused_computation.39 | loop fusion | flops 147968 | bytes 1183744 | tf_op jit(solution)/shard_map/exp | solution.py:35
  32.4 1.1 %fusion.56 = (f32[1,32,32,1]{3,0,2,1:T(1,128)S(1)}, f32[1,32,32,1]{3,0,2,1:T(1,128)S(1)}) fusion(f32[1,34,34,128]{3,0,2,1:T(1,128)S(1)} %fusion.21), kind=kLoop, calls=%fused_computation.115 | loop fusion | bytes 16384 | tf_op jit(solution)/shard_map/jit(_roll_static)/slice | solution.py:48
  33.6 1.2 %fusion.55 = (f32[1,32,32,127]{3,0,2,1:T(1,128)S(1)}, f32[1,32,32,127]{3,0,2,1:T(1,128)S(1)}) fusion(f32[1,34,34,128]{3,0,2,1:T(1,128)S(1)} %fusion.21), kind=kLoop, calls=%fused_computation.114 | loop fusion | bytes 2080768 | tf_op jit(solution)/shard_map/jit(_roll_static)/slice | solution.py:48
  34.7 3.5 %fusion.51 = (f32[7,32,32,1]{3,0,2,1:T(8,128)S(1)}, f32[7,32,32,1]{3,0,2,1:T(8,128)}) fusion(f32[7,34,34,128]{3,0,2,1:T(8,128)S(1)} %fusion.38), kind=kLoop, calls=%fused_computation.110 | loop fusion | bytes 114688 | tf_op jit(solution)/shard_map/jit(_roll_static)/slice | solution.py:46
  38.2 4.8 %fusion.50 = (f32[7,32,32,127]{3,0,2,1:T(8,128)}, f32[7,32,32,127]{3,0,2,1:T(8,128)}) fusion(f32[7,34,34,128]{3,0,2,1:T(8,128)S(1)} %fusion.38), kind=kLoop, calls=%fused_computation.109 | loop fusion | bytes 14565376 | tf_op jit(solution)/shard_map/jit(_roll_static)/slice | solution.py:46
  43.1 4.4 %fusion.29 = (f32[1,32,32,128]{3,0,2,1:T(1,128)S(1)}, f32[1,32,32,128]{3,0,2,1:T(1,128)S(1)}, f32[1,32,32,128]{3,0,2,1:T(1,128)S(1)}, f32[1,32,32,128]{3,0,2,1:T...) fusion(f32[1,34,34,128]{3,0,2,1:T(1,128)S(1)} %fusion.21, ...), kind=kLoop, calls=%fused_computation.55 | loop fusion | flops 1835008 | bytes 6815744 | tf_op jit(solution)/shard_map/mul | solution.py:50
  47.5 11.8 %fusion.46 = (bf16[7,32,32,128]{3,0,2,1:T(8,128)(2,1)S(1)}, f32[7,32,32,128]{3,0,2,1:T(8,128)S(1)}) fusion(f32[7]{0:T(128)S(1)} %fusion.42, f32[7]{0:T(128)S(1)} %get-tuple-element.57, f32[7,32,32,127]{3,0,2,1:T(8,128)} %get-tuple-element.65, f32[7,32,32,1]{3,0,2,1:T(8,128)} %get-tuple-element.67, f32[32,32,128]{2,1,0:T(8,128)S(1)} %bitcast.74, ...), kind=kLoop, calls=%fused_computation.106 | loop fusion | flops 24772608 | bytes 38142036 | tf_op jit(solution)/shard_map/convert_element_type | solution.py:100
  59.4 3.5 %collective-permute-start.6 = (bf16[7,1,32,128]{3,0,2,1:T(8,128)(2,1)S(1)}, bf16[7,1,32,128]{3,0,2,1:T(8,128)(2,1)S(1)}, u32[]{:S(2)}, u32[]{:S(2)}) collective-permute-start(bf16[7,1,32,128]{3,0,2,1:T(8,128)(2,1)S(1)} %get-tuple-element.73), channel_id=1, source_target_pairs={{2,0},{4,2},{6,4},{8,6},{10,8},{12,10},{14,12},{0,14},{3,1},{5,3},... | collective-permute-start | bytes 172040 | tf_op jit(solution)/shard_map/ppermute | solution.py:29
  62.9 2.1 %collective-permute-done.5 = bf16[7,1,32,128]{3,0,2,1:T(8,128)(2,1)S(1)} collective-permute-done((bf16[7,1,32,128]{3,0,2,1:T(8,128)(2,1)S(1)}, bf16[7,1,32,128]{3,0,2,1:T(8,128)(2,1)S(1)}, u32[]{:S(2)}, u32[]{:S(2)}) %collective-permute-start.5) | collective-permute-done | bytes 57376 | tf_op jit(solution)/shard_map/ppermute | solution.py:26
  65.1 1.2 %collective-permute-start.7 = (bf16[7,34,1,128]{3,0,2,1:T(8,128)(2,1)S(1)}, bf16[7,34,1,128]{3,0,2,1:T(8,128)(2,1)S(1)}, u32[]{:S(2)}, u32[]{:S(2)}) collective-permute-start(bf16[7,34,1,128]{3,0,2,1:T(8,128)(2,1)S(1)} %get-tuple-element.68), channel_id=1, source_target_pairs={{0,1},{1,0},{2,3},{3,2},{4,5},{5,4},{6,7},{7,6},{8,9},{9,8},{10,11... | collective-permute-start | bytes 182792 | tf_op jit(solution)/shard_map/ppermute | solution.py:26
  66.3 0.9 collective-permute-start.8
  67.1 2.3 %collective-permute-done.7 = bf16[7,34,1,128]{3,0,2,1:T(8,128)(2,1)S(1)} collective-permute-done((bf16[7,34,1,128]{3,0,2,1:T(8,128)(2,1)S(1)}, bf16[7,34,1,128]{3,0,2,1:T(8,128)(2,1)S(1)}, u32[]{:S(2)}, u32[]{:S(2)}) %collective-permute-start.7) | collective-permute-done | bytes 60960 | tf_op jit(solution)/shard_map/ppermute | solution.py:26
  69.4 1.1 %collective-permute-done.8 = bf16[7,34,1,128]{3,0,2,1:T(8,128)(2,1)S(1)} collective-permute-done((bf16[7,34,1,128]{3,0,2,1:T(8,128)(2,1)S(1)}, bf16[7,34,1,128]{3,0,2,1:T(8,128)(2,1)S(1)}, u32[]{:S(2)}, u32[]{:S(2)}) %collective-permute-start.8) | collective-permute-done | bytes 60960 | tf_op jit(solution)/shard_map/ppermute | solution.py:29
  70.6 1.3 %maximum_convert_fusion.1 = f32[7,34,34,128]{3,0,2,1:T(8,128)S(1)} fusion(bf16[7,34,1,128]{3,0,2,1:T(8,128)(2,1)S(1)} %collective-permute-done.8, bf16[7,1,32,128]{3,0,2,1:T(8,128)(2,1)S(1)} %collective-permute-done.6, bf16[7,32,32,128]{3,0,2,1:T(8,128)(2,1)S(1)} %get-tuple-element.54, bf16[7,1,32,128]{3,0,2,1:T(8,128)(2,1)S(1)} %collective-permute-done.5, ...), kind=kLoop, calls=%fused_computation.33 | loop fusion | flops 5178880 | bytes 6214656 | tf_op jit(solution)/shard_map/convert_element_type | solution.py:100
  72.0 1.2 %fusion.19 = f32[1,34,34,128]{3,0,2,1:T(1,128)S(1)} fusion(f32[7,34,34,128]{3,0,2,1:T(8,128)S(1)} %fusion.34), kind=kLoop, calls=%fused_computation.36 | loop fusion | flops 147968 | bytes 1183744 | tf_op jit(solution)/shard_map/exp | solution.py:35
  73.2 1.1 %fusion.54 = (f32[1,32,32,1]{3,0,2,1:T(1,128)S(1)}, f32[1,32,32,1]{3,0,2,1:T(1,128)S(1)}) fusion(f32[1,34,34,128]{3,0,2,1:T(1,128)S(1)} %fusion.19), kind=kLoop, calls=%fused_computation.113 | loop fusion | bytes 16384 | tf_op jit(solution)/shard_map/jit(_roll_static)/slice | solution.py:48
  74.3 1.2 %fusion.53 = (f32[1,32,32,127]{3,0,2,1:T(1,128)S(1)}, f32[1,32,32,127]{3,0,2,1:T(1,128)S(1)}) fusion(f32[1,34,34,128]{3,0,2,1:T(1,128)S(1)} %fusion.19), kind=kLoop, calls=%fused_computation.112 | loop fusion | bytes 2080768 | tf_op jit(solution)/shard_map/jit(_roll_static)/slice | solution.py:48
  75.5 3.5 %fusion.49 = (f32[7,32,32,1]{3,0,2,1:T(8,128)S(1)}, f32[7,32,32,1]{3,0,2,1:T(8,128)}) fusion(f32[7,34,34,128]{3,0,2,1:T(8,128)S(1)} %fusion.34), kind=kLoop, calls=%fused_computation.108 | loop fusion | bytes 114688 | tf_op jit(solution)/shard_map/jit(_roll_static)/slice | solution.py:46
  79.0 4.8 %fusion.48 = (f32[7,32,32,127]{3,0,2,1:T(8,128)}, f32[7,32,32,127]{3,0,2,1:T(8,128)}) fusion(f32[7,34,34,128]{3,0,2,1:T(8,128)S(1)} %fusion.34), kind=kLoop, calls=%fused_computation.107 | loop fusion | bytes 14565376 | tf_op jit(solution)/shard_map/jit(_roll_static)/slice | solution.py:46
  83.9 5.0 %fusion.25 = (f32[1,32,32,128]{3,0,2,1:T(1,128)S(1)}, f32[1,32,32,128]{3,0,2,1:T(1,128)S(1)}, f32[1,32,32,128]{3,0,2,1:T(1,128)S(1)}, f32[1,32,32,128]{3,0,2,1:T...) fusion(f32[1,34,34,128]{3,0,2,1:T(1,128)S(1)} %fusion.19, f32[1,32,32,127]{3,0,2,1:T(1,128)S(1)} %get-tuple-element.84, ...), kind=kLoop, calls=%fused_computation.47 | loop fusion | flops 1835008 | bytes 6815744 | tf_op jit(solution)/shard_map/mul | solution.py:50
  88.8 12.1 %fusion.17 = f32[1,7,32,32,128]{4,1,3,2,0:T(8,128)S(1)} fusion(f32[1,7,32,32,128]{4,3,2,1,0:T(8,128)S(1)} %copy-done, f32[7,32,32,128]{3,0,2,1:T(8,128)S(1)} %get-tuple-element.55, f32[7,32,32,127]{3,0,2,1:T(8,128)} %get-tuple-element.61, f32[7,32,32,1]{3,0,2,1:T(8,128)} %get-tuple-element.63, f32[7,32,32,1]{3,0,2,1:T(8,128)S(1)} %get-tuple-element.62, ...), kind=kLoop, calls=%fused_computation.31 | loop fusion | flops 25690112 | bytes 39977044 | tf_op jit(solution)/shard_map/broadcast_in_dim | solution.py:106
  100.9 2.5 %copy.21 = f32[1,7,32,32,128]{4,3,2,1,0:T(8,128)} copy(f32[1,7,32,32,128]{4,1,3,2,0:T(8,128)S(1)} %fusion.17) | data formatting | bytes 7340032 | tf_op jit(solution)/shard_map/broadcast_in_dim | solution.py:106
  (49 shorter events, 3.4 us)
Async XLA Ops:
  0.0 11.3 %copy-start.6 = (u32[32]{0:T(128)S(1)}, u32[32]{0:T(128)}, u32[]{:S(2)}) copy-start(u32[32]{0:T(128)} %constant.162) | copy-start | bytes 388
  0.0 12.5 %copy-start.5 = (s32[32]{0:T(128)S(1)}, s32[32]{0:T(128)}, u32[]{:S(2)}) copy-start(s32[32]{0:T(128)} %param.19) | copy-start | bytes 388
  0.0 18.0 %copy-start.3 = (f32[2,7]{1,0:T(2,128)S(1)}, f32[2,7]{1,0:T(2,128)}, u32[]{:S(2)}) copy-start(f32[2,7]{1,0:T(2,128)} %param.16) | copy-start | bytes 172
  0.0 18.0 %copy-start.2 = (s32[32,32,128]{2,1,0:T(8,128)S(1)}, s32[32,32,128]{2,1,0:T(8,128)}, u32[]{:S(2)}) copy-start(s32[32,32,128]{2,1,0:T(8,128)} %param.18) | copy-start | bytes 1572868
  0.0 18.1 %copy-start.4 = (f32[2,7]{1,0:T(2,128)S(1)}, f32[2,7]{1,0:T(2,128)}, u32[]{:S(2)}) copy-start(f32[2,7]{1,0:T(2,128)} %param.17) | copy-start | bytes 172
  5.4 12.7 %collective-permute-start.4 = (bf16[7,32,128]{2,0,1:T(8,128)(2,1)S(1)}, bf16[7,32,128]{2,0,1:T(8,128)(2,1)S(1)}, u32[]{:S(2)}, u32[]{:S(2)}) collective-permute-start(bf16[7,32,128]{2,0,1:T(8,128)(2,1)S(1)} %get-tuple-element.74), channel_id=1, source_target_pairs={{0,16},{16,0},{1,17},{17,1},{2,18},{18,2},{3,19},{19,3},{4,20},{20... | collective-permute-start | bytes 172040 | tf_op jit(solution)/shard_map/ppermute | solution.py:17
  8.5 15.4 %collective-permute-start.1 = (bf16[7,1,32,128]{3,0,2,1:T(8,128)(2,1)S(1)}, bf16[7,1,32,128]{3,0,2,1:T(8,128)(2,1)S(1)}, u32[]{:S(2)}, u32[]{:S(2)}) collective-permute-start(bf16[7,1,32,128]{3,0,2,1:T(8,128)(2,1)S(1)} %get-tuple-element.75), channel_id=1, source_target_pairs={{2,0},{4,2},{6,4},{8,6},{10,8},{12,10},{14,12},{0,14},{3,1},{5,3},... | collective-permute-start | bytes 172040 | tf_op jit(solution)/shard_map/ppermute | solution.py:29
  11.2 12.6 %collective-permute-start = (bf16[7,1,32,128]{3,0,2,1:T(8,128)(2,1)S(1)}, bf16[7,1,32,128]{3,0,2,1:T(8,128)(2,1)S(1)}, u32[]{:S(2)}, u32[]{:S(2)}) collective-permute-start(bf16[7,1,32,128]{3,0,2,1:T(8,128)(2,1)S(1)} %get-tuple-element.76), channel_id=1, source_target_pairs={{0,2},{2,4},{4,6},{6,8},{8,10},{10,12},{12,14},{14,0},{1,3},{3,5},... | collective-permute-start | bytes 172040 | tf_op jit(solution)/shard_map/ppermute | solution.py:26
  18.1 29.4 %copy-start.1 = (pred[32,32,128]{2,1,0:T(8,128)(4,1)}, pred[32,32,128]{2,1,0:T(8,128)(4,1)S(1)}, u32[]{:S(2)}) copy-start(pred[32,32,128]{2,1,0:T(8,128)(4,1)S(1)} %compare_and_fusion) | copy-start | bytes 393220
  23.9 4.4 %collective-permute-start.2 = (bf16[7,34,1,128]{3,0,2,1:T(8,128)(2,1)S(1)}, bf16[7,34,1,128]{3,0,2,1:T(8,128)(2,1)S(1)}, u32[]{:S(2)}, u32[]{:S(2)}) collective-permute-start(bf16[7,34,1,128]{3,0,2,1:T(8,128)(2,1)S(1)} %get-tuple-element.70), channel_id=1, source_target_pairs={{0,1},{1,0},{2,3},{3,2},{4,5},{5,4},{6,7},{7,6},{8,9},{9,8},{10,11... | collective-permute-start | bytes 182792 | tf_op jit(solution)/shard_map/ppermute | solution.py:26
  25.5 4.3 %collective-permute-start.3 = (bf16[7,34,1,128]{3,0,2,1:T(8,128)(2,1)S(1)}, bf16[7,34,1,128]{3,0,2,1:T(8,128)(2,1)S(1)}, u32[]{:S(2)}, u32[]{:S(2)}) collective-permute-start(bf16[7,34,1,128]{3,0,2,1:T(8,128)(2,1)S(1)} %get-tuple-element.71), channel_id=1, source_target_pairs={{1,0},{0,1},{3,2},{2,3},{5,4},{4,5},{7,6},{6,7},{9,8},{8,9},{11,10... | collective-permute-start | bytes 182792 | tf_op jit(solution)/shard_map/ppermute | solution.py:29
  43.1 4.4 %copy-start = (f32[1,7,32,32,128]{4,3,2,1,0:T(8,128)S(1)}, f32[1,7,32,32,128]{4,3,2,1,0:T(8,128)}, u32[]{:S(2)}) copy-start(f32[1,7,32,32,128]{4,3,2,1,0:T(8,128)} %param.15) | copy-start | bytes 11010052
  59.3 5.7 %collective-permute-start.5 = (bf16[7,1,32,128]{3,0,2,1:T(8,128)(2,1)S(1)}, bf16[7,1,32,128]{3,0,2,1:T(8,128)(2,1)S(1)}, u32[]{:S(2)}, u32[]{:S(2)}) collective-permute-start(bf16[7,1,32,128]{3,0,2,1:T(8,128)(2,1)S(1)} %get-tuple-element.72), channel_id=1, source_target_pairs={{0,2},{2,4},{4,6},{6,8},{8,10},{10,12},{12,14},{14,0},{1,3},{3,5},... | collective-permute-start | bytes 172040 | tf_op jit(solution)/shard_map/ppermute | solution.py:26
  59.4 5.6 %collective-permute-start.6 = (bf16[7,1,32,128]{3,0,2,1:T(8,128)(2,1)S(1)}, bf16[7,1,32,128]{3,0,2,1:T(8,128)(2,1)S(1)}, u32[]{:S(2)}, u32[]{:S(2)}) collective-permute-start(bf16[7,1,32,128]{3,0,2,1:T(8,128)(2,1)S(1)} %get-tuple-element.73), channel_id=1, source_target_pairs={{2,0},{4,2},{6,4},{8,6},{10,8},{12,10},{14,12},{0,14},{3,1},{5,3},... | collective-permute-start | bytes 172040 | tf_op jit(solution)/shard_map/ppermute | solution.py:29
  65.1 4.4 %collective-permute-start.7 = (bf16[7,34,1,128]{3,0,2,1:T(8,128)(2,1)S(1)}, bf16[7,34,1,128]{3,0,2,1:T(8,128)(2,1)S(1)}, u32[]{:S(2)}, u32[]{:S(2)}) collective-permute-start(bf16[7,34,1,128]{3,0,2,1:T(8,128)(2,1)S(1)} %get-tuple-element.68), channel_id=1, source_target_pairs={{0,1},{1,0},{2,3},{3,2},{4,5},{5,4},{6,7},{7,6},{8,9},{9,8},{10,11... | collective-permute-start | bytes 182792 | tf_op jit(solution)/shard_map/ppermute | solution.py:26
  66.3 4.3 %collective-permute-start.8 = (bf16[7,34,1,128]{3,0,2,1:T(8,128)(2,1)S(1)}, bf16[7,34,1,128]{3,0,2,1:T(8,128)(2,1)S(1)}, u32[]{:S(2)}, u32[]{:S(2)}) collective-permute-start(bf16[7,34,1,128]{3,0,2,1:T(8,128)(2,1)S(1)} %get-tuple-element.69), channel_id=1, source_target_pairs={{1,0},{0,1},{3,2},{2,3},{5,4},{4,5},{7,6},{6,7},{9,8},{8,9},{11,10... | collective-permute-start | bytes 182792 | tf_op jit(solution)/shard_map/ppermute | solution.py:29
where the time goes:
time: 104 us; the launch traced here: 103 us
  other arithmetic  39.1 us (38%)
  local copies, waits for them, and re-layouts  31.9 us (31%)
  starting transfers between devices  13.6 us (13%)
  blocking collectives  9.9 us (10%)
  waiting for transfers between devices  7.89 us (8%)
    slice x4, local copies, waits for them, and re-layouts, rates(): upper = jnp.roll(mid, -1, 3)  16.7 us
    broadcast_in_dim x1, other arithmetic, body(): return result[None]  12.1 us
    convert_element_type x1, other arithmetic, with_rim(): block.astype(jnp.bfloat16)  11.8 us
    mul x2, other arithmetic, rates(): 0.5 * (gmid + geast) * (east - mid) - 0.5 * (gmid + gwest) * (mid - west)  9.4 us
    ppermute x4, starting transfers between devices, extended(): lax.ppermute(lax.slice_in_dim(block, 0, width, axis=dim), axis, backward)  7.71 us
    unnamed x18, local copies, waits for them, and re-layouts  6.24 us
    all_gather x1, blocking collectives, body(): lax.all_gather(across.astype(jnp.bfloat16), 'gy', axis=1, tiled=True)  5.65 us
    ppermute x4, waiting for transfers between devices, extended(): lax.ppermute(lax.slice_in_dim(block, block.shape[dim] - width, None, axis...  5.25 us
  transfers between devices with their start and end apart: 9, of which 5 were waited for; matrix products, arithmetic and copies ran while one was open for 3% of the time, Pallas kernels for 0%

commit v1 on v0

v1 whole, which is shorter than its diff:
```python
import functools

import jax
import jax.numpy as jnp
from jax import lax
from jax.experimental import pallas as pl
from jax.experimental.pallas import tpu as pltpu
from jax.sharding import PartitionSpec as P

RATIO = 1.5
GAIN = 0.4
BF = jnp.bfloat16
F32 = jnp.float32


def gain(q):
    return 0.5 * jnp.exp(GAIN * jnp.tanh(q))


def shift_matrix(nz):
    row = lax.broadcasted_iota(jnp.int32, (nz, 2 * nz), 0)
    col = lax.broadcasted_iota(jnp.int32, (nz, 2 * nz), 1)
    k = jnp.where(col < nz, col, col - nz)
    up = jnp.where(k + 1 == nz, 0, k + 1)
    down = jnp.where(k == 0, nz - 1, k - 1)
    one = lambda c: jnp.where(c, 1.0, 0.0)
    own = one(row == k)
    return jnp.where(col < nz, one(row == up) - own, own - one(row == down)).astype(BF)


def scalars(dif, adv, nf):
    comp = lax.axis_index("comp")
    sign = (2 * comp - 1).astype(F32)
    return [dif[comp, f] for f in range(nf)], [adv[comp, f] * sign for f in range(nf)], 2 - comp


def masks(solid):
    return jnp.where(solid, RATIO, 1.0), jnp.where(solid, 0.0, 0.5)


def section_kernel(dims, second, *refs):
    nf, nx, ny, nz = dims
    if second:
        dif, adv, base_ref, q_ref, s_ref, o_ref, fx, sm = refs
    else:
        dif, adv, q_ref, s_ref, o_ref, fx, sm = refs
    d, c, level = scalars(dif, adv, nf)
    fx[...] = jnp.zeros_like(fx)
    sm[...] = shift_matrix(nz)
    step_x = 2

    def at(x):
        return pl.ds(pl.multiple_of(x * ny, ny), ny)

    def step(i, gc):
        diffs = []
        for k in range(step_x):
            rows = q_ref[:, at(i * step_x + k)].astype(BF).reshape(nf * ny, nz)
            diffs.append(jnp.dot(rows, sm[...], preferred_element_type=F32))
        for k in range(step_x):
            x = i * step_x + k
            here, east, west = at(x), at(jnp.minimum(x + 1, nx - 1)), at(jnp.maximum(x - 1, 0))
            ge = gain(q_ref[4, east])
            gx, gy, gz = gc + ge, gc + pltpu.roll(gc, ny - 1, 0), gc + pltpu.roll(gc, nz - 1, 1)
            gzl = pltpu.roll(gz, 1, 1)
            m, a = masks(s_ref[here] >= level)
            for f in range(nf):
                q, qe, qw = q_ref[f, here], q_ref[f, east], q_ref[f, west]
                flux = gx * (qe - q)
                total = flux - fx[f]
                fx[f] = flux
                fy = gy * (pltpu.roll(q, ny - 1, 0) - q)
                total += fy - pltpu.roll(fy, 1, 0)
                z = diffs[k][f * ny : (f + 1) * ny]
                total += gz * z[:, :nz] - gzl * z[:, nz:]
                new = q + (d[f] * (m * total) - c[f] * (a * (qe - qw)))
                if second:
                    new = 0.5 * (base_ref[f, here] + new)
                o_ref[f, here] = new
            gc = ge
        return gc

    lax.fori_loop(0, nx // step_x, step, gain(q_ref[4, at(0)]))


def border_kernel(dims, two, *refs):
    nf, nx, ny, nz = dims
    if two:
        dif, adv, imap, q_ref, first_ref, main_ref, s_ref, a_ref, b_ref, c1_ref, c2l_ref, c2h_ref = refs[:12]
        rest = refs[12:]
    else:
        (dif, adv, imap, q_ref, first_ref, main_ref, s_ref, a_ref, b_ref, c1_ref, c2l_ref, c2h_ref,
         face_ref, map_ref) = refs[:14]
        rest = refs[14:]
    out_ref, sm, lay, cor, fl, fp, ol, strips, sem = rest
    d, c, level = scalars(dif, adv, nf)
    comp = lax.axis_index("comp")
    stream, last = lax.axis_index("gx"), lax.axis_size("gx") - 1
    even = stream % 2 == 0
    sm[...] = shift_matrix(nz)

    mids = []
    for f in range(nf):
        mids.append(pltpu.make_async_copy(
            main_ref.at[f, pl.ds(2, nx - 4), pl.ds(8, ny - 16)],
            out_ref.at[f, pl.ds(2, nx - 4), pl.ds(8, ny - 16)], sem.at[0, f]))
        mids[-1].start()
    cuts = []
    for k, row in enumerate((0, ny - 8)):
        cuts.append(pltpu.make_async_copy(main_ref.at[:, :, pl.ds(row, 8)], strips.at[k], sem.at[1, k]))
        cuts[-1].start()

    LF, LN, HN, HF = range(4)
    for f in range(nf):
        av = [a_ref[2 * f].astype(F32), a_ref[2 * f + 1].astype(F32)]
        bv = [b_ref[2 * f].astype(F32), b_ref[2 * f + 1].astype(F32)]
        lay[LF, f] = jnp.where(even, bv[0], av[0])
        lay[LN, f] = jnp.where(even, bv[1], av[1])
        zero = jnp.where(stream == last, 0.0, 1.0)
        lay[HN, f] = jnp.where(even, av[0], bv[0]) * zero
        lay[HF, f] = jnp.where(even, av[1], bv[1]) * zero
        lo, hi = c2l_ref[f, pl.ds(ny, 16)].astype(F32), c2h_ref[f, pl.ds(ny, 16)].astype(F32)
        lo_b, hi_b = c2l_ref[f, pl.ds(ny - 16, 16)].astype(F32), c2h_ref[f, pl.ds(0, 16)].astype(F32)
        cor[0, f : f + 1] = jnp.where(even, lo[5:6], lo[3:4])
        cor[1, f : f + 1] = jnp.where(even, hi[4:5], hi[2:3])
        cor[2, f : f + 1] = jnp.where(even, lo[1:2], lo_b[15:16]) * zero
        cor[3, f : f + 1] = jnp.where(even, hi[0:1], hi_b[0:1]) * zero

    @pl.when(stream == 0)
    def _():
        start = lax.axis_index("gy") * ny
        if two:
            whole = 2 * ny
            mine = jnp.broadcast_to(imap[...].astype(F32), (1, ny))
            other = c2l_ref[0, pl.ds(ny, 16)].astype(F32)[6:7, :ny]
            mapping = jnp.concatenate([mine, other], axis=1)
            order = start
        else:
            whole = face_ref.shape[1]
            mapping = map_ref[...].astype(F32)
            order = 0
        rows = 40
        r = lax.broadcasted_iota(jnp.int32, (rows, whole), 0)
        want = jnp.where(r < ny, r, jnp.where(r == ny, whole - 1, ny)) + start
        want = jnp.where(want >= whole, want - whole, want).astype(F32)
        t = lax.broadcasted_iota(jnp.int32, (rows, whole), 1) + order
        t = jnp.where(t >= whole, t - whole, t).astype(F32)
        u = lax.broadcasted_iota(jnp.int32, (whole, whole), 0) + order
        u = jnp.where(u >= whole, u - whole, u).astype(F32)
        one = lambda x: jnp.where(x, 1.0, 0.0)
        pick = one(t == want).astype(BF)
        targets = one(jnp.broadcast_to(mapping, (whole, whole)) == u).astype(BF)
        inlet = lax.dot_general(pick, targets, (((1,), (1,)), ((), ())), preferred_element_type=F32)
        feed = one(jnp.broadcast_to(mapping, (rows, whole)) == want)
        choose = jnp.where(comp == 1, inlet, feed).astype(BF)
        for f in range(nf):
            if two:
                layer = jnp.concatenate([b_ref[2 * f], c2l_ref[f, pl.ds(0, ny)]], axis=0)
            else:
                layer = face_ref[f]
            ghost = jnp.dot(choose, layer, preferred_element_type=F32)
            lay[LN, f] = ghost[:ny]
            cor[0, f : f + 1] = ghost[ny : ny + 1]
            cor[1, f : f + 1] = ghost[ny + 1 : ny + 2]

    row = lax.broadcasted_iota(jnp.int32, (ny, nz), 0)

    def slab(center, before, after, low, high, solid, along_outer):
        rows = jnp.concatenate([center(f).astype(BF) for f in range(nf)], axis=0)
        diffs = jnp.dot(rows, sm[...], preferred_element_type=F32)

        def ups(v, h):
            return jnp.where(row == ny - 1, h, pltpu.roll(v, ny - 1, 0))

        def downs(v, l):
            return jnp.where(row == 0, l, pltpu.roll(v, 1, 0))

        g = gain(center(4))
        gb, ga = g + gain(before(4)), g + gain(after(4))
        gu, gd = g + ups(g, gain(high(4))), g + downs(g, gain(low(4)))
        gz = g + pltpu.roll(g, nz - 1, 1)
        gzl = pltpu.roll(gz, 1, 1)
        m, a = masks(solid)
        res = []
        for f in range(nf):
            q = center(f)
            qa, qb = after(f), before(f)
            qu, qd = ups(q, high(f)), downs(q, low(f))
            z = diffs[f * ny : (f + 1) * ny]
            total = ga * (qa - q) - gb * (q - qb) + (gu * (qu - q) - gd * (q - qd))
            total += gz * z[:, :nz] - gzl * z[:, nz:]
            grad = qa - qb if along_outer else qu - qd
            res.append(q + (d[f] * (m * total) - c[f] * (a * grad)))
        return res

    def q_layer(x):
        return lambda f: q_ref[f, x * ny : (x + 1) * ny]

    def q_plane(y):
        return lambda f: q_ref[f, pl.ds(y, nx, stride=ny)]

    def halo(k):
        return lambda f: lay[k, f]

    def corner(k):
        return lambda f: cor[k, f : f + 1]

    plane = {-2: 2 * nf + 1, -1: 3 * nf + 1, ny: 0, ny + 1: nf}

    def c_plane(y):
        return lambda f: c1_ref[plane[y] + f].astype(F32)

    def line(src, k):
        return lambda f: src(f)[k : k + 1]

    s_lay = lambda x: s_ref[x * ny : (x + 1) * ny] >= level
    s_pla = lambda y: s_ref[pl.ds(y, nx, stride=ny)] >= level
    level_f = level.astype(F32)
    m_low = jnp.where(even, b_ref[2 * nf], a_ref[2 * nf]).astype(F32) >= level_f
    m_high = jnp.where(even, a_ref[2 * nf], b_ref[2 * nf]).astype(F32) >= level_f

    def put(dst, k, vals):
        for f in range(nf):
            dst[k, f] = vals[f]

    put(fl, 0, slab(halo(LN), halo(LF), q_layer(0), corner(0), corner(1), m_low, True))

    @pl.when(stream == 0)
    def _():
        for f in range(nf):
            fl[0, f] = lay[LN, f]

    def y_line(y, x):
        return lambda f: c1_ref[plane[y] + f, pl.ds(x // 16 * 16, 16)].astype(F32)[x % 16 : x % 16 + 1]

    put(fl, 1, slab(q_layer(0), halo(LN), q_layer(1), y_line(-1, 0), y_line(ny, 0), s_lay(0), True))
    put(fl, 6, slab(q_layer(nx - 1), q_layer(nx - 2), halo(HN), y_line(-1, nx - 1), y_line(ny, nx - 1),
                    s_lay(nx - 1), True))
    put(fl, 7, slab(halo(HN), q_layer(nx - 1), halo(HF), corner(2), corner(3), m_high, True))

    @pl.when(stream == last)
    def _():
        for f in range(nf):
            fl[7, f] = jnp.zeros((ny, nz), F32)

    put(fp, 0, slab(c_plane(-1), c_plane(-2), q_plane(0), corner(0), corner(2),
                    c1_ref[4 * nf + 1].astype(F32) >= level_f, False))
    put(fp, 1, slab(q_plane(0), c_plane(-1), q_plane(1), line(halo(LN), 0), line(halo(HN), 0), s_pla(0), False))
    put(fp, 6, slab(q_plane(ny - 1), q_plane(ny - 2), c_plane(ny), line(halo(LN), ny - 1),
                    line(halo(HN), ny - 1), s_pla(ny - 1), False))
    put(fp, 7, slab(c_plane(ny), q_plane(ny - 1), c_plane(ny + 1), corner(1), corner(3),
                    c1_ref[2 * nf].astype(F32) >= level_f, False))

    for f in range(nf):
        for k, x in ((2, 1), (3, 2), (4, nx - 3), (5, nx - 2)):
            fl[k, f] = first_ref[f, x * ny : (x + 1) * ny]
            fl[k, f, 0:1] = fp[1, f, x : x + 1]
            fl[k, f, ny - 1 : ny] = fp[6, f, x : x + 1]
        for k, y in ((2, 1), (3, 2), (4, ny - 3), (5, ny - 2)):
            fp[k, f] = first_ref[f, pl.ds(y, nx, stride=ny)]
            fp[k, f, 0:1] = fl[1, f, y : y + 1]
            fp[k, f, nx - 1 : nx] = fl[6, f, y : y + 1]

    def got(src, k):
        return lambda f: src[k, f]

    def got_line(src, k, r):
        return lambda f: src[k, f, r : r + 1]

    layers = []
    for k, (n, x) in enumerate(((1, 0), (2, 1), (5, nx - 2), (6, nx - 1))):
        vals = slab(got(fl, n), got(fl, n - 1), got(fl, n + 1), got_line(fp, 0, x), got_line(fp, 7, x), s_lay(x), True)
        for f in range(nf):
            ol[k, f] = 0.5 * (q_layer(x)(f) + vals[f])
        layers.append(pltpu.make_async_copy(ol.at[k], out_ref.at[:, x], sem.at[2, k]))
        layers[-1].start()
    for copy in cuts:
        copy.wait()
    edges = []
    for k, (n, y, side, r) in enumerate(((1, 0, 0, 0), (2, 1, 0, 1), (5, ny - 2, 1, 6), (6, ny - 1, 1, 7))):
        vals = slab(got(fp, n), got(fp, n - 1), got(fp, n + 1), got_line(fl, 0, y), got_line(fl, 7, y), s_pla(y), False)
        for f in range(nf):
            strips[side, f, :, r] = 0.5 * (q_plane(y)(f) + vals[f])
        if k % 2:
            edges.append(pltpu.make_async_copy(
                strips.at[side, :, pl.ds(2, nx - 4)],
                out_ref.at[:, pl.ds(2, nx - 4), pl.ds(side * (ny - 8), 8)], sem.at[3, side]))
            edges[-1].start()
    for copy in mids + layers + edges:
        copy.wait()


VM = pl.BlockSpec(memory_space=pltpu.VMEM)
SM = pl.BlockSpec(memory_space=pltpu.SMEM)
HB = pl.BlockSpec(memory_space=pl.ANY)


def body(sizes, state, diffusivity, advection, solid_mask, iface_map):
    ngx, ngy = sizes
    q = state[0]
    nf, nx, ny, nz = q.shape
    dims = nf, nx, ny, nz
    two = ngy == 2
    even = lax.axis_index("gx") % 2 == 0

    def planes(rows, solid_row):
        return jnp.concatenate([q[:, :, r] for r in rows] + [solid_mask[None, :, solid_row].astype(F32)], 0).astype(BF)

    if two:
        swap = [(0, 1), (1, 0)]
        c1 = lax.ppermute(jnp.concatenate([planes((0, 1), 0), planes((ny - 2, ny - 1), ny - 1)], 0), "gy", swap)
    else:
        up = [(j, (j + 1) % ngy) for j in range(ngy)]
        down = [(b, a) for a, b in up]
        c1 = jnp.concatenate([lax.ppermute(planes((0, 1), 0), "gy", down),
                              lax.ppermute(planes((ny - 2, ny - 1), ny - 1), "gy", up)], 0)

    def layers(at_end):
        start = jnp.where(at_end, nx - 2, 0)
        edge = jnp.where(at_end, nx - 1, 0)
        fields = lax.dynamic_slice_in_dim(q, start, 2, 1).reshape(2 * nf, ny, nz)
        solid = lax.dynamic_slice_in_dim(solid_mask, edge, 1, 0)
        return jnp.concatenate([fields, solid.astype(F32)], 0).astype(BF)

    def both(pairs):
        return pairs + [(b, a) for a, b in pairs]

    inner = both([(k, k + 1) for k in range(0, ngx, 2)])
    a = lax.ppermute(layers(even), "gx", inner)
    outer = [(k * ngx + i, k * ngx + i + 1) for k in range(2) for i in range(1, ngx - 1, 2)]
    b = lax.ppermute(layers(~even), ("comp", "gx"), both(outer + [(0, ngx)]))

    a4, b4 = a[: 2 * nf].reshape(nf, 2, ny, nz), b[: 2 * nf].reshape(nf, 2, ny, nz)
    map_row = jnp.pad(iface_map.astype(BF), (0, nz - ny)).reshape(1, 1, nz)
    pick = lambda v, l: [v[:, l, 0:1], v[:, l, ny - 1 : ny]]
    extra = jnp.concatenate(
        [b4[:, 0]] + pick(a4, 0) + pick(a4, 1) + pick(b4, 1)
        + [jnp.broadcast_to(map_row, (nf, 1, nz)), jnp.zeros((nf, 9, nz), BF)], 1)
    if two:
        c2 = lax.ppermute(extra, "gy", swap)
        c2l, c2h, more = c2, c2, []
    else:
        c2l, c2h = lax.ppermute(extra, "gy", up), lax.ppermute(extra, "gy", down)
        more = [lax.all_gather(b4[:, 0], "gy", axis=1, tiled=True),
                lax.all_gather(iface_map, "gy", axis=0, tiled=True).reshape(1, -1)]

    flat = q.reshape(nf, nx * ny, nz)
    solid = solid_mask.reshape(nx * ny, nz)
    shape = jax.ShapeDtypeStruct((nf, nx * ny, nz), F32)
    cells = nf * nx * ny * nz

    def section(second, *args):
        return pl.pallas_call(
            functools.partial(section_kernel, dims, second),
            out_shape=shape,
            in_specs=[SM, SM] + [VM] * (len(args) + 1),
            out_specs=VM,
            scratch_shapes=[pltpu.VMEM((nf, ny, nz), F32), pltpu.VMEM((nz, 2 * nz), BF)],
            compiler_params=pltpu.CompilerParams(vmem_limit_bytes=20 << 20),
            cost_estimate=pl.CostEstimate(flops=20 * cells, bytes_accessed=8 * cells, transcendentals=cells // 4),
        )(diffusivity, advection, *args, solid)

    first = section(False, flat)
    main = section(True, flat, first)
    mb = pltpu.VMEM
    return pl.pallas_call(
        functools.partial(border_kernel, dims, two),
        out_shape=jax.ShapeDtypeStruct((nf, nx, ny, nz), F32),
        in_specs=[SM, SM, VM] + [VM] * (9 + len(more)),
        out_specs=HB,
        scratch_shapes=[
            mb((nz, 2 * nz), BF), mb((4, nf, ny, nz), F32), mb((4, 8, nz), F32), mb((8, nf, ny, nz), F32),
            mb((8, nf, nx, nz), F32), mb((4, nf, ny, nz), F32), mb((2, nf, nx, 8, nz), F32),
            pltpu.SemaphoreType.DMA((4, 8)),
        ],
        compiler_params=pltpu.CompilerParams(vmem_limit_bytes=40 << 20),
        cost_estimate=pl.CostEstimate(flops=10 * cells, bytes_accessed=8 * cells, transcendentals=cells // 4),
    )(diffusivity, advection, iface_map.reshape(1, ny), flat, first, main.reshape(nf, nx, ny, nz), solid,
      a, b, c1, c2l, c2h, *more)[None]


def solution(mesh):
    sizes = mesh.shape["gx"], mesh.shape["gy"]
    return jax.shard_map(
        functools.partial(body, sizes),
        mesh=mesh,
        in_specs=(P("comp", None, "gx", "gy", None), P(), P(), P("gx", "gy", None), P("gy")),
        out_specs=P("comp", None, "gx", "gy", None),
        check_vma=False,
    )
```

time: 104 us -> 33.9 us (0.33)
  other arithmetic: 39.1 us -> 0.81 us
  local copies, waits for them, and re-layouts: 31.9 us -> 8.65 us
  Pallas kernels: 0 us -> 16.7 us
  blocking collectives: 9.9 us -> 0 us
  waiting for transfers between devices: 7.89 us -> 0.01 us
  starting transfers between devices: 13.6 us -> 7.25 us
    slice x9 -> x3, local copies, waits for them, and re-layouts: 21.3 us -> 1.02 us  [the longest x1 1 us: planes(): solid_mask[None, :, solid_row].astype(F32)]
    pallas_call x0 -> x3, Pallas kernels: none -> 16.7 us  [the longest x2 10.3 us: section(): pl.pallas_call(functools.partial(section_kernel, dims, second), out_shape...]
    convert_element_type x4 -> x1, other arithmetic: 14.5 us -> 0.01 us  [body(): map_row = jnp.pad(iface_map.astype(BF), (0, nz - ny)).reshape(1, 1, nz)]
    broadcast_in_dim x1 -> x0, other arithmetic: 12.1 us -> none  [body(): return result[None]]
    mul x4 -> x0, other arithmetic: 9.43 us -> none  [the longest x2 9.4 us: rates(): 0.5 * (gmid + geast) * (east - mid) - 0.5 * (gmid + gwest) * (mid - west)]
    ppermute x9 -> x4, waiting for transfers between devices: 7.89 us -> 0.01 us  [the longest x1 0.01 us: body(): a = lax.ppermute(layers(even), 'gx', inner)]
    ppermute x9 -> x4, starting transfers between devices: 13.6 us -> 7.25 us  [the longest x1 4.57 us: body(): b = lax.ppermute(layers(~even), ('comp', 'gx'), both(outer + [(0, ngx)]))]
    all_gather x1 -> x0, blocking collectives: 5.65 us -> none  [body(): lax.all_gather(across.astype(jnp.bfloat16), 'gy', axis=1, tiled=True)]
  transfers between devices with their start and end apart: 9 -> 4, of which waited for: 5 -> 0; matrix products, arithmetic and copies ran while one was open for 3% -> 17% of each run, Pallas kernels for 0% -> 31%
where the time goes in v1:
time: 33.9 us; the launch traced here: 33.6 us
  Pallas kernels  16.7 us (49%)
  local copies, waits for them, and re-layouts  8.65 us (26%)
  starting transfers between devices  7.25 us (21%)
  other arithmetic  0.81 us (2%)
    pallas_call x2, Pallas kernels, section(): pl.pallas_call(functools.partial(section_kernel, dims, second), out_shape...  10.3 us
    pallas_call x1, Pallas kernels, body(): pl.pallas_call(functools.partial(border_kernel, dims, two), out_shape=jax...  6.32 us
    unnamed x17, local copies, waits for them, and re-layouts  6.27 us
    ppermute x1, starting transfers between devices, body(): b = lax.ppermute(layers(~even), ('comp', 'gx'), both(outer + [(0, ngx)]))  4.57 us
    ppermute x1, starting transfers between devices, body(): lax.ppermute(jnp.concatenate([planes((0, 1), 0), planes((ny - 2, ny - 1),...  1.56 us
    another operation x1, local copies, waits for them, and re-layouts  1.08 us
    slice x1, local copies, waits for them, and re-layouts, planes(): solid_mask[None, :, solid_row].astype(F32)  1 us
    another operation x1, other arithmetic  0.75 us
  transfers between devices with their start and end apart: 4, of which 0 were waited for; matrix products, arithmetic and copies ran while one was open for 17% of the time, Pallas kernels for 31%

profile of v1, /device:TPU:0, one launch (start us, length us, event | category | flops | bytes accessed | tf_op | source)
XLA Modules:
  0.0 33.6 jit_solution(12934032896571920248)
XLA Ops:
  0.0 0.0 copy-start.5
  0.0 0.8 %convert_convert_fusion.2 = (bf16[1,32,128]{2,1,0:T(8,128)(2,1)S(1)}, bf16[1,32,128]{2,1,0:T(8,128)(2,1)S(1)}) fusion(s32[32,32,128]{2,1,0:T(8,128)} %param.8, s32[]{:T(128)S(6)} %select_n.28, s32[]{:T(128)S(6)} %select_n.26), kind=kLoop, calls=%fused_computation.17 | loop fusion | flops 16384 | bytes 49160 | tf_op jit(solution)/shard_map/convert.17
  0.8 1.1 %dynamic-slice_convert_fusion = (bf16[1,7,2,32,128]{4,3,2,1,0:T(8,128)(2,1)S(1)}, bf16[1,7,2,32,128]{4,3,2,1,0:T(8,128)(2,1)S(1)}) fusion(f32[1,7,32,32,128]{4,3,2,1,0:T(8,128)} %param.5, s32[]{:T(128)S(6)} %select_n.27, s32[]{:T(128)S(6)} %select_n.25), kind=kLoop, calls=%fused_computation.2 | loop fusion | bytes 458760 | tf_op jit(solution)/shard_map/convert.18
  1.8 0.0 copy-start.2
  1.9 0.0 copy-start.3
  1.9 0.0 copy-start.4
  1.9 0.5 %collective-permute-start = (bf16[15,32,128]{2,1,0:T(8,128)(2,1)S(1)}, bf16[15,32,128]{2,1,0:T(8,128)(2,1)S(1)}, u32[]{:S(2)}, u32[]{:S(2)}) collective-permute-start(bf16[15,32,128]{2,1,0:T(8,128)(2,1)S(1)} %pad_maximum_fusion), channel_id=1, source_target_pairs={{0,2},{4,6},{8,10},{12,14},{2,0},{6,4},{10,8},{14,12},{1,3},{5,7},... | collective-permute-start | bytes 368648 | tf_op jit(solution)/shard_map/ppermute | solution.py:329
  2.4 4.6 %collective-permute-start.1 = (bf16[15,32,128]{2,1,0:T(8,128)(2,1)S(1)}, bf16[15,32,128]{2,1,0:T(8,128)(2,1)S(1)}, u32[]{:S(2)}, u32[]{:S(2)}) collective-permute-start(bf16[15,32,128]{2,1,0:T(8,128)(2,1)S(1)} %pad_maximum_fusion.1), channel_id=1, source_target_pairs={{2,4},{6,8},{10,12},{18,20},{22,24},{26,28},{0,16},{4,2},{8,6},{12... | collective-permute-start | bytes 368648 | tf_op jit(solution)/shard_map/ppermute | solution.py:331
  7.0 1.0 %fusion.7 = (s32[32,1,128]{2,1,0:T(1,128)S(1)}, s32[32,1,128]{2,1,0:T(1,128)S(1)}) fusion(s32[32,32,128]{2,1,0:T(8,128)} %param.8), kind=kLoop, calls=%fused_computation.29 | loop fusion | bytes 65536 | tf_op jit(solution)/shard_map/slice | solution.py:307
  8.0 4.2 %copy.40 = bf16[1,7,32,32,128]{4,2,1,3,0:T(8,128)(2,1)S(1)} copy(f32[1,7,32,32,128]{4,3,2,1,0:T(8,128)} %param.5) | data formatting | bytes 5505024 | tf_op args[0]
  12.3 1.6 %collective-permute-start.2 = (bf16[30,32,128]{2,1,0:T(8,128)(2,1)S(1)}, bf16[30,32,128]{2,1,0:T(8,128)(2,1)S(1)}, u32[]{:S(2)}, u32[]{:S(2)}) collective-permute-start(bf16[30,32,128]{2,1,0:T(8,128)(2,1)S(1)} %constant_dynamic-update-slice_fusion), channel_id=1, source_target_pairs={{0,1},{1,0},{2,3},{3,2},{4,5},{5,4},{6,7},{7,6},{8,9},{9,8},{10,11... | collective-permute-start | bytes 737288 | tf_op jit(solution)/shard_map/ppermute | solution.py:311
  13.8 0.0 copy-done.5
  13.9 0.0 collective-permute-done.refs_7_
  13.9 0.0 collective-permute-done.1.refs_8_
  14.0 0.2 concatenate.22
  14.2 0.6 %collective-permute-start.3 = (bf16[7,48,128]{2,1,0:T(8,128)(2,1)S(1)}, bf16[7,48,128]{2,1,0:T(8,128)(2,1)S(1)}, u32[]{:S(2)}, u32[]{:S(2)}) collective-permute-start(bf16[7,48,128]{2,1,0:T(8,128)(2,1)S(1)} %concatenate.22), channel_id=1, source_target_pairs={{0,1},{1,0},{2,3},{3,2},{4,5},{5,4},{6,7},{7,6},{8,9},{9,8},{10,11... | collective-permute-start | bytes 258056 | tf_op jit(solution)/shard_map/ppermute | solution.py:340
  14.8 0.0 copy-done.2
  14.8 0.0 copy-done.3
  14.8 0.0 copy-done.4
  14.8 0.0 copy-start
  14.8 2.0 %copy-done = f32[1,7,32,32,128]{4,3,2,1,0:T(8,128)S(1)} copy-done((f32[1,7,32,32,128]{4,3,2,1,0:T(8,128)S(1)}, f32[1,7,32,32,128]{4,3,2,1,0:T(8,128)}, u32[]{:S(2)}) %copy-start) | copy-done | bytes 3670040
  16.9 0.0 copy-start.1
  16.9 5.0 %shard_map.55.refs_3_.refs_4_ = f32[7,1024,128]{2,1,0:T(8,128)S(1)} custom-call(f32[2,7]{1,0:T(2,128)S(1)} %copy-done.3, f32[2,7]{1,0:T(2,128)S(1)} %copy-done.4, f32[7,1024,128]{2,1,0:T(8,128)S(1)} %bitcast.54, s32[1024,128]{1,0:T(8,128)S(1)} %bitcast.58), custom_call_target="tpu_custom_call" | custom-call | flops 18350080 | bytes 7340032 | tf_op jit(solution)/shard_map/pallas_call | solution.py:353
  21.9 0.0 copy-done.1
  21.9 5.3 %shard_map.56 = f32[7,1024,128]{2,1,0:T(8,128)S(1)} custom-call(f32[2,7]{1,0:T(2,128)S(1)} %copy-done.3, f32[2,7]{1,0:T(2,128)S(1)} %copy-done.4, f32[7,1024,128]{2,1,0:T(8,128)S(1)} %bitcast.55, f32[7,1024,128]{2,1,0:T(8,128)S(1)} %shard_map.55.refs_3_.refs_4_, s32[1024,128]{1,0:T(8,128)S(1)} %bitcast.59), custom_call_target="tpu_custom_call" | custom-call | flops 18350080 | bytes 7340032 | tf_op jit(solution)/shard_map/pallas_call | solution.py:353
  27.2 0.0 collective-permute-done.3.refs_10_.refs_11_
  27.3 0.0 collective-permute-done.2.refs_9_
  27.3 6.3 %shard_map.57 = f32[7,32,32,128]{3,2,1,0:T(8,128)} custom-call(f32[2,7]{1,0:T(2,128)S(1)} %copy-done.3, f32[2,7]{1,0:T(2,128)S(1)} %copy-done.4, s32[1,32]{1,0:T(1,128)S(1)} %bitcast.61, f32[7,1024,128]{2,1,0:T(8,128)S(1)} %bitcast.56, f32[7,1024,128]{2,1,0:T(8,128)S(1)} %shard_map.55.refs_3_.refs_4_, f32[7,32,32,128]{3,2,1,0:T(8,128)S(1)} %bitcast.57, ...), custom_call_target="tpu_custom_call" | custom-call | flops 9175040 | bytes 7340032 | tf_op jit(solution)/shard_map/pallas_call | solution.py:366
  (17 shorter events, 0.2 us)
Async XLA Ops:
  0.0 13.8 %copy-start.5 = (s32[32]{0:T(128)S(1)}, s32[32]{0:T(128)}, u32[]{:S(2)}) copy-start(s32[32]{0:T(128)} %param.9) | copy-start | bytes 388
  1.8 13.0 %copy-start.2 = (s32[32,32,128]{2,1,0:T(8,128)S(1)}, s32[32,32,128]{2,1,0:T(8,128)}, u32[]{:S(2)}) copy-start(s32[32,32,128]{2,1,0:T(8,128)} %param.8) | copy-start | bytes 1572868
  1.9 13.0 %copy-start.3 = (f32[2,7]{1,0:T(2,128)S(1)}, f32[2,7]{1,0:T(2,128)}, u32[]{:S(2)}) copy-start(f32[2,7]{1,0:T(2,128)} %refs_0_.5) | copy-start | bytes 172
  1.9 13.0 %copy-start.4 = (f32[2,7]{1,0:T(2,128)S(1)}, f32[2,7]{1,0:T(2,128)}, u32[]{:S(2)}) copy-start(f32[2,7]{1,0:T(2,128)} %refs_1_.5) | copy-start | bytes 172
  1.9 12.0 %collective-permute-start = (bf16[15,32,128]{2,1,0:T(8,128)(2,1)S(1)}, bf16[15,32,128]{2,1,0:T(8,128)(2,1)S(1)}, u32[]{:S(2)}, u32[]{:S(2)}) collective-permute-start(bf16[15,32,128]{2,1,0:T(8,128)(2,1)S(1)} %pad_maximum_fusion), channel_id=1, source_target_pairs={{0,2},{4,6},{8,10},{12,14},{2,0},{6,4},{10,8},{14,12},{1,3},{5,7},... | collective-permute-start | bytes 368648 | tf_op jit(solution)/shard_map/ppermute | solution.py:329
  2.4 11.5 %collective-permute-start.1 = (bf16[15,32,128]{2,1,0:T(8,128)(2,1)S(1)}, bf16[15,32,128]{2,1,0:T(8,128)(2,1)S(1)}, u32[]{:S(2)}, u32[]{:S(2)}) collective-permute-start(bf16[15,32,128]{2,1,0:T(8,128)(2,1)S(1)} %pad_maximum_fusion.1), channel_id=1, source_target_pairs={{2,4},{6,8},{10,12},{18,20},{22,24},{26,28},{0,16},{4,2},{8,6},{12... | collective-permute-start | bytes 368648 | tf_op jit(solution)/shard_map/ppermute | solution.py:331
  12.3 15.0 %collective-permute-start.2 = (bf16[30,32,128]{2,1,0:T(8,128)(2,1)S(1)}, bf16[30,32,128]{2,1,0:T(8,128)(2,1)S(1)}, u32[]{:S(2)}, u32[]{:S(2)}) collective-permute-start(bf16[30,32,128]{2,1,0:T(8,128)(2,1)S(1)} %constant_dynamic-update-slice_fusion), channel_id=1, source_target_pairs={{0,1},{1,0},{2,3},{3,2},{4,5},{5,4},{6,7},{7,6},{8,9},{9,8},{10,11... | collective-permute-start | bytes 737288 | tf_op jit(solution)/shard_map/ppermute | solution.py:311
  14.2 13.0 %collective-permute-start.3 = (bf16[7,48,128]{2,1,0:T(8,128)(2,1)S(1)}, bf16[7,48,128]{2,1,0:T(8,128)(2,1)S(1)}, u32[]{:S(2)}, u32[]{:S(2)}) collective-permute-start(bf16[7,48,128]{2,1,0:T(8,128)(2,1)S(1)} %concatenate.22), channel_id=1, source_target_pairs={{0,1},{1,0},{2,3},{3,2},{4,5},{5,4},{6,7},{7,6},{8,9},{9,8},{10,11... | collective-permute-start | bytes 258056 | tf_op jit(solution)/shard_map/ppermute | solution.py:340
  14.8 2.0 %copy-start = (f32[1,7,32,32,128]{4,3,2,1,0:T(8,128)S(1)}, f32[1,7,32,32,128]{4,3,2,1,0:T(8,128)}, u32[]{:S(2)}) copy-start(f32[1,7,32,32,128]{4,3,2,1,0:T(8,128)} %param.5) | copy-start | bytes 11010052
  16.9 5.0 %copy-start.1 = (f32[1,7,32,32,128]{4,3,2,1,0:T(8,128)S(1)}, f32[1,7,32,32,128]{4,3,2,1,0:T(8,128)}, u32[]{:S(2)}) copy-start(f32[1,7,32,32,128]{4,3,2,1,0:T(8,128)} %param.5) | copy-start | bytes 11010052

commit v2 on v1

--- a/solution.py
+++ b/solution.py
@@ -36,6 +36,40 @@
 
 def masks(solid):
     return jnp.where(solid, RATIO, 1.0), jnp.where(solid, 0.0, 0.5)
+
+
+def gather_kernel(dims, q_ref, s_ref, a_ref, b_ref, c_ref):
+    nf, nx, ny, nz = dims
+    even = lax.axis_index("gx") % 2 == 0
+    def layer(ref, f, k):
+        at = pl.multiple_of(k * ny, ny)
+        return (ref[pl.ds(at, ny)] if f is None else ref[f, pl.ds(at, ny)]).astype(F32).astype(BF)
+
+    a0, b0 = jnp.where(even, nx - 2, 0), jnp.where(even, 0, nx - 2)
+    a1, b1 = jnp.where(even, nx - 1, 0), jnp.where(even, 0, nx - 1)
+    for f in range(nf):
+        for k in range(2):
+            a_ref[2 * f + k] = layer(q_ref, f, a0 + k)
+            b_ref[2 * f + k] = layer(q_ref, f, b0 + k)
+        for k, y in enumerate((0, 1, ny - 2, ny - 1)):
+            c_ref[k * nf + k // 2 + f] = q_ref[f, pl.ds(y, nx, stride=ny)].astype(BF)
+    a_ref[2 * nf] = layer(s_ref, None, a1)
+    b_ref[2 * nf] = layer(s_ref, None, b1)
+    for k, y in ((2 * nf, 0), (4 * nf + 1, ny - 1)):
+        c_ref[k] = s_ref[pl.ds(y, nx, stride=ny)].astype(F32).astype(BF)
+
+
+def relay_kernel(dims, imap, a_ref, b_ref, o_ref, rows):
+    nf, nx, ny, nz = dims
+    rows[...] = jnp.zeros_like(rows)
+    rows[6:7, :ny] = imap[...].astype(F32)
+    for f in range(nf):
+        o_ref[f, :ny] = b_ref[2 * f]
+        for k, (src, n) in enumerate(((a_ref, 2 * f), (a_ref, 2 * f + 1), (b_ref, 2 * f + 1))):
+            block = src[n].astype(F32)
+            rows[2 * k : 2 * k + 1] = block[:1]
+            rows[2 * k + 1 : 2 * k + 2] = block[ny - 1 :]
+        o_ref[f, ny:] = rows[...].astype(BF)
 
 
 def section_kernel(dims, second, *refs):
@@ -301,51 +335,50 @@
     nf, nx, ny, nz = q.shape
     dims = nf, nx, ny, nz
     two = ngy == 2
-    even = lax.axis_index("gx") % 2 == 0
-
-    def planes(rows, solid_row):
-        return jnp.concatenate([q[:, :, r] for r in rows] + [solid_mask[None, :, solid_row].astype(F32)], 0).astype(BF)
+
+    flat, solid = q.reshape(nf, nx * ny, nz), solid_mask.reshape(nx * ny, nz)
+    send_a, send_b, send_c = pl.pallas_call(
+        functools.partial(gather_kernel, dims),
+        out_shape=[jax.ShapeDtypeStruct((n, ny, nz), BF) for n in (2 * nf + 1, 2 * nf + 1, 4 * nf + 2)],
+        in_specs=[VM] * 2,
+        out_specs=[VM] * 3,
+        compiler_params=pltpu.CompilerParams(vmem_limit_bytes=2 << 20),
+    )(flat, solid)
 
     if two:
         swap = [(0, 1), (1, 0)]
-        c1 = lax.ppermute(jnp.concatenate([planes((0, 1), 0), planes((ny - 2, ny - 1), ny - 1)], 0), "gy", swap)
+        c1 = lax.ppermute(send_c, "gy", swap)
     else:
         up = [(j, (j + 1) % ngy) for j in range(ngy)]
         down = [(b, a) for a, b in up]
-        c1 = jnp.concatenate([lax.ppermute(planes((0, 1), 0), "gy", down),
-                              lax.ppermute(planes((ny - 2, ny - 1), ny - 1), "gy", up)], 0)
-
-    def layers(at_end):
-        start = jnp.where(at_end, nx - 2, 0)
-        edge = jnp.where(at_end, nx - 1, 0)
-        fields = lax.dynamic_slice_in_dim(q, start, 2, 1).reshape(2 * nf, ny, nz)
-        solid = lax.dynamic_slice_in_dim(solid_mask, edge, 1, 0)
-        return jnp.concatenate([fields, solid.astype(F32)], 0).astype(BF)
+        half = 2 * nf + 1
+        c1 = jnp.concatenate([lax.ppermute(send_c[:half], "gy", down), lax.ppermute(send_c[half:], "gy", up)], 0)
 
     def both(pairs):
         return pairs + [(b, a) for a, b in pairs]
 
     inner = both([(k, k + 1) for k in range(0, ngx, 2)])
-    a = lax.ppermute(layers(even), "gx", inner)
+    a = lax.ppermute(send_a, "gx", inner)
     outer = [(k * ngx + i, k * ngx + i + 1) for k in range(2) for i in range(1, ngx - 1, 2)]
-    b = lax.ppermute(layers(~even), ("comp", "gx"), both(outer + [(0, ngx)]))
-
-    a4, b4 = a[: 2 * nf].reshape(nf, 2, ny, nz), b[: 2 * nf].reshape(nf, 2, ny, nz)
-    map_row = jnp.pad(iface_map.astype(BF), (0, nz - ny)).reshape(1, 1, nz)
-    pick = lambda v, l: [v[:, l, 0:1], v[:, l, ny - 1 : ny]]
-    extra = jnp.concatenate(
-        [b4[:, 0]] + pick(a4, 0) + pick(a4, 1) + pick(b4, 1)
-        + [jnp.broadcast_to(map_row, (nf, 1, nz)), jnp.zeros((nf, 9, nz), BF)], 1)
+    b = lax.ppermute(send_b, ("comp", "gx"), both(outer + [(0, ngx)]))
+
+    map_line = iface_map.reshape(1, ny)
+    extra = pl.pallas_call(
+        functools.partial(relay_kernel, dims),
+        out_shape=jax.ShapeDtypeStruct((nf, ny + 16, nz), BF),
+        in_specs=[VM] * 3,
+        out_specs=VM,
+        scratch_shapes=[pltpu.VMEM((16, nz), F32)],
+        compiler_params=pltpu.CompilerParams(vmem_limit_bytes=1 << 20),
+    )(map_line, a, b)
     if two:
         c2 = lax.ppermute(extra, "gy", swap)
         c2l, c2h, more = c2, c2, []
     else:
         c2l, c2h = lax.ppermute(extra, "gy", up), lax.ppermute(extra, "gy", down)
-        more = [lax.all_gather(b4[:, 0], "gy", axis=1, tiled=True),
+        more = [lax.all_gather(b[: 2 * nf : 2], "gy", axis=1, tiled=True),
                 lax.all_gather(iface_map, "gy", axis=0, tiled=True).reshape(1, -1)]
 
-    flat = q.reshape(nf, nx * ny, nz)
-    solid = solid_mask.reshape(nx * ny, nz)
     shape = jax.ShapeDtypeStruct((nf, nx * ny, nz), F32)
     cells = nf * nx * ny * nz
 
@@ -356,7 +389,7 @@
             in_specs=[SM, SM] + [VM] * (len(args) + 1),
             out_specs=VM,
             scratch_shapes=[pltpu.VMEM((nf, ny, nz), F32), pltpu.VMEM((nz, 2 * nz), BF)],
-            compiler_params=pltpu.CompilerParams(vmem_limit_bytes=20 << 20),
+            compiler_params=pltpu.CompilerParams(vmem_limit_bytes=3 << 20),
             cost_estimate=pl.CostEstimate(flops=20 * cells, bytes_accessed=8 * cells, transcendentals=cells // 4),
         )(diffusivity, advection, *args, solid)
 
@@ -373,9 +406,9 @@
             mb((8, nf, nx, nz), F32), mb((4, nf, ny, nz), F32), mb((2, nf, nx, 8, nz), F32),
             pltpu.SemaphoreType.DMA((4, 8)),
         ],
-        compiler_params=pltpu.CompilerParams(vmem_limit_bytes=40 << 20),
+        compiler_params=pltpu.CompilerParams(vmem_limit_bytes=10 << 20),
         cost_estimate=pl.CostEstimate(flops=10 * cells, bytes_accessed=8 * cells, transcendentals=cells // 4),
-    )(diffusivity, advection, iface_map.reshape(1, ny), flat, first, main.reshape(nf, nx, ny, nz), solid,
+    )(diffusivity, advection, map_line, flat, first, main.reshape(nf, nx, ny, nz), solid,
       a, b, c1, c2l, c2h, *more)[None]
 
 

time: 33.9 us -> 30.5 us (0.90)
  local copies, waits for them, and re-layouts: 8.65 us -> 3.14 us
  waiting for transfers between devices: 0.01 us -> 3.34 us
  other arithmetic: 0.81 us -> 0 us
  starting transfers between devices: 7.25 us -> 6.71 us
    ppermute x3, waiting for transfers between devices: 0.01 us -> 3.33 us  [the longest x1 3.33 us: body(): b = lax.ppermute(send_b, ('comp', 'gx'), both(outer + [(0, ngx)]))]
    unnamed x17 -> x14, local copies, waits for them, and re-layouts: 6.27 us -> 3.14 us
    another operation x1 -> x0, local copies, waits for them, and re-layouts: 1.08 us -> none
    slice x3 -> x0, local copies, waits for them, and re-layouts: 1.02 us -> none  [the longest x1 1 us: planes(): solid_mask[None, :, solid_row].astype(F32)]
    another operation x1 -> x0, other arithmetic: 0.75 us -> none
    pallas_call x0 -> x2, Pallas kernels: none -> 0.36 us  [the longest x1 0.3 us: body(): pl.pallas_call(functools.partial(gather_kernel, dims), out_shape=[jax.Sha...]
  transfers between devices with their start and end apart: 4 -> 4, of which waited for: 0 -> 1; matrix products, arithmetic and copies ran while one was open for 17% -> 0% of each run, Pallas kernels for 31% -> 34%
where the time goes in v2:
time: 30.5 us; the launch traced here: 30.3 us
  Pallas kernels  17 us (56%)
  starting transfers between devices  6.71 us (22%)
  waiting for transfers between devices  3.34 us (11%)
  local copies, waits for them, and re-layouts  3.14 us (10%)
    pallas_call x2, Pallas kernels, section(): pl.pallas_call(functools.partial(section_kernel, dims, second), out_shape...  10.3 us
    pallas_call x1, Pallas kernels, body(): pl.pallas_call(functools.partial(border_kernel, dims, two), out_shape=jax...  6.35 us
    ppermute x1, starting transfers between devices, body(): b = lax.ppermute(send_b, ('comp', 'gx'), both(outer + [(0, ngx)]))  3.42 us
    ppermute x1, waiting for transfers between devices, body(): b = lax.ppermute(send_b, ('comp', 'gx'), both(outer + [(0, ngx)]))  3.33 us
    unnamed x14, local copies, waits for them, and re-layouts  3.14 us
    ppermute x1, starting transfers between devices, body(): c1 = lax.ppermute(send_c, 'gy', swap)  3 us
  transfers between devices with their start and end apart: 4, of which 1 were waited for; matrix products, arithmetic and copies ran while one was open for 0% of the time, Pallas kernels for 34%

profile of v2, /device:TPU:0, one launch (start us, length us, event | category | flops | bytes accessed | tf_op | source)
XLA Modules:
  0.0 30.3 jit_solution(11015504972524626570)
XLA Ops:
  0.0 0.0 copy-start.6
  0.0 0.0 copy-start.5
  0.0 0.0 copy-start.4
  0.0 0.0 copy-start
  0.0 2.1 %copy-done = f32[1,7,32,32,128]{4,3,2,1,0:T(8,128)S(1)} copy-done((f32[1,7,32,32,128]{4,3,2,1,0:T(8,128)S(1)}, f32[1,7,32,32,128]{4,3,2,1,0:T(8,128)}, u32[]{:S(2)}) %copy-start) | copy-done | bytes 3670040
  2.1 0.0 copy-start.2
  2.1 1.0 %copy-done.2 = s32[32,32,128]{2,1,0:T(8,128)S(1)} copy-done((s32[32,32,128]{2,1,0:T(8,128)S(1)}, s32[32,32,128]{2,1,0:T(8,128)}, u32[]{:S(2)}) %copy-start.2) | copy-done | bytes 524312
  3.1 0.0 copy-start.1
  3.1 0.3 %shard_map.57 = (bf16[15,32,128]{2,1,0:T(8,128)(2,1)S(1)}, bf16[15,32,128]{2,1,0:T(8,128)(2,1)S(1)}, bf16[30,32,128]{2,1,0:T(8,128)(2,1)S(1)}) custom-call(f32[7,1024,128]{2,1,0:T(8,128)S(1)} %bitcast.5, s32[1024,128]{1,0:T(8,128)S(1)} %bitcast.10), custom_call_target="tpu_custom_call" | custom-call | tf_op jit(solution)/shard_map/pallas_call | solution.py:340
  3.4 3.0 %collective-permute-start.2 = (bf16[30,32,128]{2,1,0:T(8,128)(2,1)S(1)}, bf16[30,32,128]{2,1,0:T(8,128)(2,1)S(1)}, u32[]{:S(2)}, u32[]{:S(2)}) collective-permute-start(bf16[30,32,128]{2,1,0:T(8,128)(2,1)S(1)} %get-tuple-element.10), channel_id=1, source_target_pairs={{0,1},{1,0},{2,3},{3,2},{4,5},{5,4},{6,7},{7,6},{8,9},{9,8},{10,11... | collective-permute-start | bytes 737288 | tf_op jit(solution)/shard_map/ppermute | solution.py:350
  6.4 0.0 collective-permute-start
  6.4 3.4 %collective-permute-start.1 = (bf16[15,32,128]{2,1,0:T(8,128)(2,1)S(1)}, bf16[15,32,128]{2,1,0:T(8,128)(2,1)S(1)}, u32[]{:S(2)}, u32[]{:S(2)}) collective-permute-start(bf16[15,32,128]{2,1,0:T(8,128)(2,1)S(1)} %get-tuple-element.9), channel_id=1, source_target_pairs={{2,4},{6,8},{10,12},{18,20},{22,24},{26,28},{0,16},{4,2},{8,6},{12... | collective-permute-start | bytes 368648 | tf_op jit(solution)/shard_map/ppermute | solution.py:363
  9.9 0.0 collective-permute-done.a_ref.refs_7_
  9.9 3.3 %collective-permute-done.1.b_ref.refs_8_ = bf16[15,32,128]{2,1,0:T(8,128)(2,1)S(1)} collective-permute-done((bf16[15,32,128]{2,1,0:T(8,128)(2,1)S(1)}, bf16[15,32,128]{2,1,0:T(8,128)(2,1)S(1)}, u32[]{:S(2)}, u32[]{:S(2)}) %collective-permute-start.1) | collective-permute-done | bytes 122912 | tf_op jit(solution)/shard_map/ppermute | solution.py:363
  13.2 0.0 copy-done.6
  13.2 0.1 shard_map.58
  13.3 0.3 collective-permute-start.3
  13.6 0.0 copy-done.5
  13.6 0.0 copy-done.4
  13.6 0.0 copy-done.1
  13.6 5.0 %shard_map.55.refs_3_.refs_4_ = f32[7,1024,128]{2,1,0:T(8,128)S(1)} custom-call(f32[2,7]{1,0:T(2,128)S(1)} %copy-done.4, f32[2,7]{1,0:T(2,128)S(1)} %copy-done.5, f32[7,1024,128]{2,1,0:T(8,128)S(1)} %bitcast.6, s32[1024,128]{1,0:T(8,128)S(1)} %bitcast.11), custom_call_target="tpu_custom_call" | custom-call | flops 18350080 | bytes 7340032 | tf_op jit(solution)/shard_map/pallas_call | solution.py:386
  18.6 0.0 copy-start.3
  18.6 5.3 %shard_map.56 = f32[7,1024,128]{2,1,0:T(8,128)S(1)} custom-call(f32[2,7]{1,0:T(2,128)S(1)} %copy-done.4, f32[2,7]{1,0:T(2,128)S(1)} %copy-done.5, f32[7,1024,128]{2,1,0:T(8,128)S(1)} %bitcast.7, f32[7,1024,128]{2,1,0:T(8,128)S(1)} %shard_map.55.refs_3_.refs_4_, s32[1024,128]{1,0:T(8,128)S(1)} %bitcast.12), custom_call_target="tpu_custom_call" | custom-call | flops 18350080 | bytes 7340032 | tf_op jit(solution)/shard_map/pallas_call | solution.py:386
  23.9 0.0 collective-permute-done.3.refs_10_.refs_11_
  23.9 0.0 collective-permute-done.2.refs_9_
  23.9 0.0 copy-done.3
  24.0 6.3 %shard_map.59 = f32[7,32,32,128]{3,2,1,0:T(8,128)} custom-call(f32[2,7]{1,0:T(2,128)S(1)} %copy-done.4, f32[2,7]{1,0:T(2,128)S(1)} %copy-done.5, s32[1,32]{1,0:T(1,128)S(1)} %bitcast.15, f32[7,1024,128]{2,1,0:T(8,128)S(1)} %bitcast.8, f32[7,1024,128]{2,1,0:T(8,128)S(1)} %shard_map.55.refs_3_.refs_4_, f32[7,32,32,128]{3,2,1,0:T(8,128)S(1)} %bitcast.9, ...), custom_call_target="tpu_custom_call" | custom-call | flops 9175040 | bytes 7340032 | tf_op jit(solution)/shard_map/pallas_call | solution.py:399
Async XLA Ops:
  0.0 13.2 %copy-start.6 = (s32[32]{0:T(128)S(1)}, s32[32]{0:T(128)}, u32[]{:S(2)}) copy-start(s32[32]{0:T(128)} %param.9) | copy-start | bytes 388
  0.0 13.6 %copy-start.5 = (f32[2,7]{1,0:T(2,128)S(1)}, f32[2,7]{1,0:T(2,128)}, u32[]{:S(2)}) copy-start(f32[2,7]{1,0:T(2,128)} %refs_1_.5) | copy-start | bytes 172
  0.0 13.6 %copy-start.4 = (f32[2,7]{1,0:T(2,128)S(1)}, f32[2,7]{1,0:T(2,128)}, u32[]{:S(2)}) copy-start(f32[2,7]{1,0:T(2,128)} %refs_0_.5) | copy-start | bytes 172
  0.0 2.1 %copy-start = (f32[1,7,32,32,128]{4,3,2,1,0:T(8,128)S(1)}, f32[1,7,32,32,128]{4,3,2,1,0:T(8,128)}, u32[]{:S(2)}) copy-start(f32[1,7,32,32,128]{4,3,2,1,0:T(8,128)} %param.5) | copy-start | bytes 11010052
  2.1 1.0 %copy-start.2 = (s32[32,32,128]{2,1,0:T(8,128)S(1)}, s32[32,32,128]{2,1,0:T(8,128)}, u32[]{:S(2)}) copy-start(s32[32,32,128]{2,1,0:T(8,128)} %param.8) | copy-start | bytes 1572868
  3.1 10.4 %copy-start.1 = (f32[1,7,32,32,128]{4,3,2,1,0:T(8,128)S(1)}, f32[1,7,32,32,128]{4,3,2,1,0:T(8,128)}, u32[]{:S(2)}) copy-start(f32[1,7,32,32,128]{4,3,2,1,0:T(8,128)} %param.5) | copy-start | bytes 11010052
  3.4 20.5 %collective-permute-start.2 = (bf16[30,32,128]{2,1,0:T(8,128)(2,1)S(1)}, bf16[30,32,128]{2,1,0:T(8,128)(2,1)S(1)}, u32[]{:S(2)}, u32[]{:S(2)}) collective-permute-start(bf16[30,32,128]{2,1,0:T(8,128)(2,1)S(1)} %get-tuple-element.10), channel_id=1, source_target_pairs={{0,1},{1,0},{2,3},{3,2},{4,5},{5,4},{6,7},{7,6},{8,9},{9,8},{10,11... | collective-permute-start | bytes 737288 | tf_op jit(solution)/shard_map/ppermute | solution.py:350
  6.4 3.4 %collective-permute-start = (bf16[15,32,128]{2,1,0:T(8,128)(2,1)S(1)}, bf16[15,32,128]{2,1,0:T(8,128)(2,1)S(1)}, u32[]{:S(2)}, u32[]{:S(2)}) collective-permute-start(bf16[15,32,128]{2,1,0:T(8,128)(2,1)S(1)} %get-tuple-element.8), channel_id=1, source_target_pairs={{0,2},{4,6},{8,10},{12,14},{2,0},{6,4},{10,8},{14,12},{1,3},{5,7},... | collective-permute-start | bytes 368648 | tf_op jit(solution)/shard_map/ppermute | solution.py:361
  6.4 6.8 %collective-permute-start.1 = (bf16[15,32,128]{2,1,0:T(8,128)(2,1)S(1)}, bf16[15,32,128]{2,1,0:T(8,128)(2,1)S(1)}, u32[]{:S(2)}, u32[]{:S(2)}) collective-permute-start(bf16[15,32,128]{2,1,0:T(8,128)(2,1)S(1)} %get-tuple-element.9), channel_id=1, source_target_pairs={{2,4},{6,8},{10,12},{18,20},{22,24},{26,28},{0,16},{4,2},{8,6},{12... | collective-permute-start | bytes 368648 | tf_op jit(solution)/shard_map/ppermute | solution.py:363
  13.3 10.7 %collective-permute-start.3 = (bf16[7,48,128]{2,1,0:T(8,128)(2,1)S(1)}, bf16[7,48,128]{2,1,0:T(8,128)(2,1)S(1)}, u32[]{:S(2)}, u32[]{:S(2)}) collective-permute-start(bf16[7,48,128]{2,1,0:T(8,128)(2,1)S(1)} %shard_map.58), channel_id=1, source_target_pairs={{0,1},{1,0},{2,3},{3,2},{4,5},{5,4},{6,7},{7,6},{8,9},{9,8},{10,11... | collective-permute-start | bytes 258056 | tf_op jit(solution)/shard_map/ppermute | solution.py:375
  18.6 5.3 %copy-start.3 = (s32[32,32,128]{2,1,0:T(8,128)S(1)}, s32[32,32,128]{2,1,0:T(8,128)}, u32[]{:S(2)}) copy-start(s32[32,32,128]{2,1,0:T(8,128)} %param.8) | copy-start | bytes 1572868

commit v3 on v2

--- a/solution.py
+++ b/solution.py
@@ -59,7 +59,7 @@
         c_ref[k] = s_ref[pl.ds(y, nx, stride=ny)].astype(F32).astype(BF)
 
 
-def relay_kernel(dims, imap, a_ref, b_ref, o_ref, rows):
+def relay_kernel(dims, imap, a_ref, b_ref, after_ref, o_ref, rows):
     nf, nx, ny, nz = dims
     rows[...] = jnp.zeros_like(rows)
     rows[6:7, :ny] = imap[...].astype(F32)
@@ -72,49 +72,109 @@
         o_ref[f, ny:] = rows[...].astype(BF)
 
 
+def shift_pair(nz, down):
+    row = lax.broadcasted_iota(jnp.int32, (2 * nz, 2 * nz), 0)
+    col = lax.broadcasted_iota(jnp.int32, (2 * nz, 2 * nz), 1)
+    second = col >= nz
+    k = jnp.where(second, col - nz, col)
+    if down:
+        other = jnp.where(k == 0, nz - 1, k - 1)
+    else:
+        other = jnp.where(k == nz - 1, 0, k + 1)
+    other = jnp.where(second, other + nz, other)
+    one = lambda c: jnp.where(c, 1.0, 0.0)
+    diff = one(row == other) - one(row == col)
+    return (-diff if down else diff).astype(BF)
+
+
 def section_kernel(dims, second, *refs):
     nf, nx, ny, nz = dims
-    if second:
-        dif, adv, base_ref, q_ref, s_ref, o_ref, fx, sm = refs
-    else:
-        dif, adv, q_ref, s_ref, o_ref, fx, sm = refs
-    d, c, level = scalars(dif, adv, nf)
-    fx[...] = jnp.zeros_like(fx)
-    sm[...] = shift_matrix(nz)
-    step_x = 2
-
-    def at(x):
-        return pl.ds(pl.multiple_of(x * ny, ny), ny)
-
-    def step(i, gc):
-        diffs = []
-        for k in range(step_x):
-            rows = q_ref[:, at(i * step_x + k)].astype(BF).reshape(nf * ny, nz)
-            diffs.append(jnp.dot(rows, sm[...], preferred_element_type=F32))
-        for k in range(step_x):
-            x = i * step_x + k
-            here, east, west = at(x), at(jnp.minimum(x + 1, nx - 1)), at(jnp.maximum(x - 1, 0))
-            ge = gain(q_ref[4, east])
-            gx, gy, gz = gc + ge, gc + pltpu.roll(gc, ny - 1, 0), gc + pltpu.roll(gc, nz - 1, 1)
-            gzl = pltpu.roll(gz, 1, 1)
-            m, a = masks(s_ref[here] >= level)
-            for f in range(nf):
-                q, qe, qw = q_ref[f, here], q_ref[f, east], q_ref[f, west]
-                flux = gx * (qe - q)
-                total = flux - fx[f]
-                fx[f] = flux
-                fy = gy * (pltpu.roll(q, ny - 1, 0) - q)
-                total += fy - pltpu.roll(fy, 1, 0)
-                z = diffs[k][f * ny : (f + 1) * ny]
-                total += gz * z[:, :nz] - gzl * z[:, nz:]
-                new = q + (d[f] * (m * total) - c[f] * (a * (qe - qw)))
-                if second:
-                    new = 0.5 * (base_ref[f, here] + new)
-                o_ref[f, here] = new
-            gc = ge
-        return gc
-
-    lax.fori_loop(0, nx // step_x, step, gain(q_ref[4, at(0)]))
+    pairs = [(6, None), (4, 5), (0, 1), (2, 3)]
+    parts = ny // 8
+
+    def run(*accs):
+        if second:
+            dif, adv, base_ref, q_ref, s_ref, o_ref, fx, gs = refs
+        else:
+            dif, adv, q_ref, s_ref, o_ref, fx, gs = refs
+        n = len(pairs)
+        ups, downs = (accs[:n], accs[n : 2 * n]), (accs[2 * n : 3 * n], accs[3 * n :])
+        d, c, level = scalars(dif, adv, nf)
+        fx[...] = jnp.zeros_like(fx)
+        pltpu.matmul_push_rhs(shift_pair(nz, False), staging_register=0, mxu_index=0)
+        pltpu.matmul_push_rhs(shift_pair(nz, True), staging_register=0, mxu_index=1)
+
+        def at(x, k):
+            return pl.ds(x * ny + k, 8, stride=parts)
+
+        def layer(f, x):
+            return [q_ref[f, at(x, k)] for k in range(parts)]
+
+        def tall(v):
+            return jnp.concatenate(v, 0).astype(BF)
+
+        def push(x, bank, g, load=None):
+            for p, (f0, f1) in enumerate(pairs):
+                lhs = jnp.concatenate([tall(layer(f0, x)), tall(g if f1 is None else layer(f1, x))], 1)
+                pltpu.matmul_acc_lhs(ups[bank][p], lhs, load_staged_rhs=load)
+                pltpu.matmul_acc_lhs(downs[bank][p], lhs, load_staged_rhs=load)
+                load = None
+
+        def prepare(x, bank, g):
+            ge = [gain(v) for v in layer(4, jnp.minimum(x + 1, nx - 1))]
+            for k in range(parts):
+                gs[bank, 0, k] = g[k] + ge[k]
+                gs[bank, 1, k] = g[k] + (g[k + 1] if k + 1 < parts else pltpu.roll(g[0], 7, 0))
+                gs[bank, 2, k] = g[k] + g[k]
+                m, a = masks(s_ref[at(jnp.minimum(x, nx - 1), k)] >= level)
+                gs[bank, 3, k] = m
+                gs[bank, 4, k] = a
+            return ge
+
+        def compute(x, bank):
+            xe, xw = jnp.minimum(x + 1, nx - 1), jnp.maximum(x - 1, 0)
+            for p, pair in enumerate(pairs):
+                up, down = pltpu.matmul_pop(ups[bank][p]), pltpu.matmul_pop(downs[bank][p])
+                piece = lambda v, k, h: v[8 * k : 8 * k + 8, h * nz : (h + 1) * nz]
+                if pair[1] is None:
+                    gz = [gs[bank, 2, k] + piece(up, k, 1) for k in range(parts)]
+                    gzl = [gs[bank, 2, k] - piece(down, k, 1) for k in range(parts)]
+                for h, f in enumerate(pair):
+                    if f is None:
+                        continue
+                    q = layer(f, x)
+                    fy = [gs[bank, 1, k] * ((q[k + 1] if k + 1 < parts else pltpu.roll(q[0], 7, 0)) - q[k])
+                          for k in range(parts)]
+                    for k in range(parts):
+                        qe, qw = q_ref[f, at(xe, k)], q_ref[f, at(xw, k)]
+                        flux = gs[bank, 0, k] * (qe - q[k])
+                        total = flux - fx[f, k]
+                        fx[f, k] = flux
+                        total += fy[k] - (fy[k - 1] if k else pltpu.roll(fy[-1], 1, 0))
+                        total += gz[k] * piece(up, k, h) - gzl[k] * piece(down, k, h)
+                        new = q[k] + (d[f] * (gs[bank, 3, k] * total) - c[f] * (gs[bank, 4, k] * (qe - qw)))
+                        if second:
+                            new = 0.5 * (base_ref[f, at(x, k)] + new)
+                        o_ref[f, at(x, k)] = new
+
+        def step(i, g):
+            x = 2 * i
+            push(x + 1, 1, g)
+            g = prepare(x + 1, 1, g)
+            compute(x, 0)
+            push(jnp.minimum(x + 2, nx - 1), 0, g)
+            g = prepare(x + 2, 0, g)
+            compute(x + 1, 1)
+            return g
+
+        g = [gain(v) for v in layer(4, 0)]
+        push(0, 0, g, 0)
+        lax.fori_loop(0, nx // 2, step, prepare(0, 0, g))
+        for acc in ups[0] + downs[0]:
+            pltpu.matmul_pop(acc)
+
+    accs = [pltpu.ACC(m)((ny, 2 * nz), F32) for m in (0, 1) for _ in range(2 * len(pairs))]
+    pl.run_scoped(run, *accs)
 
 
 def border_kernel(dims, two, *refs):
@@ -362,15 +422,30 @@
     outer = [(k * ngx + i, k * ngx + i + 1) for k in range(2) for i in range(1, ngx - 1, 2)]
     b = lax.ppermute(send_b, ("comp", "gx"), both(outer + [(0, ngx)]))
 
+    shape = jax.ShapeDtypeStruct((nf, nx * ny, nz), F32)
+    cells = nf * nx * ny * nz
+
+    def section(second, *args):
+        return pl.pallas_call(
+            functools.partial(section_kernel, dims, second),
+            out_shape=shape,
+            in_specs=[SM, SM] + [VM] * (len(args) + 1),
+            out_specs=VM,
+            scratch_shapes=[pltpu.VMEM((nf, ny // 8, 8, nz), F32), pltpu.VMEM((2, 5, ny // 8, 8, nz), F32)],
+            compiler_params=pltpu.CompilerParams(vmem_limit_bytes=3 << 20),
+            cost_estimate=pl.CostEstimate(flops=20 * cells, bytes_accessed=8 * cells, transcendentals=cells // 4),
+        )(diffusivity, advection, *args, solid)
+
+    first = section(False, flat)
     map_line = iface_map.reshape(1, ny)
     extra = pl.pallas_call(
         functools.partial(relay_kernel, dims),
         out_shape=jax.ShapeDtypeStruct((nf, ny + 16, nz), BF),
-        in_specs=[VM] * 3,
+        in_specs=[VM] * 3 + [HB],
         out_specs=VM,
         scratch_shapes=[pltpu.VMEM((16, nz), F32)],
         compiler_params=pltpu.CompilerParams(vmem_limit_bytes=1 << 20),
-    )(map_line, a, b)
+    )(map_line, a, b, first)
     if two:
         c2 = lax.ppermute(extra, "gy", swap)
         c2l, c2h, more = c2, c2, []
@@ -379,21 +454,6 @@
         more = [lax.all_gather(b[: 2 * nf : 2], "gy", axis=1, tiled=True),
                 lax.all_gather(iface_map, "gy", axis=0, tiled=True).reshape(1, -1)]
 
-    shape = jax.ShapeDtypeStruct((nf, nx * ny, nz), F32)
-    cells = nf * nx * ny * nz
-
-    def section(second, *args):
-        return pl.pallas_call(
-            functools.partial(section_kernel, dims, second),
-            out_shape=shape,
-            in_specs=[SM, SM] + [VM] * (len(args) + 1),
-            out_specs=VM,
-            scratch_shapes=[pltpu.VMEM((nf, ny, nz), F32), pltpu.VMEM((nz, 2 * nz), BF)],
-            compiler_params=pltpu.CompilerParams(vmem_limit_bytes=3 << 20),
-            cost_estimate=pl.CostEstimate(flops=20 * cells, bytes_accessed=8 * cells, transcendentals=cells // 4),
-        )(diffusivity, advection, *args, solid)
-
-    first = section(False, flat)
     main = section(True, flat, first)
     mb = pltpu.VMEM
     return pl.pallas_call(

time: 30.5 us -> 26 us (0.85)
  waiting for transfers between devices: 3.34 us -> 0.02 us
  Pallas kernels: 17 us -> 15.4 us
  starting transfers between devices: 6.71 us -> 7.16 us
    ppermute x1, waiting for transfers between devices: 3.33 us -> 0.01 us  [body(): b = lax.ppermute(send_b, ('comp', 'gx'), both(outer + [(0, ngx)]))]
    pallas_call x2, Pallas kernels: 10.3 us -> 8.69 us  [section(): pl.pallas_call(functools.partial(section_kernel, dims, second), out_shape...]
    ppermute x1, starting transfers between devices: 0.29 us -> 0.61 us  [body(): c2 = lax.ppermute(extra, 'gy', swap)]
  transfers between devices with their start and end apart: 4 -> 4, of which waited for: 1 -> 0; matrix products, arithmetic and copies ran while one was open for 0% -> 0% of each run, Pallas kernels for 34% -> 34%
where the time goes in v3:
time: 26 us; the launch traced here: 25.8 us
  Pallas kernels  15.4 us (59%)
  starting transfers between devices  7.16 us (28%)
  local copies, waits for them, and re-layouts  3.12 us (12%)
    pallas_call x2, Pallas kernels, section(): pl.pallas_call(functools.partial(section_kernel, dims, second), out_shape...  8.69 us
    pallas_call x1, Pallas kernels, body(): pl.pallas_call(functools.partial(border_kernel, dims, two), out_shape=jax...  6.34 us
    ppermute x1, starting transfers between devices, body(): b = lax.ppermute(send_b, ('comp', 'gx'), both(outer + [(0, ngx)]))  3.55 us
    unnamed x14, local copies, waits for them, and re-layouts  3.12 us
    ppermute x1, starting transfers between devices, body(): c1 = lax.ppermute(send_c, 'gy', swap)  3 us
    ppermute x1, starting transfers between devices, body(): c2 = lax.ppermute(extra, 'gy', swap)  0.61 us
  transfers between devices with their start and end apart: 4, of which 0 were waited for; matrix products, arithmetic and copies ran while one was open for 0% of the time, Pallas kernels for 34%

profile of v3, /device:TPU:0, one launch (start us, length us, event | category | flops | bytes accessed | tf_op | source)
XLA Modules:
  0.0 25.8 jit_solution(3276790895289626452)
XLA Ops:
  0.0 0.0 copy-start.5
  0.0 0.0 copy-start.4
  0.0 0.0 copy-start
  0.0 2.1 %copy-done = f32[1,7,32,32,128]{4,3,2,1,0:T(8,128)S(1)} copy-done((f32[1,7,32,32,128]{4,3,2,1,0:T(8,128)S(1)}, f32[1,7,32,32,128]{4,3,2,1,0:T(8,128)}, u32[]{:S(2)}) %copy-start) | copy-done | bytes 3670040
  2.1 0.0 copy-start.2
  2.1 1.0 %copy-done.2 = s32[32,32,128]{2,1,0:T(8,128)S(1)} copy-done((s32[32,32,128]{2,1,0:T(8,128)S(1)}, s32[32,32,128]{2,1,0:T(8,128)}, u32[]{:S(2)}) %copy-start.2) | copy-done | bytes 524312
  3.1 0.0 copy-start.1
  3.1 0.3 %shard_map.57 = (bf16[15,32,128]{2,1,0:T(8,128)(2,1)S(1)}, bf16[15,32,128]{2,1,0:T(8,128)(2,1)S(1)}, bf16[30,32,128]{2,1,0:T(8,128)(2,1)S(1)}) custom-call(f32[7,1024,128]{2,1,0:T(8,128)S(1)} %bitcast.5, s32[1024,128]{1,0:T(8,128)S(1)} %bitcast.10), custom_call_target="tpu_custom_call" | custom-call | tf_op jit(solution)/shard_map/pallas_call | solution.py:400
  3.4 3.0 %collective-permute-start.2 = (bf16[30,32,128]{2,1,0:T(8,128)(2,1)S(1)}, bf16[30,32,128]{2,1,0:T(8,128)(2,1)S(1)}, u32[]{:S(2)}, u32[]{:S(2)}) collective-permute-start(bf16[30,32,128]{2,1,0:T(8,128)(2,1)S(1)} %get-tuple-element.10), channel_id=1, source_target_pairs={{0,1},{1,0},{2,3},{3,2},{4,5},{5,4},{6,7},{7,6},{8,9},{9,8},{10,11... | collective-permute-start | bytes 737288 | tf_op jit(solution)/shard_map/ppermute | solution.py:410
  6.4 0.0 collective-permute-start
  6.4 0.0 copy-start.6
  6.4 3.5 %collective-permute-start.1 = (bf16[15,32,128]{2,1,0:T(8,128)(2,1)S(1)}, bf16[15,32,128]{2,1,0:T(8,128)(2,1)S(1)}, u32[]{:S(2)}, u32[]{:S(2)}) collective-permute-start(bf16[15,32,128]{2,1,0:T(8,128)(2,1)S(1)} %get-tuple-element.9), channel_id=1, source_target_pairs={{2,4},{6,8},{10,12},{18,20},{22,24},{26,28},{0,16},{4,2},{8,6},{12... | collective-permute-start | bytes 368648 | tf_op jit(solution)/shard_map/ppermute | solution.py:423
  10.0 0.0 copy-done.5
  10.0 0.0 copy-done.4
  10.0 0.0 copy-done.1
  10.0 4.1 %shard_map.55.refs_3_.after_ref.refs_4_ = f32[7,1024,128]{2,1,0:T(8,128)S(1)} custom-call(f32[2,7]{1,0:T(2,128)S(1)} %copy-done.4, f32[2,7]{1,0:T(2,128)S(1)} %copy-done.5, f32[7,1024,128]{2,1,0:T(8,128)S(1)} %bitcast.6, s32[1024,128]{1,0:T(8,128)S(1)} %bitcast.11), custom_call_target="tpu_custom_call" | custom-call | flops 18350080 | bytes 7340032 | tf_op jit(solution)/shard_map/pallas_call | solution.py:429
  14.2 0.0 collective-permute-done.a_ref.refs_7_
  14.2 0.0 collective-permute-done.1.b_ref.refs_8_
  14.2 0.0 copy-done.6
  14.2 0.1 shard_map.58
  14.2 0.0 copy-start.3
  14.3 0.6 %collective-permute-start.3 = (bf16[7,48,128]{2,1,0:T(8,128)(2,1)S(1)}, bf16[7,48,128]{2,1,0:T(8,128)(2,1)S(1)}, u32[]{:S(2)}, u32[]{:S(2)}) collective-permute-start(bf16[7,48,128]{2,1,0:T(8,128)(2,1)S(1)} %shard_map.58), channel_id=1, source_target_pairs={{0,1},{1,0},{2,3},{3,2},{4,5},{5,4},{6,7},{7,6},{8,9},{9,8},{10,11... | collective-permute-start | bytes 258056 | tf_op jit(solution)/shard_map/ppermute | solution.py:450
  14.9 4.6 %shard_map.56 = f32[7,1024,128]{2,1,0:T(8,128)S(1)} custom-call(f32[2,7]{1,0:T(2,128)S(1)} %copy-done.4, f32[2,7]{1,0:T(2,128)S(1)} %copy-done.5, f32[7,1024,128]{2,1,0:T(8,128)S(1)} %bitcast.7, f32[7,1024,128]{2,1,0:T(8,128)S(1)} %shard_map.55.refs_3_.after_ref.refs_4_, s32[1024,128]{1,0:T(8,128)S(1)} %bitcast.12), custom_call_target="tpu_custom_call" | custom-call | flops 18350080 | bytes 7340032 | tf_op jit(solution)/shard_map/pallas_call | solution.py:429
  19.4 0.0 collective-permute-done.3.refs_10_.refs_11_
  19.4 0.0 collective-permute-done.2.refs_9_
  19.5 0.0 copy-done.3
  19.5 6.3 %shard_map.59 = f32[7,32,32,128]{3,2,1,0:T(8,128)} custom-call(f32[2,7]{1,0:T(2,128)S(1)} %copy-done.4, f32[2,7]{1,0:T(2,128)S(1)} %copy-done.5, s32[1,32]{1,0:T(1,128)S(1)} %bitcast.15, f32[7,1024,128]{2,1,0:T(8,128)S(1)} %bitcast.8, f32[7,1024,128]{2,1,0:T(8,128)S(1)} %shard_map.55.refs_3_.after_ref.refs_4_, f32[7,32,32,128]{3,2,1,0:T(8,128)S(1)} %bitcast.9, ...), custom_call_target="tpu_custom_call" | custom-call | flops 9175040 | bytes 7340032 | tf_op jit(solution)/shard_map/pallas_call | solution.py:459
Async XLA Ops:
  0.0 10.0 %copy-start.5 = (f32[2,7]{1,0:T(2,128)S(1)}, f32[2,7]{1,0:T(2,128)}, u32[]{:S(2)}) copy-start(f32[2,7]{1,0:T(2,128)} %refs_1_.5) | copy-start | bytes 172
  0.0 10.0 %copy-start.4 = (f32[2,7]{1,0:T(2,128)S(1)}, f32[2,7]{1,0:T(2,128)}, u32[]{:S(2)}) copy-start(f32[2,7]{1,0:T(2,128)} %refs_0_.5) | copy-start | bytes 172
  0.0 2.1 %copy-start = (f32[1,7,32,32,128]{4,3,2,1,0:T(8,128)S(1)}, f32[1,7,32,32,128]{4,3,2,1,0:T(8,128)}, u32[]{:S(2)}) copy-start(f32[1,7,32,32,128]{4,3,2,1,0:T(8,128)} %param.5) | copy-start | bytes 11010052
  2.1 1.0 %copy-start.2 = (s32[32,32,128]{2,1,0:T(8,128)S(1)}, s32[32,32,128]{2,1,0:T(8,128)}, u32[]{:S(2)}) copy-start(s32[32,32,128]{2,1,0:T(8,128)} %param.8) | copy-start | bytes 1572868
  3.1 6.9 %copy-start.1 = (f32[1,7,32,32,128]{4,3,2,1,0:T(8,128)S(1)}, f32[1,7,32,32,128]{4,3,2,1,0:T(8,128)}, u32[]{:S(2)}) copy-start(f32[1,7,32,32,128]{4,3,2,1,0:T(8,128)} %param.5) | copy-start | bytes 11010052
  3.4 16.0 %collective-permute-start.2 = (bf16[30,32,128]{2,1,0:T(8,128)(2,1)S(1)}, bf16[30,32,128]{2,1,0:T(8,128)(2,1)S(1)}, u32[]{:S(2)}, u32[]{:S(2)}) collective-permute-start(bf16[30,32,128]{2,1,0:T(8,128)(2,1)S(1)} %get-tuple-element.10), channel_id=1, source_target_pairs={{0,1},{1,0},{2,3},{3,2},{4,5},{5,4},{6,7},{7,6},{8,9},{9,8},{10,11... | collective-permute-start | bytes 737288 | tf_op jit(solution)/shard_map/ppermute | solution.py:410
  6.4 7.7 %collective-permute-start = (bf16[15,32,128]{2,1,0:T(8,128)(2,1)S(1)}, bf16[15,32,128]{2,1,0:T(8,128)(2,1)S(1)}, u32[]{:S(2)}, u32[]{:S(2)}) collective-permute-start(bf16[15,32,128]{2,1,0:T(8,128)(2,1)S(1)} %get-tuple-element.8), channel_id=1, source_target_pairs={{0,2},{4,6},{8,10},{12,14},{2,0},{6,4},{10,8},{14,12},{1,3},{5,7},... | collective-permute-start | bytes 368648 | tf_op jit(solution)/shard_map/ppermute | solution.py:421
  6.4 7.8 %copy-start.6 = (s32[32]{0:T(128)S(1)}, s32[32]{0:T(128)}, u32[]{:S(2)}) copy-start(s32[32]{0:T(128)} %param.9) | copy-start | bytes 388
  6.4 7.7 %collective-permute-start.1 = (bf16[15,32,128]{2,1,0:T(8,128)(2,1)S(1)}, bf16[15,32,128]{2,1,0:T(8,128)(2,1)S(1)}, u32[]{:S(2)}, u32[]{:S(2)}) collective-permute-start(bf16[15,32,128]{2,1,0:T(8,128)(2,1)S(1)} %get-tuple-element.9), channel_id=1, source_target_pairs={{2,4},{6,8},{10,12},{18,20},{22,24},{26,28},{0,16},{4,2},{8,6},{12... | collective-permute-start | bytes 368648 | tf_op jit(solution)/shard_map/ppermute | solution.py:423
  14.2 5.2 %copy-start.3 = (s32[32,32,128]{2,1,0:T(8,128)S(1)}, s32[32,32,128]{2,1,0:T(8,128)}, u32[]{:S(2)}) copy-start(s32[32,32,128]{2,1,0:T(8,128)} %param.8) | copy-start | bytes 1572868
  14.3 5.2 %collective-permute-start.3 = (bf16[7,48,128]{2,1,0:T(8,128)(2,1)S(1)}, bf16[7,48,128]{2,1,0:T(8,128)(2,1)S(1)}, u32[]{:S(2)}, u32[]{:S(2)}) collective-permute-start(bf16[7,48,128]{2,1,0:T(8,128)(2,1)S(1)} %shard_map.58), channel_id=1, source_target_pairs={{0,1},{1,0},{2,3},{3,2},{4,5},{5,4},{6,7},{7,6},{8,9},{9,8},{10,11... | collective-permute-start | bytes 258056 | tf_op jit(solution)/shard_map/ppermute | solution.py:450

commit v4 on v3

--- a/solution.py
+++ b/solution.py
@@ -9,12 +9,13 @@
 
 RATIO = 1.5
 GAIN = 0.4
+LOG2E = 1.4426950408889634
 BF = jnp.bfloat16
 F32 = jnp.float32
 
 
 def gain(q):
-    return 0.5 * jnp.exp(GAIN * jnp.tanh(q))
+    return jnp.exp2(GAIN * LOG2E * jnp.tanh(q) - 1.0)
 
 
 def shift_matrix(nz):
@@ -100,6 +101,9 @@
         n = len(pairs)
         ups, downs = (accs[:n], accs[n : 2 * n]), (accs[2 * n : 3 * n], accs[3 * n :])
         d, c, level = scalars(dif, adv, nf)
+        lo, hi = (1, nx - 2) if second else (0, nx - 1)
+        closed = (0, ny - 2) if second else (ny - 1,)
+        sub = lax.broadcasted_iota(jnp.int32, (8, nz), 0)
         fx[...] = jnp.zeros_like(fx)
         pltpu.matmul_push_rhs(shift_pair(nz, False), staging_register=0, mxu_index=0)
         pltpu.matmul_push_rhs(shift_pair(nz, True), staging_register=0, mxu_index=1)
@@ -121,18 +125,22 @@
                 load = None
 
         def prepare(x, bank, g):
-            ge = [gain(v) for v in layer(4, jnp.minimum(x + 1, nx - 1))]
+            ge = [gain(v) for v in layer(4, jnp.minimum(x + 1, hi))]
             for k in range(parts):
                 gs[bank, 0, k] = g[k] + ge[k]
-                gs[bank, 1, k] = g[k] + (g[k + 1] if k + 1 < parts else pltpu.roll(g[0], 7, 0))
+                face = g[k] + (g[k + 1] if k + 1 < parts else pltpu.roll(g[0], 7, 0))
+                for y in closed:
+                    if y % parts == k:
+                        face = jnp.where(sub == y // parts, 0.0, face)
+                gs[bank, 1, k] = face
                 gs[bank, 2, k] = g[k] + g[k]
-                m, a = masks(s_ref[at(jnp.minimum(x, nx - 1), k)] >= level)
+                m, a = masks(s_ref[at(jnp.minimum(x, hi), k)] >= level)
                 gs[bank, 3, k] = m
                 gs[bank, 4, k] = a
             return ge
 
         def compute(x, bank):
-            xe, xw = jnp.minimum(x + 1, nx - 1), jnp.maximum(x - 1, 0)
+            xe, xw = jnp.minimum(x + 1, hi), jnp.maximum(x - 1, lo)
             for p, pair in enumerate(pairs):
                 up, down = pltpu.matmul_pop(ups[bank][p]), pltpu.matmul_pop(downs[bank][p])
                 piece = lambda v, k, h: v[8 * k : 8 * k + 8, h * nz : (h + 1) * nz]
@@ -158,18 +166,18 @@
                         o_ref[f, at(x, k)] = new
 
         def step(i, g):
-            x = 2 * i
+            x = 2 * i + lo
             push(x + 1, 1, g)
             g = prepare(x + 1, 1, g)
             compute(x, 0)
-            push(jnp.minimum(x + 2, nx - 1), 0, g)
+            push(jnp.minimum(x + 2, hi), 0, g)
             g = prepare(x + 2, 0, g)
             compute(x + 1, 1)
             return g
 
-        g = [gain(v) for v in layer(4, 0)]
-        push(0, 0, g, 0)
-        lax.fori_loop(0, nx // 2, step, prepare(0, 0, g))
+        g = [gain(v) for v in layer(4, lo)]
+        push(lo, 0, g, 0)
+        lax.fori_loop(0, (hi + 1 - lo) // 2, step, prepare(lo, 0, g))
         for acc in ups[0] + downs[0]:
             pltpu.matmul_pop(acc)
 
@@ -186,11 +194,12 @@
         (dif, adv, imap, q_ref, first_ref, main_ref, s_ref, a_ref, b_ref, c1_ref, c2l_ref, c2h_ref,
          face_ref, map_ref) = refs[:14]
         rest = refs[14:]
-    out_ref, sm, lay, cor, fl, fp, ol, strips, sem = rest
+    out_ref, sm, lay, pla, ms, cor, fl, fp, cx, cy, ol, strips, zin, zout, sem = rest
     d, c, level = scalars(dif, adv, nf)
     comp = lax.axis_index("comp")
     stream, last = lax.axis_index("gx"), lax.axis_size("gx") - 1
     even = stream % 2 == 0
+    parts = ny // 8
     sm[...] = shift_matrix(nz)
 
     mids = []
@@ -204,21 +213,28 @@
         cuts.append(pltpu.make_async_copy(main_ref.at[:, :, pl.ds(row, 8)], strips.at[k], sem.at[1, k]))
         cuts[-1].start()
 
-    LF, LN, HN, HF = range(4)
+    FAR_LO, LO, HI, FAR_HI = range(4)
+    inside = jnp.where(stream == last, 0.0, 1.0)
     for f in range(nf):
         av = [a_ref[2 * f].astype(F32), a_ref[2 * f + 1].astype(F32)]
         bv = [b_ref[2 * f].astype(F32), b_ref[2 * f + 1].astype(F32)]
-        lay[LF, f] = jnp.where(even, bv[0], av[0])
-        lay[LN, f] = jnp.where(even, bv[1], av[1])
-        zero = jnp.where(stream == last, 0.0, 1.0)
-        lay[HN, f] = jnp.where(even, av[0], bv[0]) * zero
-        lay[HF, f] = jnp.where(even, av[1], bv[1]) * zero
+        lay[FAR_LO, f] = jnp.where(even, bv[0], av[0])
+        lay[LO, f] = jnp.where(even, bv[1], av[1])
+        lay[HI, f] = jnp.where(even, av[0], bv[0]) * inside
+        lay[FAR_HI, f] = jnp.where(even, av[1], bv[1]) * inside
+        for n, k in enumerate((2 * nf + 1, 3 * nf + 1, 0, nf)):
+            pla[n, f] = c1_ref[k + f].astype(F32)
         lo, hi = c2l_ref[f, pl.ds(ny, 16)].astype(F32), c2h_ref[f, pl.ds(ny, 16)].astype(F32)
         lo_b, hi_b = c2l_ref[f, pl.ds(ny - 16, 16)].astype(F32), c2h_ref[f, pl.ds(0, 16)].astype(F32)
         cor[0, f : f + 1] = jnp.where(even, lo[5:6], lo[3:4])
         cor[1, f : f + 1] = jnp.where(even, hi[4:5], hi[2:3])
-        cor[2, f : f + 1] = jnp.where(even, lo[1:2], lo_b[15:16]) * zero
-        cor[3, f : f + 1] = jnp.where(even, hi[0:1], hi_b[0:1]) * zero
+        cor[2, f : f + 1] = jnp.where(even, lo[1:2], lo_b[15:16]) * inside
+        cor[3, f : f + 1] = jnp.where(even, hi[0:1], hi_b[0:1]) * inside
+    am, bm = a_ref[2 * nf].astype(F32), b_ref[2 * nf].astype(F32)
+    ms[0] = jnp.where(even, bm, am)
+    ms[1] = jnp.where(even, am, bm)
+    ms[2] = c1_ref[4 * nf + 1].astype(F32)
+    ms[3] = c1_ref[2 * nf].astype(F32)
 
     @pl.when(stream == 0)
     def _():
@@ -233,7 +249,7 @@
             whole = face_ref.shape[1]
             mapping = map_ref[...].astype(F32)
             order = 0
-        rows = 40
+        rows = ny + 8
         r = lax.broadcasted_iota(jnp.int32, (rows, whole), 0)
         want = jnp.where(r < ny, r, jnp.where(r == ny, whole - 1, ny)) + start
         want = jnp.where(want >= whole, want - whole, want).astype(F32)
@@ -249,138 +265,178 @@
         choose = jnp.where(comp == 1, inlet, feed).astype(BF)
         for f in range(nf):
             if two:
-                layer = jnp.concatenate([b_ref[2 * f], c2l_ref[f, pl.ds(0, ny)]], axis=0)
+                face = jnp.concatenate([b_ref[2 * f], c2l_ref[f, pl.ds(0, ny)]], axis=0)
             else:
-                layer = face_ref[f]
-            ghost = jnp.dot(choose, layer, preferred_element_type=F32)
-            lay[LN, f] = ghost[:ny]
+                face = face_ref[f]
+            ghost = jnp.dot(choose, face, preferred_element_type=F32)
+            lay[LO, f] = ghost[:ny]
             cor[0, f : f + 1] = ghost[ny : ny + 1]
             cor[1, f : f + 1] = ghost[ny + 1 : ny + 2]
 
-    row = lax.broadcasted_iota(jnp.int32, (ny, nz), 0)
-
-    def slab(center, before, after, low, high, solid, along_outer):
-        rows = jnp.concatenate([center(f).astype(BF) for f in range(nf)], axis=0)
-        diffs = jnp.dot(rows, sm[...], preferred_element_type=F32)
-
-        def ups(v, h):
-            return jnp.where(row == ny - 1, h, pltpu.roll(v, ny - 1, 0))
-
-        def downs(v, l):
-            return jnp.where(row == 0, l, pltpu.roll(v, 1, 0))
-
-        g = gain(center(4))
-        gb, ga = g + gain(before(4)), g + gain(after(4))
-        gu, gd = g + ups(g, gain(high(4))), g + downs(g, gain(low(4)))
-        gz = g + pltpu.roll(g, nz - 1, 1)
-        gzl = pltpu.roll(gz, 1, 1)
-        m, a = masks(solid)
+    sub = lax.broadcasted_iota(jnp.int32, (8, nz), 0)
+    every = range(parts)
+
+    def held(ref, *at):
+        return lambda f, k: ref[(*at, f, pl.ds(k, 8, stride=parts))]
+
+    def q_layer(x):
+        return lambda f, k: q_ref[f, pl.ds(x * ny + k, 8, stride=parts)]
+
+    def q_plane(y):
+        return lambda f, k: q_ref[f, pl.ds(k * ny + y, 8, stride=parts * ny)]
+
+    def s_layer(x):
+        return lambda k: s_ref[pl.ds(x * ny + k, 8, stride=parts)] >= level
+
+    def s_plane(y):
+        return lambda k: s_ref[pl.ds(k * ny + y, 8, stride=parts * ny)] >= level
+
+    def s_halo(n):
+        edge = level.astype(F32)
+        return lambda k: ms[n, pl.ds(k, 8, stride=parts)] >= edge
+
+    def gains(src):
+        return [gain(src(4, k)) for k in every]
+
+    def line(src, r):
+        return lambda f: src(f, r % parts)[r // parts : r // parts + 1]
+
+    def corner(n):
+        return lambda f: cor[n, f : f + 1]
+
+    def got_line(ref, n, r):
+        return lambda f: ref[n, f, r : r + 1]
+
+    def put(ref, n, vals):
+        for f in range(nf):
+            for k in every:
+                ref[n, f, pl.ds(k, 8, stride=parts)] = vals[f][k]
+
+    def products(centers):
+        gs = []
+        for n, src in enumerate(centers):
+            gs.append(gains(src))
+            tall = [src(f, k) for f in range(nf) for k in every] + gs[-1]
+            zin[pl.ds(n * (nf + 1) * ny, (nf + 1) * ny)] = jnp.concatenate(tall, 0).astype(BF)
+        zout[...] = jnp.dot(zin[...], sm[...], preferred_element_type=F32)
+        return gs
+
+    def slab(n, g, center, before, after, low, high, solid, along_outer):
+        def z(f, k, h):
+            return zout[(n * (nf + 1) + f) * ny + 8 * k : (n * (nf + 1) + f) * ny + 8 * k + 8, h * nz : (h + 1) * nz]
+
+        def ups(v, edge):
+            return v[1:] + [jnp.where(sub == 7, edge, pltpu.roll(v[0], 7, 0))]
+
+        def downs(v, edge):
+            return [jnp.where(sub == 0, edge, pltpu.roll(v[-1], 1, 0))] + v[:-1]
+
+        gb, ga = gains(before), gains(after)
+        gu, gd = ups(g, gain(high(4))), downs(g, gain(low(4)))
+        ga, gb, gu, gd = ([x + y for x, y in zip(g, v)] for v in (ga, gb, gu, gd))
+        gz = [2.0 * g[k] + z(nf, k, 0) for k in every]
+        gzl = [2.0 * g[k] - z(nf, k, 1) for k in every]
+        ma = [masks(solid(k)) for k in every]
         res = []
         for f in range(nf):
-            q = center(f)
-            qa, qb = after(f), before(f)
+            q = [center(f, k) for k in every]
             qu, qd = ups(q, high(f)), downs(q, low(f))
-            z = diffs[f * ny : (f + 1) * ny]
-            total = ga * (qa - q) - gb * (q - qb) + (gu * (qu - q) - gd * (q - qd))
-            total += gz * z[:, :nz] - gzl * z[:, nz:]
-            grad = qa - qb if along_outer else qu - qd
-            res.append(q + (d[f] * (m * total) - c[f] * (a * grad)))
+            vals = []
+            for k in every:
+                da, db, du, dd = after(f, k) - q[k], q[k] - before(f, k), qu[k] - q[k], q[k] - qd[k]
+                total = ga[k] * da - gb[k] * db + (gu[k] * du - gd[k] * dd)
+                total += gz[k] * z(f, k, 0) - gzl[k] * z(f, k, 1)
+                grad = da + db if along_outer else du + dd
+                vals.append(q[k] + (d[f] * (ma[k][0] * total) - c[f] * (ma[k][1] * grad)))
+            res.append(vals)
         return res
 
-    def q_layer(x):
-        return lambda f: q_ref[f, x * ny : (x + 1) * ny]
-
-    def q_plane(y):
-        return lambda f: q_ref[f, pl.ds(y, nx, stride=ny)]
-
-    def halo(k):
-        return lambda f: lay[k, f]
-
-    def corner(k):
-        return lambda f: cor[k, f : f + 1]
-
-    plane = {-2: 2 * nf + 1, -1: 3 * nf + 1, ny: 0, ny + 1: nf}
-
-    def c_plane(y):
-        return lambda f: c1_ref[plane[y] + f].astype(F32)
-
-    def line(src, k):
-        return lambda f: src(f)[k : k + 1]
-
-    s_lay = lambda x: s_ref[x * ny : (x + 1) * ny] >= level
-    s_pla = lambda y: s_ref[pl.ds(y, nx, stride=ny)] >= level
-    level_f = level.astype(F32)
-    m_low = jnp.where(even, b_ref[2 * nf], a_ref[2 * nf]).astype(F32) >= level_f
-    m_high = jnp.where(even, a_ref[2 * nf], b_ref[2 * nf]).astype(F32) >= level_f
-
-    def put(dst, k, vals):
+    def passed(here, there, solid, along_x, ahead):
+        g = [x + y for x, y in zip(gains(here), gains(there))]
+        ma = [masks(solid(k)) for k in every]
+        res = []
         for f in range(nf):
-            dst[k, f] = vals[f]
-
-    put(fl, 0, slab(halo(LN), halo(LF), q_layer(0), corner(0), corner(1), m_low, True))
+            vals = []
+            for k in every:
+                diff = there(f, k) - here(f, k)
+                add = d[f] * (ma[k][0] * (g[k] * diff))
+                if along_x:
+                    half = c[f] * (ma[k][1] * diff)
+                    add = add - half if ahead else add + half
+                vals.append(add)
+            res.append(vals)
+        return res
+
+    g = products([held(lay, LO), held(lay, HI), held(pla, LO), held(pla, HI)])
+    put(fl, 0, slab(0, g[0], held(lay, LO), held(lay, FAR_LO), q_layer(0), corner(0), corner(1), s_halo(0), True))
+    put(fl, 5, slab(1, g[1], held(lay, HI), q_layer(nx - 1), held(lay, FAR_HI), corner(2), corner(3), s_halo(1), True))
+    put(fp, 0, slab(2, g[2], held(pla, LO), held(pla, FAR_LO), q_plane(0), corner(0), corner(2), s_halo(2), False))
+    put(fp, 5, slab(3, g[3], held(pla, HI), q_plane(ny - 1), held(pla, FAR_HI), corner(1), corner(3), s_halo(3), False))
 
     @pl.when(stream == 0)
     def _():
-        for f in range(nf):
-            fl[0, f] = lay[LN, f]
-
-    def y_line(y, x):
-        return lambda f: c1_ref[plane[y] + f, pl.ds(x // 16 * 16, 16)].astype(F32)[x % 16 : x % 16 + 1]
-
-    put(fl, 1, slab(q_layer(0), halo(LN), q_layer(1), y_line(-1, 0), y_line(ny, 0), s_lay(0), True))
-    put(fl, 6, slab(q_layer(nx - 1), q_layer(nx - 2), halo(HN), y_line(-1, nx - 1), y_line(ny, nx - 1),
-                    s_lay(nx - 1), True))
-    put(fl, 7, slab(halo(HN), q_layer(nx - 1), halo(HF), corner(2), corner(3), m_high, True))
+        fl[0] = lay[LO]
 
     @pl.when(stream == last)
     def _():
+        fl[5] = jnp.zeros(fl.shape[1:], F32)
+
+    put(cx, 0, passed(q_layer(0), held(lay, LO), s_layer(0), True, False))
+    put(cx, 1, passed(q_layer(nx - 1), held(lay, HI), s_layer(nx - 1), True, True))
+    put(cy, 0, passed(q_plane(0), held(pla, LO), s_plane(0), False, False))
+    put(cy, 1, passed(q_plane(ny - 1), held(pla, HI), s_plane(ny - 1), False, True))
+    for f in range(nf):
+        for n, x in ((1, 0), (2, 1), (3, nx - 2), (4, nx - 1)):
+            v = first_ref[f, x * ny : (x + 1) * ny]
+            fl[n, f] = v + cx[n // 4, f] if n in (1, 4) else v
+            fl[n, f, 0:1] += cy[0, f, x : x + 1]
+            fl[n, f, ny - 1 : ny] += cy[1, f, x : x + 1]
+        for n, y in ((1, 0), (2, 1), (3, ny - 2), (4, ny - 1)):
+            v = first_ref[f, pl.ds(y, nx, stride=ny)]
+            fp[n, f] = v + cy[n // 4, f] if n in (1, 4) else v
+            fp[n, f, 0:1] += cx[0, f, y : y + 1]
+            fp[n, f, nx - 1 : nx] += cx[1, f, y : y + 1]
+
+    g = products([held(fl, 1), held(fl, 4), held(fp, 1), held(fp, 4)])
+
+    def ended(src, vals):
+        return [[0.5 * (src(f, k) + vals[f][k]) for k in every] for f in range(nf)]
+
+    copies = []
+    for n, (m, x) in enumerate(((1, 0), (4, nx - 1))):
+        vals = slab(n, g[n], held(fl, m), held(fl, m - 1), held(fl, m + 1), got_line(fp, 0, x), got_line(fp, 5, x),
+                    s_layer(x), True)
+        put(ol, 3 * n, ended(q_layer(x), vals))
+        copies.append(pltpu.make_async_copy(ol.at[3 * n], out_ref.at[:, x], sem.at[2, 3 * n]))
+        copies[-1].start()
+    for n, (m, y) in enumerate(((1, 0), (4, ny - 1))):
+        vals = slab(2 + n, g[2 + n], held(fp, m), held(fp, m - 1), held(fp, m + 1), got_line(fl, 0, y),
+                    got_line(fl, 5, y), s_plane(y), False)
+        put(cy, n, ended(q_plane(y), vals))
+    put(fp, 0, passed(held(fp, 2), held(fp, 1), s_plane(1), False, False))
+    put(fp, 5, passed(held(fp, 3), held(fp, 4), s_plane(ny - 2), False, True))
+    put(cx, 0, passed(held(fl, 2), held(fl, 1), s_layer(1), True, False))
+    put(cx, 1, passed(held(fl, 3), held(fl, 4), s_layer(nx - 2), True, True))
+    for n, x in ((0, 1), (1, nx - 2)):
         for f in range(nf):
-            fl[7, f] = jnp.zeros((ny, nz), F32)
-
-    put(fp, 0, slab(c_plane(-1), c_plane(-2), q_plane(0), corner(0), corner(2),
-                    c1_ref[4 * nf + 1].astype(F32) >= level_f, False))
-    put(fp, 1, slab(q_plane(0), c_plane(-1), q_plane(1), line(halo(LN), 0), line(halo(HN), 0), s_pla(0), False))
-    put(fp, 6, slab(q_plane(ny - 1), q_plane(ny - 2), c_plane(ny), line(halo(LN), ny - 1),
-                    line(halo(HN), ny - 1), s_pla(ny - 1), False))
-    put(fp, 7, slab(c_plane(ny), q_plane(ny - 1), c_plane(ny + 1), corner(1), corner(3),
-                    c1_ref[2 * nf].astype(F32) >= level_f, False))
-
-    for f in range(nf):
-        for k, x in ((2, 1), (3, 2), (4, nx - 3), (5, nx - 2)):
-            fl[k, f] = first_ref[f, x * ny : (x + 1) * ny]
-            fl[k, f, 0:1] = fp[1, f, x : x + 1]
-            fl[k, f, ny - 1 : ny] = fp[6, f, x : x + 1]
-        for k, y in ((2, 1), (3, 2), (4, ny - 3), (5, ny - 2)):
-            fp[k, f] = first_ref[f, pl.ds(y, nx, stride=ny)]
-            fp[k, f, 0:1] = fl[1, f, y : y + 1]
-            fp[k, f, nx - 1 : nx] = fl[6, f, y : y + 1]
-
-    def got(src, k):
-        return lambda f: src[k, f]
-
-    def got_line(src, k, r):
-        return lambda f: src[k, f, r : r + 1]
-
-    layers = []
-    for k, (n, x) in enumerate(((1, 0), (2, 1), (5, nx - 2), (6, nx - 1))):
-        vals = slab(got(fl, n), got(fl, n - 1), got(fl, n + 1), got_line(fp, 0, x), got_line(fp, 7, x), s_lay(x), True)
+            k = n + 1
+            ol[k, f] = main_ref[f, x] + 0.5 * cx[n, f]
+            ol[k, f, 0:1] = cy[0, f, x : x + 1]
+            ol[k, f, 1:2] += 0.5 * fp[0, f, x : x + 1]
+            ol[k, f, ny - 2 : ny - 1] += 0.5 * fp[5, f, x : x + 1]
+            ol[k, f, ny - 1 : ny] = cy[1, f, x : x + 1]
+        copies.append(pltpu.make_async_copy(ol.at[n + 1], out_ref.at[:, x], sem.at[2, n + 1]))
+        copies[-1].start()
+    for n, (end, near) in enumerate(((0, 1), (7, 6))):
+        cuts[n].wait()
         for f in range(nf):
-            ol[k, f] = 0.5 * (q_layer(x)(f) + vals[f])
-        layers.append(pltpu.make_async_copy(ol.at[k], out_ref.at[:, x], sem.at[2, k]))
-        layers[-1].start()
-    for copy in cuts:
-        copy.wait()
-    edges = []
-    for k, (n, y, side, r) in enumerate(((1, 0, 0, 0), (2, 1, 0, 1), (5, ny - 2, 1, 6), (6, ny - 1, 1, 7))):
-        vals = slab(got(fp, n), got(fp, n - 1), got(fp, n + 1), got_line(fl, 0, y), got_line(fl, 7, y), s_pla(y), False)
-        for f in range(nf):
-            strips[side, f, :, r] = 0.5 * (q_plane(y)(f) + vals[f])
-        if k % 2:
-            edges.append(pltpu.make_async_copy(
-                strips.at[side, :, pl.ds(2, nx - 4)],
-                out_ref.at[:, pl.ds(2, nx - 4), pl.ds(side * (ny - 8), 8)], sem.at[3, side]))
-            edges[-1].start()
-    for copy in mids + layers + edges:
+            strips[n, f, :, end] = cy[n, f]
+            strips[n, f, :, near] += 0.5 * fp[5 * n, f]
+        copies.append(pltpu.make_async_copy(
+            strips.at[n, :, pl.ds(2, nx - 4)],
+            out_ref.at[:, pl.ds(2, nx - 4), pl.ds(n * (ny - 8), 8)], sem.at[3, n]))
+        copies[-1].start()
+    for copy in mids + copies:
         copy.wait()
 
 
@@ -462,8 +518,10 @@
         in_specs=[SM, SM, VM] + [VM] * (9 + len(more)),
         out_specs=HB,
         scratch_shapes=[
-            mb((nz, 2 * nz), BF), mb((4, nf, ny, nz), F32), mb((4, 8, nz), F32), mb((8, nf, ny, nz), F32),
-            mb((8, nf, nx, nz), F32), mb((4, nf, ny, nz), F32), mb((2, nf, nx, 8, nz), F32),
+            mb((nz, 2 * nz), BF), mb((4, nf, ny, nz), F32), mb((4, nf, nx, nz), F32), mb((4, ny, nz), F32),
+            mb((4, 8, nz), F32), mb((6, nf, ny, nz), F32), mb((6, nf, nx, nz), F32), mb((2, nf, ny, nz), F32),
+            mb((2, nf, nx, nz), F32), mb((4, nf, ny, nz), F32), mb((2, nf, nx, 8, nz), F32),
+            mb((4 * (nf + 1) * ny, nz), BF), mb((4 * (nf + 1) * ny, 2 * nz), F32),
             pltpu.SemaphoreType.DMA((4, 8)),
         ],
         compiler_params=pltpu.CompilerParams(vmem_limit_bytes=10 << 20),

time: 26 us -> 24.8 us (0.954)
  Pallas kernels: 15.4 us -> 14.2 us
    pallas_call x1, Pallas kernels: 6.34 us -> 5.41 us  [body(): pl.pallas_call(functools.partial(border_kernel, dims, two), out_shape=jax...]
    pallas_call x2, Pallas kernels: 8.69 us -> 8.38 us  [section(): pl.pallas_call(functools.partial(section_kernel, dims, second), out_shape...]
where the time goes in v4:
time: 24.8 us; the launch traced here: 24.6 us
  Pallas kernels  14.2 us (57%)
  starting transfers between devices  7.16 us (29%)
  local copies, waits for them, and re-layouts  3.12 us (13%)
    pallas_call x2, Pallas kernels, section(): pl.pallas_call(functools.partial(section_kernel, dims, second), out_shape...  8.38 us
    pallas_call x1, Pallas kernels, body(): pl.pallas_call(functools.partial(border_kernel, dims, two), out_shape=jax...  5.41 us
    ppermute x1, starting transfers between devices, body(): b = lax.ppermute(send_b, ('comp', 'gx'), both(outer + [(0, ngx)]))  3.55 us
    unnamed x14, local copies, waits for them, and re-layouts  3.12 us
    ppermute x1, starting transfers between devices, body(): c1 = lax.ppermute(send_c, 'gy', swap)  3 us
    ppermute x1, starting transfers between devices, body(): c2 = lax.ppermute(extra, 'gy', swap)  0.61 us
  transfers between devices with their start and end apart: 4, of which 0 were waited for; matrix products, arithmetic and copies ran while one was open for 0% of the time, Pallas kernels for 34%

profile of v4, /device:TPU:0, one launch (start us, length us, event | category | flops | bytes accessed | tf_op | source)
XLA Modules:
  0.0 24.6 jit_solution(9818118439888522313)
XLA Ops:
  0.0 0.0 copy-start.5
  0.0 0.0 copy-start.4
  0.0 0.0 copy-start
  0.0 2.1 %copy-done = f32[1,7,32,32,128]{4,3,2,1,0:T(8,128)S(1)} copy-done((f32[1,7,32,32,128]{4,3,2,1,0:T(8,128)S(1)}, f32[1,7,32,32,128]{4,3,2,1,0:T(8,128)}, u32[]{:S(2)}) %copy-start) | copy-done | bytes 3670040
  2.1 0.0 copy-start.2
  2.1 1.0 %copy-done.2 = s32[32,32,128]{2,1,0:T(8,128)S(1)} copy-done((s32[32,32,128]{2,1,0:T(8,128)S(1)}, s32[32,32,128]{2,1,0:T(8,128)}, u32[]{:S(2)}) %copy-start.2) | copy-done | bytes 524312
  3.1 0.0 copy-start.1
  3.1 0.3 %shard_map.57 = (bf16[15,32,128]{2,1,0:T(8,128)(2,1)S(1)}, bf16[15,32,128]{2,1,0:T(8,128)(2,1)S(1)}, bf16[30,32,128]{2,1,0:T(8,128)(2,1)S(1)}) custom-call(f32[7,1024,128]{2,1,0:T(8,128)S(1)} %bitcast.5, s32[1024,128]{1,0:T(8,128)S(1)} %bitcast.10), custom_call_target="tpu_custom_call" | custom-call | tf_op jit(solution)/shard_map/pallas_call | solution.py:456
  3.4 3.0 %collective-permute-start.2 = (bf16[30,32,128]{2,1,0:T(8,128)(2,1)S(1)}, bf16[30,32,128]{2,1,0:T(8,128)(2,1)S(1)}, u32[]{:S(2)}, u32[]{:S(2)}) collective-permute-start(bf16[30,32,128]{2,1,0:T(8,128)(2,1)S(1)} %get-tuple-element.10), channel_id=1, source_target_pairs={{0,1},{1,0},{2,3},{3,2},{4,5},{5,4},{6,7},{7,6},{8,9},{9,8},{10,11... | collective-permute-start | bytes 737288 | tf_op jit(solution)/shard_map/ppermute | solution.py:466
  6.4 0.0 collective-permute-start
  6.4 0.0 copy-start.6
  6.4 3.5 %collective-permute-start.1 = (bf16[15,32,128]{2,1,0:T(8,128)(2,1)S(1)}, bf16[15,32,128]{2,1,0:T(8,128)(2,1)S(1)}, u32[]{:S(2)}, u32[]{:S(2)}) collective-permute-start(bf16[15,32,128]{2,1,0:T(8,128)(2,1)S(1)} %get-tuple-element.9), channel_id=1, source_target_pairs={{2,4},{6,8},{10,12},{18,20},{22,24},{26,28},{0,16},{4,2},{8,6},{12... | collective-permute-start | bytes 368648 | tf_op jit(solution)/shard_map/ppermute | solution.py:479
  10.0 0.0 copy-done.5
  10.0 0.0 copy-done.4
  10.0 0.0 copy-done.1
  10.0 4.0 %shard_map.55.refs_3_.after_ref.refs_4_ = f32[7,1024,128]{2,1,0:T(8,128)S(1)} custom-call(f32[2,7]{1,0:T(2,128)S(1)} %copy-done.4, f32[2,7]{1,0:T(2,128)S(1)} %copy-done.5, f32[7,1024,128]{2,1,0:T(8,128)S(1)} %bitcast.6, s32[1024,128]{1,0:T(8,128)S(1)} %bitcast.11), custom_call_target="tpu_custom_call" | custom-call | flops 18350080 | bytes 7340032 | tf_op jit(solution)/shard_map/pallas_call | solution.py:485
  14.0 0.0 collective-permute-done.a_ref.refs_7_
  14.1 0.0 collective-permute-done.1.b_ref.refs_8_
  14.1 0.0 copy-done.6
  14.1 0.1 shard_map.58
  14.1 0.0 copy-start.3
  14.1 0.6 %collective-permute-start.3 = (bf16[7,48,128]{2,1,0:T(8,128)(2,1)S(1)}, bf16[7,48,128]{2,1,0:T(8,128)(2,1)S(1)}, u32[]{:S(2)}, u32[]{:S(2)}) collective-permute-start(bf16[7,48,128]{2,1,0:T(8,128)(2,1)S(1)} %shard_map.58), channel_id=1, source_target_pairs={{0,1},{1,0},{2,3},{3,2},{4,5},{5,4},{6,7},{7,6},{8,9},{9,8},{10,11... | collective-permute-start | bytes 258056 | tf_op jit(solution)/shard_map/ppermute | solution.py:506
  14.7 4.4 %shard_map.56 = f32[7,1024,128]{2,1,0:T(8,128)S(1)} custom-call(f32[2,7]{1,0:T(2,128)S(1)} %copy-done.4, f32[2,7]{1,0:T(2,128)S(1)} %copy-done.5, f32[7,1024,128]{2,1,0:T(8,128)S(1)} %bitcast.7, f32[7,1024,128]{2,1,0:T(8,128)S(1)} %shard_map.55.refs_3_.after_ref.refs_4_, s32[1024,128]{1,0:T(8,128)S(1)} %bitcast.12), custom_call_target="tpu_custom_call" | custom-call | flops 18350080 | bytes 7340032 | tf_op jit(solution)/shard_map/pallas_call | solution.py:485
  19.1 0.0 collective-permute-done.3.refs_10_.refs_11_
  19.1 0.0 collective-permute-done.2.refs_9_
  19.1 0.0 copy-done.3
  19.2 5.4 %shard_map.59 = f32[7,32,32,128]{3,2,1,0:T(8,128)} custom-call(f32[2,7]{1,0:T(2,128)S(1)} %copy-done.4, f32[2,7]{1,0:T(2,128)S(1)} %copy-done.5, s32[1,32]{1,0:T(1,128)S(1)} %bitcast.15, f32[7,1024,128]{2,1,0:T(8,128)S(1)} %bitcast.8, f32[7,1024,128]{2,1,0:T(8,128)S(1)} %shard_map.55.refs_3_.after_ref.refs_4_, f32[7,32,32,128]{3,2,1,0:T(8,128)S(1)} %bitcast.9, ...), custom_call_target="tpu_custom_call" | custom-call | flops 9175040 | bytes 7340032 | tf_op jit(solution)/shard_map/pallas_call | solution.py:515
Async XLA Ops:
  0.0 10.0 %copy-start.5 = (f32[2,7]{1,0:T(2,128)S(1)}, f32[2,7]{1,0:T(2,128)}, u32[]{:S(2)}) copy-start(f32[2,7]{1,0:T(2,128)} %refs_1_.5) | copy-start | bytes 172
  0.0 10.0 %copy-start.4 = (f32[2,7]{1,0:T(2,128)S(1)}, f32[2,7]{1,0:T(2,128)}, u32[]{:S(2)}) copy-start(f32[2,7]{1,0:T(2,128)} %refs_0_.5) | copy-start | bytes 172
  0.0 2.1 %copy-start = (f32[1,7,32,32,128]{4,3,2,1,0:T(8,128)S(1)}, f32[1,7,32,32,128]{4,3,2,1,0:T(8,128)}, u32[]{:S(2)}) copy-start(f32[1,7,32,32,128]{4,3,2,1,0:T(8,128)} %param.5) | copy-start | bytes 11010052
  2.1 1.0 %copy-start.2 = (s32[32,32,128]{2,1,0:T(8,128)S(1)}, s32[32,32,128]{2,1,0:T(8,128)}, u32[]{:S(2)}) copy-start(s32[32,32,128]{2,1,0:T(8,128)} %param.8) | copy-start | bytes 1572868
  3.1 6.9 %copy-start.1 = (f32[1,7,32,32,128]{4,3,2,1,0:T(8,128)S(1)}, f32[1,7,32,32,128]{4,3,2,1,0:T(8,128)}, u32[]{:S(2)}) copy-start(f32[1,7,32,32,128]{4,3,2,1,0:T(8,128)} %param.5) | copy-start | bytes 11010052
  3.4 15.7 %collective-permute-start.2 = (bf16[30,32,128]{2,1,0:T(8,128)(2,1)S(1)}, bf16[30,32,128]{2,1,0:T(8,128)(2,1)S(1)}, u32[]{:S(2)}, u32[]{:S(2)}) collective-permute-start(bf16[30,32,128]{2,1,0:T(8,128)(2,1)S(1)} %get-tuple-element.10), channel_id=1, source_target_pairs={{0,1},{1,0},{2,3},{3,2},{4,5},{5,4},{6,7},{7,6},{8,9},{9,8},{10,11... | collective-permute-start | bytes 737288 | tf_op jit(solution)/shard_map/ppermute | solution.py:466
  6.4 7.6 %collective-permute-start = (bf16[15,32,128]{2,1,0:T(8,128)(2,1)S(1)}, bf16[15,32,128]{2,1,0:T(8,128)(2,1)S(1)}, u32[]{:S(2)}, u32[]{:S(2)}) collective-permute-start(bf16[15,32,128]{2,1,0:T(8,128)(2,1)S(1)} %get-tuple-element.8), channel_id=1, source_target_pairs={{0,2},{4,6},{8,10},{12,14},{2,0},{6,4},{10,8},{14,12},{1,3},{5,7},... | collective-permute-start | bytes 368648 | tf_op jit(solution)/shard_map/ppermute | solution.py:477
  6.4 7.6 %copy-start.6 = (s32[32]{0:T(128)S(1)}, s32[32]{0:T(128)}, u32[]{:S(2)}) copy-start(s32[32]{0:T(128)} %param.9) | copy-start | bytes 388
  6.4 7.6 %collective-permute-start.1 = (bf16[15,32,128]{2,1,0:T(8,128)(2,1)S(1)}, bf16[15,32,128]{2,1,0:T(8,128)(2,1)S(1)}, u32[]{:S(2)}, u32[]{:S(2)}) collective-permute-start(bf16[15,32,128]{2,1,0:T(8,128)(2,1)S(1)} %get-tuple-element.9), channel_id=1, source_target_pairs={{2,4},{6,8},{10,12},{18,20},{22,24},{26,28},{0,16},{4,2},{8,6},{12... | collective-permute-start | bytes 368648 | tf_op jit(solution)/shard_map/ppermute | solution.py:479
  14.1 5.0 %copy-start.3 = (s32[32,32,128]{2,1,0:T(8,128)S(1)}, s32[32,32,128]{2,1,0:T(8,128)}, u32[]{:S(2)}) copy-start(s32[32,32,128]{2,1,0:T(8,128)} %param.8) | copy-start | bytes 1572868
  14.1 5.0 %collective-permute-start.3 = (bf16[7,48,128]{2,1,0:T(8,128)(2,1)S(1)}, bf16[7,48,128]{2,1,0:T(8,128)(2,1)S(1)}, u32[]{:S(2)}, u32[]{:S(2)}) collective-permute-start(bf16[7,48,128]{2,1,0:T(8,128)(2,1)S(1)} %shard_map.58), channel_id=1, source_target_pairs={{0,1},{1,0},{2,3},{3,2},{4,5},{5,4},{6,7},{7,6},{8,9},{9,8},{10,11... | collective-permute-start | bytes 258056 | tf_op jit(solution)/shard_map/ppermute | solution.py:506

commit v5 on v4

--- a/solution.py
+++ b/solution.py
@@ -194,7 +194,7 @@
         (dif, adv, imap, q_ref, first_ref, main_ref, s_ref, a_ref, b_ref, c1_ref, c2l_ref, c2h_ref,
          face_ref, map_ref) = refs[:14]
         rest = refs[14:]
-    out_ref, sm, lay, pla, ms, cor, fl, fp, cx, cy, ol, strips, zin, zout, sem = rest
+    out_ref, sm, lay, pla, qp, ms, cor, fl, fp, cx, cy, ep, ol, strips, zin, zout, sem = rest
     d, c, level = scalars(dif, adv, nf)
     comp = lax.axis_index("comp")
     stream, last = lax.axis_index("gx"), lax.axis_size("gx") - 1
@@ -224,6 +224,8 @@
         lay[FAR_HI, f] = jnp.where(even, av[1], bv[1]) * inside
         for n, k in enumerate((2 * nf + 1, 3 * nf + 1, 0, nf)):
             pla[n, f] = c1_ref[k + f].astype(F32)
+        for n, y in enumerate((0, ny - 1)):
+            qp[n, f] = q_ref[f, pl.ds(y, nx, stride=ny)]
         lo, hi = c2l_ref[f, pl.ds(ny, 16)].astype(F32), c2h_ref[f, pl.ds(ny, 16)].astype(F32)
         lo_b, hi_b = c2l_ref[f, pl.ds(ny - 16, 16)].astype(F32), c2h_ref[f, pl.ds(0, 16)].astype(F32)
         cor[0, f : f + 1] = jnp.where(even, lo[5:6], lo[3:4])
@@ -283,7 +285,7 @@
         return lambda f, k: q_ref[f, pl.ds(x * ny + k, 8, stride=parts)]
 
     def q_plane(y):
-        return lambda f, k: q_ref[f, pl.ds(k * ny + y, 8, stride=parts * ny)]
+        return held(qp, 0 if y == 0 else 1)
 
     def s_layer(x):
         return lambda k: s_ref[pl.ds(x * ny + k, 8, stride=parts)] >= level
@@ -403,38 +405,36 @@
         return [[0.5 * (src(f, k) + vals[f][k]) for k in every] for f in range(nf)]
 
     copies = []
-    for n, (m, x) in enumerate(((1, 0), (4, nx - 1))):
+    put(ep, 0, passed(held(fp, 2), held(fp, 1), s_plane(1), False, False))
+    put(ep, 1, passed(held(fp, 3), held(fp, 4), s_plane(ny - 2), False, True))
+    for n, (m, y, end, near) in enumerate(((1, 0, 0, 1), (4, ny - 1, 7, 6))):
+        vals = slab(2 + n, g[2 + n], held(fp, m), held(fp, m - 1), held(fp, m + 1), got_line(fl, 0, y),
+                    got_line(fl, 5, y), s_plane(y), False)
+        put(cy, n, ended(q_plane(y), vals))
+        cuts[n].wait()
+        for f in range(nf):
+            strips[n, f, :, end] = cy[n, f]
+            strips[n, f, :, near] += 0.5 * ep[n, f]
+        copies.append(pltpu.make_async_copy(
+            strips.at[n, :, pl.ds(2, nx - 4)],
+            out_ref.at[:, pl.ds(2, nx - 4), pl.ds(n * (ny - 8), 8)], sem.at[3, n]))
+        copies[-1].start()
+    put(cx, 0, passed(held(fl, 2), held(fl, 1), s_layer(1), True, False))
+    put(cx, 1, passed(held(fl, 3), held(fl, 4), s_layer(nx - 2), True, True))
+    for n, (m, x, near) in enumerate(((1, 0, 1), (4, nx - 1, nx - 2))):
+        for f in range(nf):
+            k = n + 1
+            ol[k, f] = main_ref[f, near] + 0.5 * cx[n, f]
+            ol[k, f, 0:1] = cy[0, f, near : near + 1]
+            ol[k, f, 1:2] += 0.5 * ep[0, f, near : near + 1]
+            ol[k, f, ny - 2 : ny - 1] += 0.5 * ep[1, f, near : near + 1]
+            ol[k, f, ny - 1 : ny] = cy[1, f, near : near + 1]
+        copies.append(pltpu.make_async_copy(ol.at[k], out_ref.at[:, near], sem.at[2, k]))
+        copies[-1].start()
         vals = slab(n, g[n], held(fl, m), held(fl, m - 1), held(fl, m + 1), got_line(fp, 0, x), got_line(fp, 5, x),
                     s_layer(x), True)
         put(ol, 3 * n, ended(q_layer(x), vals))
         copies.append(pltpu.make_async_copy(ol.at[3 * n], out_ref.at[:, x], sem.at[2, 3 * n]))
-        copies[-1].start()
-    for n, (m, y) in enumerate(((1, 0), (4, ny - 1))):
-        vals = slab(2 + n, g[2 + n], held(fp, m), held(fp, m - 1), held(fp, m + 1), got_line(fl, 0, y),
-                    got_line(fl, 5, y), s_plane(y), False)
-        put(cy, n, ended(q_plane(y), vals))
-    put(fp, 0, passed(held(fp, 2), held(fp, 1), s_plane(1), False, False))
-    put(fp, 5, passed(held(fp, 3), held(fp, 4), s_plane(ny - 2), False, True))
-    put(cx, 0, passed(held(fl, 2), held(fl, 1), s_layer(1), True, False))
-    put(cx, 1, passed(held(fl, 3), held(fl, 4), s_layer(nx - 2), True, True))
-    for n, x in ((0, 1), (1, nx - 2)):
-        for f in range(nf):
-            k = n + 1
-            ol[k, f] = main_ref[f, x] + 0.5 * cx[n, f]
-            ol[k, f, 0:1] = cy[0, f, x : x + 1]
-            ol[k, f, 1:2] += 0.5 * fp[0, f, x : x + 1]
-            ol[k, f, ny - 2 : ny - 1] += 0.5 * fp[5, f, x : x + 1]
-            ol[k, f, ny - 1 : ny] = cy[1, f, x : x + 1]
-        copies.append(pltpu.make_async_copy(ol.at[n + 1], out_ref.at[:, x], sem.at[2, n + 1]))
-        copies[-1].start()
-    for n, (end, near) in enumerate(((0, 1), (7, 6))):
-        cuts[n].wait()
-        for f in range(nf):
-            strips[n, f, :, end] = cy[n, f]
-            strips[n, f, :, near] += 0.5 * fp[5 * n, f]
-        copies.append(pltpu.make_async_copy(
-            strips.at[n, :, pl.ds(2, nx - 4)],
-            out_ref.at[:, pl.ds(2, nx - 4), pl.ds(n * (ny - 8), 8)], sem.at[3, n]))
         copies[-1].start()
     for copy in mids + copies:
         copy.wait()
@@ -518,9 +518,9 @@
         in_specs=[SM, SM, VM] + [VM] * (9 + len(more)),
         out_specs=HB,
         scratch_shapes=[
-            mb((nz, 2 * nz), BF), mb((4, nf, ny, nz), F32), mb((4, nf, nx, nz), F32), mb((4, ny, nz), F32),
+            mb((nz, 2 * nz), BF), mb((4, nf, ny, nz), F32), mb((4, nf, nx, nz), F32), mb((2, nf, nx, nz), F32), mb((4, ny, nz), F32),
             mb((4, 8, nz), F32), mb((6, nf, ny, nz), F32), mb((6, nf, nx, nz), F32), mb((2, nf, ny, nz), F32),
-            mb((2, nf, nx, nz), F32), mb((4, nf, ny, nz), F32), mb((2, nf, nx, 8, nz), F32),
+            mb((2, nf, nx, nz), F32), mb((2, nf, nx, nz), F32), mb((4, nf, ny, nz), F32), mb((2, nf, nx, 8, nz), F32),
             mb((4 * (nf + 1) * ny, nz), BF), mb((4 * (nf + 1) * ny, 2 * nz), F32),
             pltpu.SemaphoreType.DMA((4, 8)),
         ],

time: 24.8 us -> 24.1 us (0.972)
  Pallas kernels: 14.2 us -> 13.5 us
    pallas_call x1, Pallas kernels: 5.41 us -> 4.79 us  [body(): pl.pallas_call(functools.partial(border_kernel, dims, two), out_shape=jax...]
  transfers between devices with their start and end apart: 4 -> 4, of which waited for: 0 -> 0; matrix products, arithmetic and copies ran while one was open for 0% -> 0% of each run, Pallas kernels for 34% -> 35%
where the time goes in v5:
time: 24.1 us; the launch traced here: 23.9 us
  Pallas kernels  13.5 us (56%)
  starting transfers between devices  7.16 us (30%)
  local copies, waits for them, and re-layouts  3.12 us (13%)
    pallas_call x2, Pallas kernels, section(): pl.pallas_call(functools.partial(section_kernel, dims, second), out_shape...  8.38 us
    pallas_call x1, Pallas kernels, body(): pl.pallas_call(functools.partial(border_kernel, dims, two), out_shape=jax...  4.79 us
    ppermute x1, starting transfers between devices, body(): b = lax.ppermute(send_b, ('comp', 'gx'), both(outer + [(0, ngx)]))  3.55 us
    unnamed x14, local copies, waits for them, and re-layouts  3.12 us
    ppermute x1, starting transfers between devices, body(): c1 = lax.ppermute(send_c, 'gy', swap)  3 us
    ppermute x1, starting transfers between devices, body(): c2 = lax.ppermute(extra, 'gy', swap)  0.61 us
  transfers between devices with their start and end apart: 4, of which 0 were waited for; matrix products, arithmetic and copies ran while one was open for 0% of the time, Pallas kernels for 35%

profile of v5, /device:TPU:0, one launch (start us, length us, event | category | flops | bytes accessed | tf_op | source)
XLA Modules:
  0.0 23.9 jit_solution(15685481008063935452)
XLA Ops:
  0.0 0.0 copy-start.5
  0.0 0.0 copy-start.4
  0.0 0.0 copy-start
  0.0 2.1 %copy-done = f32[1,7,32,32,128]{4,3,2,1,0:T(8,128)S(1)} copy-done((f32[1,7,32,32,128]{4,3,2,1,0:T(8,128)S(1)}, f32[1,7,32,32,128]{4,3,2,1,0:T(8,128)}, u32[]{:S(2)}) %copy-start) | copy-done | bytes 3670040
  2.1 0.0 copy-start.2
  2.1 1.0 %copy-done.2 = s32[32,32,128]{2,1,0:T(8,128)S(1)} copy-done((s32[32,32,128]{2,1,0:T(8,128)S(1)}, s32[32,32,128]{2,1,0:T(8,128)}, u32[]{:S(2)}) %copy-start.2) | copy-done | bytes 524312
  3.1 0.0 copy-start.1
  3.1 0.3 %shard_map.57 = (bf16[15,32,128]{2,1,0:T(8,128)(2,1)S(1)}, bf16[15,32,128]{2,1,0:T(8,128)(2,1)S(1)}, bf16[30,32,128]{2,1,0:T(8,128)(2,1)S(1)}) custom-call(f32[7,1024,128]{2,1,0:T(8,128)S(1)} %bitcast.5, s32[1024,128]{1,0:T(8,128)S(1)} %bitcast.10), custom_call_target="tpu_custom_call" | custom-call | tf_op jit(solution)/shard_map/pallas_call | solution.py:456
  3.4 3.0 %collective-permute-start.2 = (bf16[30,32,128]{2,1,0:T(8,128)(2,1)S(1)}, bf16[30,32,128]{2,1,0:T(8,128)(2,1)S(1)}, u32[]{:S(2)}, u32[]{:S(2)}) collective-permute-start(bf16[30,32,128]{2,1,0:T(8,128)(2,1)S(1)} %get-tuple-element.10), channel_id=1, source_target_pairs={{0,1},{1,0},{2,3},{3,2},{4,5},{5,4},{6,7},{7,6},{8,9},{9,8},{10,11... | collective-permute-start | bytes 737288 | tf_op jit(solution)/shard_map/ppermute | solution.py:466
  6.4 0.0 collective-permute-start
  6.4 0.0 copy-start.6
  6.4 3.5 %collective-permute-start.1 = (bf16[15,32,128]{2,1,0:T(8,128)(2,1)S(1)}, bf16[15,32,128]{2,1,0:T(8,128)(2,1)S(1)}, u32[]{:S(2)}, u32[]{:S(2)}) collective-permute-start(bf16[15,32,128]{2,1,0:T(8,128)(2,1)S(1)} %get-tuple-element.9), channel_id=1, source_target_pairs={{2,4},{6,8},{10,12},{18,20},{22,24},{26,28},{0,16},{4,2},{8,6},{12... | collective-permute-start | bytes 368648 | tf_op jit(solution)/shard_map/ppermute | solution.py:479
  10.0 0.0 copy-done.5
  10.0 0.0 copy-done.4
  10.0 0.0 copy-done.1
  10.0 4.0 %shard_map.55.refs_3_.after_ref.refs_4_ = f32[7,1024,128]{2,1,0:T(8,128)S(1)} custom-call(f32[2,7]{1,0:T(2,128)S(1)} %copy-done.4, f32[2,7]{1,0:T(2,128)S(1)} %copy-done.5, f32[7,1024,128]{2,1,0:T(8,128)S(1)} %bitcast.6, s32[1024,128]{1,0:T(8,128)S(1)} %bitcast.11), custom_call_target="tpu_custom_call" | custom-call | flops 18350080 | bytes 7340032 | tf_op jit(solution)/shard_map/pallas_call | solution.py:485
  14.0 0.0 collective-permute-done.a_ref.refs_7_
  14.1 0.0 collective-permute-done.1.b_ref.refs_8_
  14.1 0.0 copy-done.6
  14.1 0.1 shard_map.58
  14.1 0.0 copy-start.3
  14.1 0.6 %collective-permute-start.3 = (bf16[7,48,128]{2,1,0:T(8,128)(2,1)S(1)}, bf16[7,48,128]{2,1,0:T(8,128)(2,1)S(1)}, u32[]{:S(2)}, u32[]{:S(2)}) collective-permute-start(bf16[7,48,128]{2,1,0:T(8,128)(2,1)S(1)} %shard_map.58), channel_id=1, source_target_pairs={{0,1},{1,0},{2,3},{3,2},{4,5},{5,4},{6,7},{7,6},{8,9},{9,8},{10,11... | collective-permute-start | bytes 258056 | tf_op jit(solution)/shard_map/ppermute | solution.py:506
  14.7 4.4 %shard_map.56 = f32[7,1024,128]{2,1,0:T(8,128)S(1)} custom-call(f32[2,7]{1,0:T(2,128)S(1)} %copy-done.4, f32[2,7]{1,0:T(2,128)S(1)} %copy-done.5, f32[7,1024,128]{2,1,0:T(8,128)S(1)} %bitcast.7, f32[7,1024,128]{2,1,0:T(8,128)S(1)} %shard_map.55.refs_3_.after_ref.refs_4_, s32[1024,128]{1,0:T(8,128)S(1)} %bitcast.12), custom_call_target="tpu_custom_call" | custom-call | flops 18350080 | bytes 7340032 | tf_op jit(solution)/shard_map/pallas_call | solution.py:485
  19.1 0.0 collective-permute-done.3.refs_10_.refs_11_
  19.1 0.0 collective-permute-done.2.refs_9_
  19.1 0.0 copy-done.3
  19.2 4.8 %shard_map.59 = f32[7,32,32,128]{3,2,1,0:T(8,128)} custom-call(f32[2,7]{1,0:T(2,128)S(1)} %copy-done.4, f32[2,7]{1,0:T(2,128)S(1)} %copy-done.5, s32[1,32]{1,0:T(1,128)S(1)} %bitcast.15, f32[7,1024,128]{2,1,0:T(8,128)S(1)} %bitcast.8, f32[7,1024,128]{2,1,0:T(8,128)S(1)} %shard_map.55.refs_3_.after_ref.refs_4_, f32[7,32,32,128]{3,2,1,0:T(8,128)S(1)} %bitcast.9, ...), custom_call_target="tpu_custom_call" | custom-call | flops 9175040 | bytes 7340032 | tf_op jit(solution)/shard_map/pallas_call | solution.py:515
Async XLA Ops:
  0.0 10.0 %copy-start.5 = (f32[2,7]{1,0:T(2,128)S(1)}, f32[2,7]{1,0:T(2,128)}, u32[]{:S(2)}) copy-start(f32[2,7]{1,0:T(2,128)} %refs_1_.5) | copy-start | bytes 172
  0.0 10.0 %copy-start.4 = (f32[2,7]{1,0:T(2,128)S(1)}, f32[2,7]{1,0:T(2,128)}, u32[]{:S(2)}) copy-start(f32[2,7]{1,0:T(2,128)} %refs_0_.5) | copy-start | bytes 172
  0.0 2.1 %copy-start = (f32[1,7,32,32,128]{4,3,2,1,0:T(8,128)S(1)}, f32[1,7,32,32,128]{4,3,2,1,0:T(8,128)}, u32[]{:S(2)}) copy-start(f32[1,7,32,32,128]{4,3,2,1,0:T(8,128)} %param.5) | copy-start | bytes 11010052
  2.1 1.0 %copy-start.2 = (s32[32,32,128]{2,1,0:T(8,128)S(1)}, s32[32,32,128]{2,1,0:T(8,128)}, u32[]{:S(2)}) copy-start(s32[32,32,128]{2,1,0:T(8,128)} %param.8) | copy-start | bytes 1572868
  3.1 6.9 %copy-start.1 = (f32[1,7,32,32,128]{4,3,2,1,0:T(8,128)S(1)}, f32[1,7,32,32,128]{4,3,2,1,0:T(8,128)}, u32[]{:S(2)}) copy-start(f32[1,7,32,32,128]{4,3,2,1,0:T(8,128)} %param.5) | copy-start | bytes 11010052
  3.4 15.7 %collective-permute-start.2 = (bf16[30,32,128]{2,1,0:T(8,128)(2,1)S(1)}, bf16[30,32,128]{2,1,0:T(8,128)(2,1)S(1)}, u32[]{:S(2)}, u32[]{:S(2)}) collective-permute-start(bf16[30,32,128]{2,1,0:T(8,128)(2,1)S(1)} %get-tuple-element.10), channel_id=1, source_target_pairs={{0,1},{1,0},{2,3},{3,2},{4,5},{5,4},{6,7},{7,6},{8,9},{9,8},{10,11... | collective-permute-start | bytes 737288 | tf_op jit(solution)/shard_map/ppermute | solution.py:466
  6.4 7.6 %collective-permute-start = (bf16[15,32,128]{2,1,0:T(8,128)(2,1)S(1)}, bf16[15,32,128]{2,1,0:T(8,128)(2,1)S(1)}, u32[]{:S(2)}, u32[]{:S(2)}) collective-permute-start(bf16[15,32,128]{2,1,0:T(8,128)(2,1)S(1)} %get-tuple-element.8), channel_id=1, source_target_pairs={{0,2},{4,6},{8,10},{12,14},{2,0},{6,4},{10,8},{14,12},{1,3},{5,7},... | collective-permute-start | bytes 368648 | tf_op jit(solution)/shard_map/ppermute | solution.py:477
  6.4 7.6 %copy-start.6 = (s32[32]{0:T(128)S(1)}, s32[32]{0:T(128)}, u32[]{:S(2)}) copy-start(s32[32]{0:T(128)} %param.9) | copy-start | bytes 388
  6.4 7.6 %collective-permute-start.1 = (bf16[15,32,128]{2,1,0:T(8,128)(2,1)S(1)}, bf16[15,32,128]{2,1,0:T(8,128)(2,1)S(1)}, u32[]{:S(2)}, u32[]{:S(2)}) collective-permute-start(bf16[15,32,128]{2,1,0:T(8,128)(2,1)S(1)} %get-tuple-element.9), channel_id=1, source_target_pairs={{2,4},{6,8},{10,12},{18,20},{22,24},{26,28},{0,16},{4,2},{8,6},{12... | collective-permute-start | bytes 368648 | tf_op jit(solution)/shard_map/ppermute | solution.py:479
  14.1 5.0 %copy-start.3 = (s32[32,32,128]{2,1,0:T(8,128)S(1)}, s32[32,32,128]{2,1,0:T(8,128)}, u32[]{:S(2)}) copy-start(s32[32,32,128]{2,1,0:T(8,128)} %param.8) | copy-start | bytes 1572868
  14.1 5.0 %collective-permute-start.3 = (bf16[7,48,128]{2,1,0:T(8,128)(2,1)S(1)}, bf16[7,48,128]{2,1,0:T(8,128)(2,1)S(1)}, u32[]{:S(2)}, u32[]{:S(2)}) collective-permute-start(bf16[7,48,128]{2,1,0:T(8,128)(2,1)S(1)} %shard_map.58), channel_id=1, source_target_pairs={{0,1},{1,0},{2,3},{3,2},{4,5},{5,4},{6,7},{7,6},{8,9},{9,8},{10,11... | collective-permute-start | bytes 258056 | tf_op jit(solution)/shard_map/ppermute | solution.py:506

commit v6 on v5

--- a/solution.py
+++ b/solution.py
@@ -476,7 +476,7 @@
     inner = both([(k, k + 1) for k in range(0, ngx, 2)])
     a = lax.ppermute(send_a, "gx", inner)
     outer = [(k * ngx + i, k * ngx + i + 1) for k in range(2) for i in range(1, ngx - 1, 2)]
-    b = lax.ppermute(send_b, ("comp", "gx"), both(outer + [(0, ngx)]))
+    b = lax.ppermute(send_b, ("comp", "gx"), both(outer + [(0, ngx), (ngx - 1, 2 * ngx - 1)]))
 
     shape = jax.ShapeDtypeStruct((nf, nx * ny, nz), F32)
     cells = nf * nx * ny * nz

time: 24.1 us -> 22 us (0.913)
  starting transfers between devices: 7.16 us -> 5.12 us
    ppermute x1, starting transfers between devices: 3.55 us -> 1.52 us  [body(): lax.ppermute(send_b, ('comp', 'gx'), both(outer + [(0, ngx), (ngx - 1, 2...]
  transfers between devices with their start and end apart: 4 -> 4, of which waited for: 0 -> 0; matrix products, arithmetic and copies ran while one was open for 0% -> 0% of each run, Pallas kernels for 35% -> 39%
where the time goes in v6:
time: 22 us; the launch traced here: 21.9 us
  Pallas kernels  13.5 us (61%)
  starting transfers between devices  5.12 us (23%)
  local copies, waits for them, and re-layouts  3.12 us (14%)
    pallas_call x2, Pallas kernels, section(): pl.pallas_call(functools.partial(section_kernel, dims, second), out_shape...  8.39 us
    pallas_call x1, Pallas kernels, body(): pl.pallas_call(functools.partial(border_kernel, dims, two), out_shape=jax...  4.78 us
    unnamed x14, local copies, waits for them, and re-layouts  3.12 us
    ppermute x1, starting transfers between devices, body(): c1 = lax.ppermute(send_c, 'gy', swap)  3 us
    ppermute x1, starting transfers between devices, body(): lax.ppermute(send_b, ('comp', 'gx'), both(outer + [(0, ngx), (ngx - 1, 2...  1.52 us
    ppermute x1, starting transfers between devices, body(): c2 = lax.ppermute(extra, 'gy', swap)  0.59 us
  transfers between devices with their start and end apart: 4, of which 0 were waited for; matrix products, arithmetic and copies ran while one was open for 0% of the time, Pallas kernels for 39%

profile of v6, /device:TPU:0, one launch (start us, length us, event | category | flops | bytes accessed | tf_op | source)
XLA Modules:
  0.0 21.9 jit_solution(16870971259284928490)
XLA Ops:
  0.0 0.0 copy-start.5
  0.0 0.0 copy-start.4
  0.0 0.0 copy-start
  0.0 2.1 %copy-done = f32[1,7,32,32,128]{4,3,2,1,0:T(8,128)S(1)} copy-done((f32[1,7,32,32,128]{4,3,2,1,0:T(8,128)S(1)}, f32[1,7,32,32,128]{4,3,2,1,0:T(8,128)}, u32[]{:S(2)}) %copy-start) | copy-done | bytes 3670040
  2.1 0.0 copy-start.2
  2.1 1.0 %copy-done.2 = s32[32,32,128]{2,1,0:T(8,128)S(1)} copy-done((s32[32,32,128]{2,1,0:T(8,128)S(1)}, s32[32,32,128]{2,1,0:T(8,128)}, u32[]{:S(2)}) %copy-start.2) | copy-done | bytes 524312
  3.1 0.0 copy-start.1
  3.1 0.3 %shard_map.57 = (bf16[15,32,128]{2,1,0:T(8,128)(2,1)S(1)}, bf16[15,32,128]{2,1,0:T(8,128)(2,1)S(1)}, bf16[30,32,128]{2,1,0:T(8,128)(2,1)S(1)}) custom-call(f32[7,1024,128]{2,1,0:T(8,128)S(1)} %bitcast.5, s32[1024,128]{1,0:T(8,128)S(1)} %bitcast.10), custom_call_target="tpu_custom_call" | custom-call | tf_op jit(solution)/shard_map/pallas_call | solution.py:456
  3.4 3.0 %collective-permute-start.2 = (bf16[30,32,128]{2,1,0:T(8,128)(2,1)S(1)}, bf16[30,32,128]{2,1,0:T(8,128)(2,1)S(1)}, u32[]{:S(2)}, u32[]{:S(2)}) collective-permute-start(bf16[30,32,128]{2,1,0:T(8,128)(2,1)S(1)} %get-tuple-element.10), channel_id=1, source_target_pairs={{0,1},{1,0},{2,3},{3,2},{4,5},{5,4},{6,7},{7,6},{8,9},{9,8},{10,11... | collective-permute-start | bytes 737288 | tf_op jit(solution)/shard_map/ppermute | solution.py:466
  6.4 0.0 collective-permute-start
  6.4 0.0 copy-start.6
  6.4 1.5 %collective-permute-start.1 = (bf16[15,32,128]{2,1,0:T(8,128)(2,1)S(1)}, bf16[15,32,128]{2,1,0:T(8,128)(2,1)S(1)}, u32[]{:S(2)}, u32[]{:S(2)}) collective-permute-start(bf16[15,32,128]{2,1,0:T(8,128)(2,1)S(1)} %get-tuple-element.9), channel_id=1, source_target_pairs={{2,4},{6,8},{10,12},{18,20},{22,24},{26,28},{0,16},{14,30},{4,2},{... | collective-permute-start | bytes 368648 | tf_op jit(solution)/shard_map/ppermute | solution.py:479
  7.9 0.0 copy-done.5
  8.0 0.0 copy-done.4
  8.0 0.0 copy-done.1
  8.0 4.0 %shard_map.55.refs_3_.after_ref.refs_4_ = f32[7,1024,128]{2,1,0:T(8,128)S(1)} custom-call(f32[2,7]{1,0:T(2,128)S(1)} %copy-done.4, f32[2,7]{1,0:T(2,128)S(1)} %copy-done.5, f32[7,1024,128]{2,1,0:T(8,128)S(1)} %bitcast.6, s32[1024,128]{1,0:T(8,128)S(1)} %bitcast.11), custom_call_target="tpu_custom_call" | custom-call | flops 18350080 | bytes 7340032 | tf_op jit(solution)/shard_map/pallas_call | solution.py:485
  12.0 0.0 collective-permute-done.a_ref.refs_7_
  12.0 0.0 collective-permute-done.1.b_ref.refs_8_
  12.0 0.0 copy-done.6
  12.0 0.1 shard_map.58
  12.1 0.0 copy-start.3
  12.1 0.6 %collective-permute-start.3 = (bf16[7,48,128]{2,1,0:T(8,128)(2,1)S(1)}, bf16[7,48,128]{2,1,0:T(8,128)(2,1)S(1)}, u32[]{:S(2)}, u32[]{:S(2)}) collective-permute-start(bf16[7,48,128]{2,1,0:T(8,128)(2,1)S(1)} %shard_map.58), channel_id=1, source_target_pairs={{0,1},{1,0},{2,3},{3,2},{4,5},{5,4},{6,7},{7,6},{8,9},{9,8},{10,11... | collective-permute-start | bytes 258056 | tf_op jit(solution)/shard_map/ppermute | solution.py:506
  12.7 4.4 %shard_map.56 = f32[7,1024,128]{2,1,0:T(8,128)S(1)} custom-call(f32[2,7]{1,0:T(2,128)S(1)} %copy-done.4, f32[2,7]{1,0:T(2,128)S(1)} %copy-done.5, f32[7,1024,128]{2,1,0:T(8,128)S(1)} %bitcast.7, f32[7,1024,128]{2,1,0:T(8,128)S(1)} %shard_map.55.refs_3_.after_ref.refs_4_, s32[1024,128]{1,0:T(8,128)S(1)} %bitcast.12), custom_call_target="tpu_custom_call" | custom-call | flops 18350080 | bytes 7340032 | tf_op jit(solution)/shard_map/pallas_call | solution.py:485
  17.0 0.0 collective-permute-done.3.refs_10_.refs_11_
  17.1 0.0 collective-permute-done.2.refs_9_
  17.1 0.0 copy-done.3
  17.1 4.8 %shard_map.59 = f32[7,32,32,128]{3,2,1,0:T(8,128)} custom-call(f32[2,7]{1,0:T(2,128)S(1)} %copy-done.4, f32[2,7]{1,0:T(2,128)S(1)} %copy-done.5, s32[1,32]{1,0:T(1,128)S(1)} %bitcast.15, f32[7,1024,128]{2,1,0:T(8,128)S(1)} %bitcast.8, f32[7,1024,128]{2,1,0:T(8,128)S(1)} %shard_map.55.refs_3_.after_ref.refs_4_, f32[7,32,32,128]{3,2,1,0:T(8,128)S(1)} %bitcast.9, ...), custom_call_target="tpu_custom_call" | custom-call | flops 9175040 | bytes 7340032 | tf_op jit(solution)/shard_map/pallas_call | solution.py:515
Async XLA Ops:
  0.0 8.0 %copy-start.5 = (f32[2,7]{1,0:T(2,128)S(1)}, f32[2,7]{1,0:T(2,128)}, u32[]{:S(2)}) copy-start(f32[2,7]{1,0:T(2,128)} %refs_1_.5) | copy-start | bytes 172
  0.0 8.0 %copy-start.4 = (f32[2,7]{1,0:T(2,128)S(1)}, f32[2,7]{1,0:T(2,128)}, u32[]{:S(2)}) copy-start(f32[2,7]{1,0:T(2,128)} %refs_0_.5) | copy-start | bytes 172
  0.0 2.1 %copy-start = (f32[1,7,32,32,128]{4,3,2,1,0:T(8,128)S(1)}, f32[1,7,32,32,128]{4,3,2,1,0:T(8,128)}, u32[]{:S(2)}) copy-start(f32[1,7,32,32,128]{4,3,2,1,0:T(8,128)} %param.5) | copy-start | bytes 11010052
  2.1 1.0 %copy-start.2 = (s32[32,32,128]{2,1,0:T(8,128)S(1)}, s32[32,32,128]{2,1,0:T(8,128)}, u32[]{:S(2)}) copy-start(s32[32,32,128]{2,1,0:T(8,128)} %param.8) | copy-start | bytes 1572868
  3.1 4.8 %copy-start.1 = (f32[1,7,32,32,128]{4,3,2,1,0:T(8,128)S(1)}, f32[1,7,32,32,128]{4,3,2,1,0:T(8,128)}, u32[]{:S(2)}) copy-start(f32[1,7,32,32,128]{4,3,2,1,0:T(8,128)} %param.5) | copy-start | bytes 11010052
  3.4 13.6 %collective-permute-start.2 = (bf16[30,32,128]{2,1,0:T(8,128)(2,1)S(1)}, bf16[30,32,128]{2,1,0:T(8,128)(2,1)S(1)}, u32[]{:S(2)}, u32[]{:S(2)}) collective-permute-start(bf16[30,32,128]{2,1,0:T(8,128)(2,1)S(1)} %get-tuple-element.10), channel_id=1, source_target_pairs={{0,1},{1,0},{2,3},{3,2},{4,5},{5,4},{6,7},{7,6},{8,9},{9,8},{10,11... | collective-permute-start | bytes 737288 | tf_op jit(solution)/shard_map/ppermute | solution.py:466
  6.4 5.6 %collective-permute-start = (bf16[15,32,128]{2,1,0:T(8,128)(2,1)S(1)}, bf16[15,32,128]{2,1,0:T(8,128)(2,1)S(1)}, u32[]{:S(2)}, u32[]{:S(2)}) collective-permute-start(bf16[15,32,128]{2,1,0:T(8,128)(2,1)S(1)} %get-tuple-element.8), channel_id=1, source_target_pairs={{0,2},{4,6},{8,10},{12,14},{2,0},{6,4},{10,8},{14,12},{1,3},{5,7},... | collective-permute-start | bytes 368648 | tf_op jit(solution)/shard_map/ppermute | solution.py:477
  6.4 5.6 %copy-start.6 = (s32[32]{0:T(128)S(1)}, s32[32]{0:T(128)}, u32[]{:S(2)}) copy-start(s32[32]{0:T(128)} %param.9) | copy-start | bytes 388
  6.4 5.6 %collective-permute-start.1 = (bf16[15,32,128]{2,1,0:T(8,128)(2,1)S(1)}, bf16[15,32,128]{2,1,0:T(8,128)(2,1)S(1)}, u32[]{:S(2)}, u32[]{:S(2)}) collective-permute-start(bf16[15,32,128]{2,1,0:T(8,128)(2,1)S(1)} %get-tuple-element.9), channel_id=1, source_target_pairs={{2,4},{6,8},{10,12},{18,20},{22,24},{26,28},{0,16},{14,30},{4,2},{... | collective-permute-start | bytes 368648 | tf_op jit(solution)/shard_map/ppermute | solution.py:479
  12.1 5.0 %copy-start.3 = (s32[32,32,128]{2,1,0:T(8,128)S(1)}, s32[32,32,128]{2,1,0:T(8,128)}, u32[]{:S(2)}) copy-start(s32[32,32,128]{2,1,0:T(8,128)} %param.8) | copy-start | bytes 1572868
  12.1 5.0 %collective-permute-start.3 = (bf16[7,48,128]{2,1,0:T(8,128)(2,1)S(1)}, bf16[7,48,128]{2,1,0:T(8,128)(2,1)S(1)}, u32[]{:S(2)}, u32[]{:S(2)}) collective-permute-start(bf16[7,48,128]{2,1,0:T(8,128)(2,1)S(1)} %shard_map.58), channel_id=1, source_target_pairs={{0,1},{1,0},{2,3},{3,2},{4,5},{5,4},{6,7},{7,6},{8,9},{9,8},{10,11... | collective-permute-start | bytes 258056 | tf_op jit(solution)/shard_map/ppermute | solution.py:506

commit v7 on v6

--- a/solution.py
+++ b/solution.py
@@ -194,7 +194,7 @@
         (dif, adv, imap, q_ref, first_ref, main_ref, s_ref, a_ref, b_ref, c1_ref, c2l_ref, c2h_ref,
          face_ref, map_ref) = refs[:14]
         rest = refs[14:]
-    out_ref, sm, lay, pla, qp, ms, cor, fl, fp, cx, cy, ep, ol, strips, zin, zout, sem = rest
+    out_ref, sm, lay, pla, qp, ms, cor, fl, fp, cx, cy, ep, ol, strips, zout, sem = rest
     d, c, level = scalars(dif, adv, nf)
     comp = lax.axis_index("comp")
     stream, last = lax.axis_index("gx"), lax.axis_size("gx") - 1
@@ -319,13 +319,12 @@
         for n, src in enumerate(centers):
             gs.append(gains(src))
             tall = [src(f, k) for f in range(nf) for k in every] + gs[-1]
-            zin[pl.ds(n * (nf + 1) * ny, (nf + 1) * ny)] = jnp.concatenate(tall, 0).astype(BF)
-        zout[...] = jnp.dot(zin[...], sm[...], preferred_element_type=F32)
+            zout[n] = jnp.dot(jnp.concatenate(tall, 0).astype(BF), sm[...], preferred_element_type=F32)
         return gs
 
     def slab(n, g, center, before, after, low, high, solid, along_outer):
         def z(f, k, h):
-            return zout[(n * (nf + 1) + f) * ny + 8 * k : (n * (nf + 1) + f) * ny + 8 * k + 8, h * nz : (h + 1) * nz]
+            return zout[n, f * ny + 8 * k : f * ny + 8 * k + 8, h * nz : (h + 1) * nz]
 
         def ups(v, edge):
             return v[1:] + [jnp.where(sub == 7, edge, pltpu.roll(v[0], 7, 0))]
@@ -370,18 +369,13 @@
         return res
 
     g = products([held(lay, LO), held(lay, HI), held(pla, LO), held(pla, HI)])
-    put(fl, 0, slab(0, g[0], held(lay, LO), held(lay, FAR_LO), q_layer(0), corner(0), corner(1), s_halo(0), True))
-    put(fl, 5, slab(1, g[1], held(lay, HI), q_layer(nx - 1), held(lay, FAR_HI), corner(2), corner(3), s_halo(1), True))
+    ghost, ahead = held(lay, LO), jnp.where(stream == last, 0.0, 1.0)
+    vals = slab(0, g[0], held(lay, LO), held(lay, FAR_LO), q_layer(0), corner(0), corner(1), s_halo(0), True)
+    put(fl, 0, [[jnp.where(stream == 0, ghost(f, k), vals[f][k]) for k in every] for f in range(nf)])
+    vals = slab(1, g[1], held(lay, HI), q_layer(nx - 1), held(lay, FAR_HI), corner(2), corner(3), s_halo(1), True)
+    put(fl, 5, [[ahead * vals[f][k] for k in every] for f in range(nf)])
     put(fp, 0, slab(2, g[2], held(pla, LO), held(pla, FAR_LO), q_plane(0), corner(0), corner(2), s_halo(2), False))
     put(fp, 5, slab(3, g[3], held(pla, HI), q_plane(ny - 1), held(pla, FAR_HI), corner(1), corner(3), s_halo(3), False))
-
-    @pl.when(stream == 0)
-    def _():
-        fl[0] = lay[LO]
-
-    @pl.when(stream == last)
-    def _():
-        fl[5] = jnp.zeros(fl.shape[1:], F32)
 
     put(cx, 0, passed(q_layer(0), held(lay, LO), s_layer(0), True, False))
     put(cx, 1, passed(q_layer(nx - 1), held(lay, HI), s_layer(nx - 1), True, True))
@@ -521,7 +515,7 @@
             mb((nz, 2 * nz), BF), mb((4, nf, ny, nz), F32), mb((4, nf, nx, nz), F32), mb((2, nf, nx, nz), F32), mb((4, ny, nz), F32),
             mb((4, 8, nz), F32), mb((6, nf, ny, nz), F32), mb((6, nf, nx, nz), F32), mb((2, nf, ny, nz), F32),
             mb((2, nf, nx, nz), F32), mb((2, nf, nx, nz), F32), mb((4, nf, ny, nz), F32), mb((2, nf, nx, 8, nz), F32),
-            mb((4 * (nf + 1) * ny, nz), BF), mb((4 * (nf + 1) * ny, 2 * nz), F32),
+            mb((4, (nf + 1) * ny, 2 * nz), F32),
             pltpu.SemaphoreType.DMA((4, 8)),
         ],
         compiler_params=pltpu.CompilerParams(vmem_limit_bytes=10 << 20),

time: 22 us -> 21.9 us (level)
  no operation moved by 1% of the time
where the time goes in v7:
time: 21.9 us; the launch traced here: 21.8 us
  Pallas kernels  13.4 us (61%)
  starting transfers between devices  5.12 us (23%)
  local copies, waits for them, and re-layouts  3.12 us (14%)
    pallas_call x2, Pallas kernels, section(): pl.pallas_call(functools.partial(section_kernel, dims, second), out_shape...  8.39 us
    pallas_call x1, Pallas kernels, body(): pl.pallas_call(functools.partial(border_kernel, dims, two), out_shape=jax...  4.67 us
    unnamed x14, local copies, waits for them, and re-layouts  3.12 us
    ppermute x1, starting transfers between devices, body(): c1 = lax.ppermute(send_c, 'gy', swap)  3 us
    ppermute x1, starting transfers between devices, body(): lax.ppermute(send_b, ('comp', 'gx'), both(outer + [(0, ngx), (ngx - 1, 2...  1.52 us
    ppermute x1, starting transfers between devices, body(): c2 = lax.ppermute(extra, 'gy', swap)  0.59 us
  transfers between devices with their start and end apart: 4, of which 0 were waited for; matrix products, arithmetic and copies ran while one was open for 0% of the time, Pallas kernels for 39%

profile of v7, /device:TPU:0, one launch (start us, length us, event | category | flops | bytes accessed | tf_op | source)
XLA Modules:
  0.0 21.8 jit_solution(15403847236358378073)
XLA Ops:
  0.0 0.0 copy-start.5
  0.0 0.0 copy-start.4
  0.0 0.0 copy-start
  0.0 2.1 %copy-done = f32[1,7,32,32,128]{4,3,2,1,0:T(8,128)S(1)} copy-done((f32[1,7,32,32,128]{4,3,2,1,0:T(8,128)S(1)}, f32[1,7,32,32,128]{4,3,2,1,0:T(8,128)}, u32[]{:S(2)}) %copy-start) | copy-done | bytes 3670040
  2.1 0.0 copy-start.2
  2.1 1.0 %copy-done.2 = s32[32,32,128]{2,1,0:T(8,128)S(1)} copy-done((s32[32,32,128]{2,1,0:T(8,128)S(1)}, s32[32,32,128]{2,1,0:T(8,128)}, u32[]{:S(2)}) %copy-start.2) | copy-done | bytes 524312
  3.1 0.0 copy-start.1
  3.1 0.3 %shard_map.57 = (bf16[15,32,128]{2,1,0:T(8,128)(2,1)S(1)}, bf16[15,32,128]{2,1,0:T(8,128)(2,1)S(1)}, bf16[30,32,128]{2,1,0:T(8,128)(2,1)S(1)}) custom-call(f32[7,1024,128]{2,1,0:T(8,128)S(1)} %bitcast.5, s32[1024,128]{1,0:T(8,128)S(1)} %bitcast.10), custom_call_target="tpu_custom_call" | custom-call | tf_op jit(solution)/shard_map/pallas_call | solution.py:450
  3.4 3.0 %collective-permute-start.2 = (bf16[30,32,128]{2,1,0:T(8,128)(2,1)S(1)}, bf16[30,32,128]{2,1,0:T(8,128)(2,1)S(1)}, u32[]{:S(2)}, u32[]{:S(2)}) collective-permute-start(bf16[30,32,128]{2,1,0:T(8,128)(2,1)S(1)} %get-tuple-element.10), channel_id=1, source_target_pairs={{0,1},{1,0},{2,3},{3,2},{4,5},{5,4},{6,7},{7,6},{8,9},{9,8},{10,11... | collective-permute-start | bytes 737288 | tf_op jit(solution)/shard_map/ppermute | solution.py:460
  6.4 0.0 collective-permute-start
  6.4 0.0 copy-start.6
  6.4 1.5 %collective-permute-start.1 = (bf16[15,32,128]{2,1,0:T(8,128)(2,1)S(1)}, bf16[15,32,128]{2,1,0:T(8,128)(2,1)S(1)}, u32[]{:S(2)}, u32[]{:S(2)}) collective-permute-start(bf16[15,32,128]{2,1,0:T(8,128)(2,1)S(1)} %get-tuple-element.9), channel_id=1, source_target_pairs={{2,4},{6,8},{10,12},{18,20},{22,24},{26,28},{0,16},{14,30},{4,2},{... | collective-permute-start | bytes 368648 | tf_op jit(solution)/shard_map/ppermute | solution.py:473
  7.9 0.0 copy-done.5
  8.0 0.0 copy-done.4
  8.0 0.0 copy-done.1
  8.0 4.0 %shard_map.55.refs_3_.after_ref.refs_4_ = f32[7,1024,128]{2,1,0:T(8,128)S(1)} custom-call(f32[2,7]{1,0:T(2,128)S(1)} %copy-done.4, f32[2,7]{1,0:T(2,128)S(1)} %copy-done.5, f32[7,1024,128]{2,1,0:T(8,128)S(1)} %bitcast.6, s32[1024,128]{1,0:T(8,128)S(1)} %bitcast.11), custom_call_target="tpu_custom_call" | custom-call | flops 18350080 | bytes 7340032 | tf_op jit(solution)/shard_map/pallas_call | solution.py:479
  12.0 0.0 collective-permute-done.a_ref.refs_7_
  12.0 0.0 collective-permute-done.1.b_ref.refs_8_
  12.0 0.0 copy-done.6
  12.0 0.1 shard_map.58
  12.1 0.0 copy-start.3
  12.1 0.6 %collective-permute-start.3 = (bf16[7,48,128]{2,1,0:T(8,128)(2,1)S(1)}, bf16[7,48,128]{2,1,0:T(8,128)(2,1)S(1)}, u32[]{:S(2)}, u32[]{:S(2)}) collective-permute-start(bf16[7,48,128]{2,1,0:T(8,128)(2,1)S(1)} %shard_map.58), channel_id=1, source_target_pairs={{0,1},{1,0},{2,3},{3,2},{4,5},{5,4},{6,7},{7,6},{8,9},{9,8},{10,11... | collective-permute-start | bytes 258056 | tf_op jit(solution)/shard_map/ppermute | solution.py:500
  12.7 4.4 %shard_map.56 = f32[7,1024,128]{2,1,0:T(8,128)S(1)} custom-call(f32[2,7]{1,0:T(2,128)S(1)} %copy-done.4, f32[2,7]{1,0:T(2,128)S(1)} %copy-done.5, f32[7,1024,128]{2,1,0:T(8,128)S(1)} %bitcast.7, f32[7,1024,128]{2,1,0:T(8,128)S(1)} %shard_map.55.refs_3_.after_ref.refs_4_, s32[1024,128]{1,0:T(8,128)S(1)} %bitcast.12), custom_call_target="tpu_custom_call" | custom-call | flops 18350080 | bytes 7340032 | tf_op jit(solution)/shard_map/pallas_call | solution.py:479
  17.0 0.0 collective-permute-done.3.refs_10_.refs_11_
  17.1 0.0 collective-permute-done.2.refs_9_
  17.1 0.0 copy-done.3
  17.1 4.7 %shard_map.59 = f32[7,32,32,128]{3,2,1,0:T(8,128)} custom-call(f32[2,7]{1,0:T(2,128)S(1)} %copy-done.4, f32[2,7]{1,0:T(2,128)S(1)} %copy-done.5, s32[1,32]{1,0:T(1,128)S(1)} %bitcast.15, f32[7,1024,128]{2,1,0:T(8,128)S(1)} %bitcast.8, f32[7,1024,128]{2,1,0:T(8,128)S(1)} %shard_map.55.refs_3_.after_ref.refs_4_, f32[7,32,32,128]{3,2,1,0:T(8,128)S(1)} %bitcast.9, ...), custom_call_target="tpu_custom_call" | custom-call | flops 9175040 | bytes 7340032 | tf_op jit(solution)/shard_map/pallas_call | solution.py:509
Async XLA Ops:
  0.0 8.0 %copy-start.5 = (f32[2,7]{1,0:T(2,128)S(1)}, f32[2,7]{1,0:T(2,128)}, u32[]{:S(2)}) copy-start(f32[2,7]{1,0:T(2,128)} %refs_1_.5) | copy-start | bytes 172
  0.0 8.0 %copy-start.4 = (f32[2,7]{1,0:T(2,128)S(1)}, f32[2,7]{1,0:T(2,128)}, u32[]{:S(2)}) copy-start(f32[2,7]{1,0:T(2,128)} %refs_0_.5) | copy-start | bytes 172
  0.0 2.1 %copy-start = (f32[1,7,32,32,128]{4,3,2,1,0:T(8,128)S(1)}, f32[1,7,32,32,128]{4,3,2,1,0:T(8,128)}, u32[]{:S(2)}) copy-start(f32[1,7,32,32,128]{4,3,2,1,0:T(8,128)} %param.5) | copy-start | bytes 11010052
  2.1 1.0 %copy-start.2 = (s32[32,32,128]{2,1,0:T(8,128)S(1)}, s32[32,32,128]{2,1,0:T(8,128)}, u32[]{:S(2)}) copy-start(s32[32,32,128]{2,1,0:T(8,128)} %param.8) | copy-start | bytes 1572868
  3.1 4.8 %copy-start.1 = (f32[1,7,32,32,128]{4,3,2,1,0:T(8,128)S(1)}, f32[1,7,32,32,128]{4,3,2,1,0:T(8,128)}, u32[]{:S(2)}) copy-start(f32[1,7,32,32,128]{4,3,2,1,0:T(8,128)} %param.5) | copy-start | bytes 11010052
  3.4 13.6 %collective-permute-start.2 = (bf16[30,32,128]{2,1,0:T(8,128)(2,1)S(1)}, bf16[30,32,128]{2,1,0:T(8,128)(2,1)S(1)}, u32[]{:S(2)}, u32[]{:S(2)}) collective-permute-start(bf16[30,32,128]{2,1,0:T(8,128)(2,1)S(1)} %get-tuple-element.10), channel_id=1, source_target_pairs={{0,1},{1,0},{2,3},{3,2},{4,5},{5,4},{6,7},{7,6},{8,9},{9,8},{10,11... | collective-permute-start | bytes 737288 | tf_op jit(solution)/shard_map/ppermute | solution.py:460
  6.4 5.6 %collective-permute-start = (bf16[15,32,128]{2,1,0:T(8,128)(2,1)S(1)}, bf16[15,32,128]{2,1,0:T(8,128)(2,1)S(1)}, u32[]{:S(2)}, u32[]{:S(2)}) collective-permute-start(bf16[15,32,128]{2,1,0:T(8,128)(2,1)S(1)} %get-tuple-element.8), channel_id=1, source_target_pairs={{0,2},{4,6},{8,10},{12,14},{2,0},{6,4},{10,8},{14,12},{1,3},{5,7},... | collective-permute-start | bytes 368648 | tf_op jit(solution)/shard_map/ppermute | solution.py:471
  6.4 5.6 %copy-start.6 = (s32[32]{0:T(128)S(1)}, s32[32]{0:T(128)}, u32[]{:S(2)}) copy-start(s32[32]{0:T(128)} %param.9) | copy-start | bytes 388
  6.4 5.6 %collective-permute-start.1 = (bf16[15,32,128]{2,1,0:T(8,128)(2,1)S(1)}, bf16[15,32,128]{2,1,0:T(8,128)(2,1)S(1)}, u32[]{:S(2)}, u32[]{:S(2)}) collective-permute-start(bf16[15,32,128]{2,1,0:T(8,128)(2,1)S(1)} %get-tuple-element.9), channel_id=1, source_target_pairs={{2,4},{6,8},{10,12},{18,20},{22,24},{26,28},{0,16},{14,30},{4,2},{... | collective-permute-start | bytes 368648 | tf_op jit(solution)/shard_map/ppermute | solution.py:473
  12.1 5.0 %copy-start.3 = (s32[32,32,128]{2,1,0:T(8,128)S(1)}, s32[32,32,128]{2,1,0:T(8,128)}, u32[]{:S(2)}) copy-start(s32[32,32,128]{2,1,0:T(8,128)} %param.8) | copy-start | bytes 1572868
  12.1 5.0 %collective-permute-start.3 = (bf16[7,48,128]{2,1,0:T(8,128)(2,1)S(1)}, bf16[7,48,128]{2,1,0:T(8,128)(2,1)S(1)}, u32[]{:S(2)}, u32[]{:S(2)}) collective-permute-start(bf16[7,48,128]{2,1,0:T(8,128)(2,1)S(1)} %shard_map.58), channel_id=1, source_target_pairs={{0,1},{1,0},{2,3},{3,2},{4,5},{5,4},{6,7},{7,6},{8,9},{9,8},{10,11... | collective-permute-start | bytes 258056 | tf_op jit(solution)/shard_map/ppermute | solution.py:500

commit v8 on v7

--- a/solution.py
+++ b/solution.py
@@ -102,6 +102,7 @@
         ups, downs = (accs[:n], accs[n : 2 * n]), (accs[2 * n : 3 * n], accs[3 * n :])
         d, c, level = scalars(dif, adv, nf)
         lo, hi = (1, nx - 2) if second else (0, nx - 1)
+        deep = next(n for n in (8, 6, 4, 2) if (hi + 1 - lo) % n == 0)
         closed = (0, ny - 2) if second else (ny - 1,)
         sub = lax.broadcasted_iota(jnp.int32, (8, nz), 0)
         fx[...] = jnp.zeros_like(fx)
@@ -166,18 +167,19 @@
                         o_ref[f, at(x, k)] = new
 
         def step(i, g):
-            x = 2 * i + lo
-            push(x + 1, 1, g)
-            g = prepare(x + 1, 1, g)
-            compute(x, 0)
-            push(jnp.minimum(x + 2, hi), 0, g)
-            g = prepare(x + 2, 0, g)
-            compute(x + 1, 1)
+            for j in range(0, deep, 2):
+                x = deep * i + lo + j
+                push(x + 1, 1, g)
+                g = prepare(x + 1, 1, g)
+                compute(x, 0)
+                push(jnp.minimum(x + 2, hi), 0, g)
+                g = prepare(x + 2, 0, g)
+                compute(x + 1, 1)
             return g
 
         g = [gain(v) for v in layer(4, lo)]
         push(lo, 0, g, 0)
-        lax.fori_loop(0, (hi + 1 - lo) // 2, step, prepare(lo, 0, g))
+        lax.fori_loop(0, (hi + 1 - lo) // deep, step, prepare(lo, 0, g))
         for acc in ups[0] + downs[0]:
             pltpu.matmul_pop(acc)
 

time: 21.9 us -> 21.3 us (0.973)
  Pallas kernels: 13.4 us -> 12.7 us
    pallas_call x2, Pallas kernels: 8.39 us -> 7.66 us  [section(): pl.pallas_call(functools.partial(section_kernel, dims, second), out_shape...]
  transfers between devices with their start and end apart: 4 -> 4, of which waited for: 0 -> 1; matrix products, arithmetic and copies ran while one was open for 0% -> 0% of each run, Pallas kernels for 39% -> 36%
where the time goes in v8:
time: 21.3 us; the launch traced here: 21.2 us
  Pallas kernels  12.7 us (60%)
  starting transfers between devices  5.12 us (24%)
  local copies, waits for them, and re-layouts  3.12 us (15%)
    pallas_call x2, Pallas kernels, section(): pl.pallas_call(functools.partial(section_kernel, dims, second), out_shape...  7.66 us
    pallas_call x1, Pallas kernels, body(): pl.pallas_call(functools.partial(border_kernel, dims, two), out_shape=jax...  4.67 us
    unnamed x14, local copies, waits for them, and re-layouts  3.12 us
    ppermute x1, starting transfers between devices, body(): c1 = lax.ppermute(send_c, 'gy', swap)  3 us
    ppermute x1, starting transfers between devices, body(): lax.ppermute(send_b, ('comp', 'gx'), both(outer + [(0, ngx), (ngx - 1, 2...  1.52 us
    ppermute x1, starting transfers between devices, body(): c2 = lax.ppermute(extra, 'gy', swap)  0.59 us
  transfers between devices with their start and end apart: 4, of which 1 were waited for; matrix products, arithmetic and copies ran while one was open for 0% of the time, Pallas kernels for 36%

profile of v8, /device:TPU:0, one launch (start us, length us, event | category | flops | bytes accessed | tf_op | source)
XLA Modules:
  0.0 21.2 jit_solution(5794635087498857731)
XLA Ops:
  0.0 0.0 copy-start.5
  0.0 0.0 copy-start.4
  0.0 0.0 copy-start
  0.0 2.1 %copy-done = f32[1,7,32,32,128]{4,3,2,1,0:T(8,128)S(1)} copy-done((f32[1,7,32,32,128]{4,3,2,1,0:T(8,128)S(1)}, f32[1,7,32,32,128]{4,3,2,1,0:T(8,128)}, u32[]{:S(2)}) %copy-start) | copy-done | bytes 3670040
  2.1 0.0 copy-start.2
  2.1 1.0 %copy-done.2 = s32[32,32,128]{2,1,0:T(8,128)S(1)} copy-done((s32[32,32,128]{2,1,0:T(8,128)S(1)}, s32[32,32,128]{2,1,0:T(8,128)}, u32[]{:S(2)}) %copy-start.2) | copy-done | bytes 524312
  3.1 0.0 copy-start.1
  3.1 0.3 %shard_map.57 = (bf16[15,32,128]{2,1,0:T(8,128)(2,1)S(1)}, bf16[15,32,128]{2,1,0:T(8,128)(2,1)S(1)}, bf16[30,32,128]{2,1,0:T(8,128)(2,1)S(1)}) custom-call(f32[7,1024,128]{2,1,0:T(8,128)S(1)} %bitcast.5, s32[1024,128]{1,0:T(8,128)S(1)} %bitcast.10), custom_call_target="tpu_custom_call" | custom-call | tf_op jit(solution)/shard_map/pallas_call | solution.py:452
  3.4 3.0 %collective-permute-start.2 = (bf16[30,32,128]{2,1,0:T(8,128)(2,1)S(1)}, bf16[30,32,128]{2,1,0:T(8,128)(2,1)S(1)}, u32[]{:S(2)}, u32[]{:S(2)}) collective-permute-start(bf16[30,32,128]{2,1,0:T(8,128)(2,1)S(1)} %get-tuple-element.10), channel_id=1, source_target_pairs={{0,1},{1,0},{2,3},{3,2},{4,5},{5,4},{6,7},{7,6},{8,9},{9,8},{10,11... | collective-permute-start | bytes 737288 | tf_op jit(solution)/shard_map/ppermute | solution.py:462
  6.4 0.0 collective-permute-start
  6.4 0.0 copy-start.6
  6.4 1.5 %collective-permute-start.1 = (bf16[15,32,128]{2,1,0:T(8,128)(2,1)S(1)}, bf16[15,32,128]{2,1,0:T(8,128)(2,1)S(1)}, u32[]{:S(2)}, u32[]{:S(2)}) collective-permute-start(bf16[15,32,128]{2,1,0:T(8,128)(2,1)S(1)} %get-tuple-element.9), channel_id=1, source_target_pairs={{2,4},{6,8},{10,12},{18,20},{22,24},{26,28},{0,16},{14,30},{4,2},{... | collective-permute-start | bytes 368648 | tf_op jit(solution)/shard_map/ppermute | solution.py:475
  7.9 0.0 copy-done.5
  8.0 0.0 copy-done.4
  8.0 0.0 copy-done.1
  8.0 3.7 %shard_map.55.refs_3_.after_ref.refs_4_ = f32[7,1024,128]{2,1,0:T(8,128)S(1)} custom-call(f32[2,7]{1,0:T(2,128)S(1)} %copy-done.4, f32[2,7]{1,0:T(2,128)S(1)} %copy-done.5, f32[7,1024,128]{2,1,0:T(8,128)S(1)} %bitcast.6, s32[1024,128]{1,0:T(8,128)S(1)} %bitcast.11), custom_call_target="tpu_custom_call" | custom-call | flops 18350080 | bytes 7340032 | tf_op jit(solution)/shard_map/pallas_call | solution.py:481
  11.7 0.0 collective-permute-done.a_ref.refs_7_
  11.7 0.0 collective-permute-done.1.b_ref.refs_8_
  11.7 0.0 copy-done.6
  11.8 0.1 shard_map.58
  11.8 0.0 copy-start.3
  11.8 0.6 %collective-permute-start.3 = (bf16[7,48,128]{2,1,0:T(8,128)(2,1)S(1)}, bf16[7,48,128]{2,1,0:T(8,128)(2,1)S(1)}, u32[]{:S(2)}, u32[]{:S(2)}) collective-permute-start(bf16[7,48,128]{2,1,0:T(8,128)(2,1)S(1)} %shard_map.58), channel_id=1, source_target_pairs={{0,1},{1,0},{2,3},{3,2},{4,5},{5,4},{6,7},{7,6},{8,9},{9,8},{10,11... | collective-permute-start | bytes 258056 | tf_op jit(solution)/shard_map/ppermute | solution.py:502
  12.4 3.9 %shard_map.56 = f32[7,1024,128]{2,1,0:T(8,128)S(1)} custom-call(f32[2,7]{1,0:T(2,128)S(1)} %copy-done.4, f32[2,7]{1,0:T(2,128)S(1)} %copy-done.5, f32[7,1024,128]{2,1,0:T(8,128)S(1)} %bitcast.7, f32[7,1024,128]{2,1,0:T(8,128)S(1)} %shard_map.55.refs_3_.after_ref.refs_4_, s32[1024,128]{1,0:T(8,128)S(1)} %bitcast.12), custom_call_target="tpu_custom_call" | custom-call | flops 18350080 | bytes 7340032 | tf_op jit(solution)/shard_map/pallas_call | solution.py:481
  16.3 0.2 collective-permute-done.3.refs_10_.refs_11_
  16.5 0.0 collective-permute-done.2.refs_9_
  16.5 0.0 copy-done.3
  16.5 4.7 %shard_map.59 = f32[7,32,32,128]{3,2,1,0:T(8,128)} custom-call(f32[2,7]{1,0:T(2,128)S(1)} %copy-done.4, f32[2,7]{1,0:T(2,128)S(1)} %copy-done.5, s32[1,32]{1,0:T(1,128)S(1)} %bitcast.15, f32[7,1024,128]{2,1,0:T(8,128)S(1)} %bitcast.8, f32[7,1024,128]{2,1,0:T(8,128)S(1)} %shard_map.55.refs_3_.after_ref.refs_4_, f32[7,32,32,128]{3,2,1,0:T(8,128)S(1)} %bitcast.9, ...), custom_call_target="tpu_custom_call" | custom-call | flops 9175040 | bytes 7340032 | tf_op jit(solution)/shard_map/pallas_call | solution.py:511
Async XLA Ops:
  0.0 8.0 %copy-start.5 = (f32[2,7]{1,0:T(2,128)S(1)}, f32[2,7]{1,0:T(2,128)}, u32[]{:S(2)}) copy-start(f32[2,7]{1,0:T(2,128)} %refs_1_.5) | copy-start | bytes 172
  0.0 8.0 %copy-start.4 = (f32[2,7]{1,0:T(2,128)S(1)}, f32[2,7]{1,0:T(2,128)}, u32[]{:S(2)}) copy-start(f32[2,7]{1,0:T(2,128)} %refs_0_.5) | copy-start | bytes 172
  0.0 2.1 %copy-start = (f32[1,7,32,32,128]{4,3,2,1,0:T(8,128)S(1)}, f32[1,7,32,32,128]{4,3,2,1,0:T(8,128)}, u32[]{:S(2)}) copy-start(f32[1,7,32,32,128]{4,3,2,1,0:T(8,128)} %param.5) | copy-start | bytes 11010052
  2.1 1.0 %copy-start.2 = (s32[32,32,128]{2,1,0:T(8,128)S(1)}, s32[32,32,128]{2,1,0:T(8,128)}, u32[]{:S(2)}) copy-start(s32[32,32,128]{2,1,0:T(8,128)} %param.8) | copy-start | bytes 1572868
  3.1 4.8 %copy-start.1 = (f32[1,7,32,32,128]{4,3,2,1,0:T(8,128)S(1)}, f32[1,7,32,32,128]{4,3,2,1,0:T(8,128)}, u32[]{:S(2)}) copy-start(f32[1,7,32,32,128]{4,3,2,1,0:T(8,128)} %param.5) | copy-start | bytes 11010052
  3.4 13.1 %collective-permute-start.2 = (bf16[30,32,128]{2,1,0:T(8,128)(2,1)S(1)}, bf16[30,32,128]{2,1,0:T(8,128)(2,1)S(1)}, u32[]{:S(2)}, u32[]{:S(2)}) collective-permute-start(bf16[30,32,128]{2,1,0:T(8,128)(2,1)S(1)} %get-tuple-element.10), channel_id=1, source_target_pairs={{0,1},{1,0},{2,3},{3,2},{4,5},{5,4},{6,7},{7,6},{8,9},{9,8},{10,11... | collective-permute-start | bytes 737288 | tf_op jit(solution)/shard_map/ppermute | solution.py:462
  6.4 5.3 %collective-permute-start = (bf16[15,32,128]{2,1,0:T(8,128)(2,1)S(1)}, bf16[15,32,128]{2,1,0:T(8,128)(2,1)S(1)}, u32[]{:S(2)}, u32[]{:S(2)}) collective-permute-start(bf16[15,32,128]{2,1,0:T(8,128)(2,1)S(1)} %get-tuple-element.8), channel_id=1, source_target_pairs={{0,2},{4,6},{8,10},{12,14},{2,0},{6,4},{10,8},{14,12},{1,3},{5,7},... | collective-permute-start | bytes 368648 | tf_op jit(solution)/shard_map/ppermute | solution.py:473
  6.4 5.3 %copy-start.6 = (s32[32]{0:T(128)S(1)}, s32[32]{0:T(128)}, u32[]{:S(2)}) copy-start(s32[32]{0:T(128)} %param.9) | copy-start | bytes 388
  6.4 5.3 %collective-permute-start.1 = (bf16[15,32,128]{2,1,0:T(8,128)(2,1)S(1)}, bf16[15,32,128]{2,1,0:T(8,128)(2,1)S(1)}, u32[]{:S(2)}, u32[]{:S(2)}) collective-permute-start(bf16[15,32,128]{2,1,0:T(8,128)(2,1)S(1)} %get-tuple-element.9), channel_id=1, source_target_pairs={{2,4},{6,8},{10,12},{18,20},{22,24},{26,28},{0,16},{14,30},{4,2},{... | collective-permute-start | bytes 368648 | tf_op jit(solution)/shard_map/ppermute | solution.py:475
  11.8 4.7 %copy-start.3 = (s32[32,32,128]{2,1,0:T(8,128)S(1)}, s32[32,32,128]{2,1,0:T(8,128)}, u32[]{:S(2)}) copy-start(s32[32,32,128]{2,1,0:T(8,128)} %param.8) | copy-start | bytes 1572868
  11.8 4.7 %collective-permute-start.3 = (bf16[7,48,128]{2,1,0:T(8,128)(2,1)S(1)}, bf16[7,48,128]{2,1,0:T(8,128)(2,1)S(1)}, u32[]{:S(2)}, u32[]{:S(2)}) collective-permute-start(bf16[7,48,128]{2,1,0:T(8,128)(2,1)S(1)} %shard_map.58), channel_id=1, source_target_pairs={{0,1},{1,0},{2,3},{3,2},{4,5},{5,4},{6,7},{7,6},{8,9},{9,8},{10,11... | collective-permute-start | bytes 258056 | tf_op jit(solution)/shard_map/ppermute | solution.py:502

commit v9 on v8

--- a/solution.py
+++ b/solution.py
@@ -102,7 +102,7 @@
         ups, downs = (accs[:n], accs[n : 2 * n]), (accs[2 * n : 3 * n], accs[3 * n :])
         d, c, level = scalars(dif, adv, nf)
         lo, hi = (1, nx - 2) if second else (0, nx - 1)
-        deep = next(n for n in (8, 6, 4, 2) if (hi + 1 - lo) % n == 0)
+        deep = next(n for n in (16, 10, 2) if (hi + 1 - lo) % n == 0)
         closed = (0, ny - 2) if second else (ny - 1,)
         sub = lax.broadcasted_iota(jnp.int32, (8, nz), 0)
         fx[...] = jnp.zeros_like(fx)

time: 21.3 us -> 21.2 us (level)
  no operation moved by 1% of the time
where the time goes in v9:
time: 21.2 us; the launch traced here: 21 us
  Pallas kernels  12.5 us (59%)
  starting transfers between devices  5.11 us (24%)
  local copies, waits for them, and re-layouts  3.12 us (15%)
  waiting for transfers between devices  0.24 us (1%)
    pallas_call x2, Pallas kernels, section(): pl.pallas_call(functools.partial(section_kernel, dims, second), out_shape...  7.47 us
    pallas_call x1, Pallas kernels, body(): pl.pallas_call(functools.partial(border_kernel, dims, two), out_shape=jax...  4.67 us
    unnamed x14, local copies, waits for them, and re-layouts  3.12 us
    ppermute x1, starting transfers between devices, body(): c1 = lax.ppermute(send_c, 'gy', swap)  3 us
    ppermute x1, starting transfers between devices, body(): lax.ppermute(send_b, ('comp', 'gx'), both(outer + [(0, ngx), (ngx - 1, 2...  1.52 us
    ppermute x1, starting transfers between devices, body(): c2 = lax.ppermute(extra, 'gy', swap)  0.59 us
  transfers between devices with their start and end apart: 4, of which 1 were waited for; matrix products, arithmetic and copies ran while one was open for 0% of the time, Pallas kernels for 36%

profile of v9, /device:TPU:0, one launch (start us, length us, event | category | flops | bytes accessed | tf_op | source)
XLA Modules:
  0.0 21.0 jit_solution(8743265869820970629)
XLA Ops:
  0.0 0.0 copy-start.5
  0.0 0.0 copy-start.4
  0.0 0.0 copy-start
  0.0 2.1 %copy-done = f32[1,7,32,32,128]{4,3,2,1,0:T(8,128)S(1)} copy-done((f32[1,7,32,32,128]{4,3,2,1,0:T(8,128)S(1)}, f32[1,7,32,32,128]{4,3,2,1,0:T(8,128)}, u32[]{:S(2)}) %copy-start) | copy-done | bytes 3670040
  2.1 0.0 copy-start.2
  2.1 1.0 %copy-done.2 = s32[32,32,128]{2,1,0:T(8,128)S(1)} copy-done((s32[32,32,128]{2,1,0:T(8,128)S(1)}, s32[32,32,128]{2,1,0:T(8,128)}, u32[]{:S(2)}) %copy-start.2) | copy-done | bytes 524312
  3.1 0.0 copy-start.1
  3.1 0.3 %shard_map.57 = (bf16[15,32,128]{2,1,0:T(8,128)(2,1)S(1)}, bf16[15,32,128]{2,1,0:T(8,128)(2,1)S(1)}, bf16[30,32,128]{2,1,0:T(8,128)(2,1)S(1)}) custom-call(f32[7,1024,128]{2,1,0:T(8,128)S(1)} %bitcast.5, s32[1024,128]{1,0:T(8,128)S(1)} %bitcast.10), custom_call_target="tpu_custom_call" | custom-call | tf_op jit(solution)/shard_map/pallas_call | solution.py:452
  3.4 3.0 %collective-permute-start.2 = (bf16[30,32,128]{2,1,0:T(8,128)(2,1)S(1)}, bf16[30,32,128]{2,1,0:T(8,128)(2,1)S(1)}, u32[]{:S(2)}, u32[]{:S(2)}) collective-permute-start(bf16[30,32,128]{2,1,0:T(8,128)(2,1)S(1)} %get-tuple-element.10), channel_id=1, source_target_pairs={{0,1},{1,0},{2,3},{3,2},{4,5},{5,4},{6,7},{7,6},{8,9},{9,8},{10,11... | collective-permute-start | bytes 737288 | tf_op jit(solution)/shard_map/ppermute | solution.py:462
  6.4 0.0 collective-permute-start
  6.4 0.0 copy-start.6
  6.4 1.5 %collective-permute-start.1 = (bf16[15,32,128]{2,1,0:T(8,128)(2,1)S(1)}, bf16[15,32,128]{2,1,0:T(8,128)(2,1)S(1)}, u32[]{:S(2)}, u32[]{:S(2)}) collective-permute-start(bf16[15,32,128]{2,1,0:T(8,128)(2,1)S(1)} %get-tuple-element.9), channel_id=1, source_target_pairs={{2,4},{6,8},{10,12},{18,20},{22,24},{26,28},{0,16},{14,30},{4,2},{... | collective-permute-start | bytes 368648 | tf_op jit(solution)/shard_map/ppermute | solution.py:475
  7.9 0.0 copy-done.5
  8.0 0.0 copy-done.4
  8.0 0.0 copy-done.1
  8.0 3.6 %shard_map.55.refs_3_.after_ref.refs_4_ = f32[7,1024,128]{2,1,0:T(8,128)S(1)} custom-call(f32[2,7]{1,0:T(2,128)S(1)} %copy-done.4, f32[2,7]{1,0:T(2,128)S(1)} %copy-done.5, f32[7,1024,128]{2,1,0:T(8,128)S(1)} %bitcast.6, s32[1024,128]{1,0:T(8,128)S(1)} %bitcast.11), custom_call_target="tpu_custom_call" | custom-call | flops 18350080 | bytes 7340032 | tf_op jit(solution)/shard_map/pallas_call | solution.py:481
  11.6 0.0 collective-permute-done.a_ref.refs_7_
  11.6 0.0 collective-permute-done.1.b_ref.refs_8_
  11.6 0.0 copy-done.6
  11.6 0.1 shard_map.58
  11.7 0.0 copy-start.3
  11.7 0.6 %collective-permute-start.3 = (bf16[7,48,128]{2,1,0:T(8,128)(2,1)S(1)}, bf16[7,48,128]{2,1,0:T(8,128)(2,1)S(1)}, u32[]{:S(2)}, u32[]{:S(2)}) collective-permute-start(bf16[7,48,128]{2,1,0:T(8,128)(2,1)S(1)} %shard_map.58), channel_id=1, source_target_pairs={{0,1},{1,0},{2,3},{3,2},{4,5},{5,4},{6,7},{7,6},{8,9},{9,8},{10,11... | collective-permute-start | bytes 258056 | tf_op jit(solution)/shard_map/ppermute | solution.py:502
  12.3 3.9 %shard_map.56 = f32[7,1024,128]{2,1,0:T(8,128)S(1)} custom-call(f32[2,7]{1,0:T(2,128)S(1)} %copy-done.4, f32[2,7]{1,0:T(2,128)S(1)} %copy-done.5, f32[7,1024,128]{2,1,0:T(8,128)S(1)} %bitcast.7, f32[7,1024,128]{2,1,0:T(8,128)S(1)} %shard_map.55.refs_3_.after_ref.refs_4_, s32[1024,128]{1,0:T(8,128)S(1)} %bitcast.12), custom_call_target="tpu_custom_call" | custom-call | flops 18350080 | bytes 7340032 | tf_op jit(solution)/shard_map/pallas_call | solution.py:481
  16.1 0.2 %collective-permute-done.3.refs_10_.refs_11_ = bf16[7,48,128]{2,1,0:T(8,128)(2,1)S(1)} collective-permute-done((bf16[7,48,128]{2,1,0:T(8,128)(2,1)S(1)}, bf16[7,48,128]{2,1,0:T(8,128)(2,1)S(1)}, u32[]{:S(2)}, u32[]{:S(2)}) %collective-permute-start.3) | collective-permute-done | bytes 86048 | tf_op jit(solution)/shard_map/ppermute | solution.py:502
  16.4 0.0 collective-permute-done.2.refs_9_
  16.4 0.0 copy-done.3
  16.4 4.7 %shard_map.59 = f32[7,32,32,128]{3,2,1,0:T(8,128)} custom-call(f32[2,7]{1,0:T(2,128)S(1)} %copy-done.4, f32[2,7]{1,0:T(2,128)S(1)} %copy-done.5, s32[1,32]{1,0:T(1,128)S(1)} %bitcast.15, f32[7,1024,128]{2,1,0:T(8,128)S(1)} %bitcast.8, f32[7,1024,128]{2,1,0:T(8,128)S(1)} %shard_map.55.refs_3_.after_ref.refs_4_, f32[7,32,32,128]{3,2,1,0:T(8,128)S(1)} %bitcast.9, ...), custom_call_target="tpu_custom_call" | custom-call | flops 9175040 | bytes 7340032 | tf_op jit(solution)/shard_map/pallas_call | solution.py:511
Async XLA Ops:
  0.0 8.0 %copy-start.5 = (f32[2,7]{1,0:T(2,128)S(1)}, f32[2,7]{1,0:T(2,128)}, u32[]{:S(2)}) copy-start(f32[2,7]{1,0:T(2,128)} %refs_1_.5) | copy-start | bytes 172
  0.0 8.0 %copy-start.4 = (f32[2,7]{1,0:T(2,128)S(1)}, f32[2,7]{1,0:T(2,128)}, u32[]{:S(2)}) copy-start(f32[2,7]{1,0:T(2,128)} %refs_0_.5) | copy-start | bytes 172
  0.0 2.1 %copy-start = (f32[1,7,32,32,128]{4,3,2,1,0:T(8,128)S(1)}, f32[1,7,32,32,128]{4,3,2,1,0:T(8,128)}, u32[]{:S(2)}) copy-start(f32[1,7,32,32,128]{4,3,2,1,0:T(8,128)} %param.5) | copy-start | bytes 11010052
  2.1 1.0 %copy-start.2 = (s32[32,32,128]{2,1,0:T(8,128)S(1)}, s32[32,32,128]{2,1,0:T(8,128)}, u32[]{:S(2)}) copy-start(s32[32,32,128]{2,1,0:T(8,128)} %param.8) | copy-start | bytes 1572868
  3.1 4.8 %copy-start.1 = (f32[1,7,32,32,128]{4,3,2,1,0:T(8,128)S(1)}, f32[1,7,32,32,128]{4,3,2,1,0:T(8,128)}, u32[]{:S(2)}) copy-start(f32[1,7,32,32,128]{4,3,2,1,0:T(8,128)} %param.5) | copy-start | bytes 11010052
  3.4 12.9 %collective-permute-start.2 = (bf16[30,32,128]{2,1,0:T(8,128)(2,1)S(1)}, bf16[30,32,128]{2,1,0:T(8,128)(2,1)S(1)}, u32[]{:S(2)}, u32[]{:S(2)}) collective-permute-start(bf16[30,32,128]{2,1,0:T(8,128)(2,1)S(1)} %get-tuple-element.10), channel_id=1, source_target_pairs={{0,1},{1,0},{2,3},{3,2},{4,5},{5,4},{6,7},{7,6},{8,9},{9,8},{10,11... | collective-permute-start | bytes 737288 | tf_op jit(solution)/shard_map/ppermute | solution.py:462
  6.4 5.2 %collective-permute-start = (bf16[15,32,128]{2,1,0:T(8,128)(2,1)S(1)}, bf16[15,32,128]{2,1,0:T(8,128)(2,1)S(1)}, u32[]{:S(2)}, u32[]{:S(2)}) collective-permute-start(bf16[15,32,128]{2,1,0:T(8,128)(2,1)S(1)} %get-tuple-element.8), channel_id=1, source_target_pairs={{0,2},{4,6},{8,10},{12,14},{2,0},{6,4},{10,8},{14,12},{1,3},{5,7},... | collective-permute-start | bytes 368648 | tf_op jit(solution)/shard_map/ppermute | solution.py:473
  6.4 5.2 %copy-start.6 = (s32[32]{0:T(128)S(1)}, s32[32]{0:T(128)}, u32[]{:S(2)}) copy-start(s32[32]{0:T(128)} %param.9) | copy-start | bytes 388
  6.4 5.2 %collective-permute-start.1 = (bf16[15,32,128]{2,1,0:T(8,128)(2,1)S(1)}, bf16[15,32,128]{2,1,0:T(8,128)(2,1)S(1)}, u32[]{:S(2)}, u32[]{:S(2)}) collective-permute-start(bf16[15,32,128]{2,1,0:T(8,128)(2,1)S(1)} %get-tuple-element.9), channel_id=1, source_target_pairs={{2,4},{6,8},{10,12},{18,20},{22,24},{26,28},{0,16},{14,30},{4,2},{... | collective-permute-start | bytes 368648 | tf_op jit(solution)/shard_map/ppermute | solution.py:475
  11.7 4.7 %copy-start.3 = (s32[32,32,128]{2,1,0:T(8,128)S(1)}, s32[32,32,128]{2,1,0:T(8,128)}, u32[]{:S(2)}) copy-start(s32[32,32,128]{2,1,0:T(8,128)} %param.8) | copy-start | bytes 1572868
  11.7 4.7 %collective-permute-start.3 = (bf16[7,48,128]{2,1,0:T(8,128)(2,1)S(1)}, bf16[7,48,128]{2,1,0:T(8,128)(2,1)S(1)}, u32[]{:S(2)}, u32[]{:S(2)}) collective-permute-start(bf16[7,48,128]{2,1,0:T(8,128)(2,1)S(1)} %shard_map.58), channel_id=1, source_target_pairs={{0,1},{1,0},{2,3},{3,2},{4,5},{5,4},{6,7},{7,6},{8,9},{9,8},{10,11... | collective-permute-start | bytes 258056 | tf_op jit(solution)/shard_map/ppermute | solution.py:502
